TPU v7x, 32 devices: a whole 2x2x4 slice. The times are simulated.
32 devices in a mesh: seq: 4 (over z), tok: 8 (over y, x, core).
Axes of the slice: x: 2, y: 2, z: 4, core: 2. Of those that a mesh axis runs over, the one named last changes fastest.
Arguments:
- tokens: bfloat16 [4, 1024, 1024], P('seq', 'tok'), may hold values from -6 to 6
- cotangent: bfloat16 [4, 1024, 1024], P('seq', 'tok'), may hold values from -6 to 6
- owners: int32 [5409], replicated, may hold values from 0 to 31, as said below
- master: float32 [8160, 2048], P(('seq', 'tok')), may hold values from -4 to 4
- first_moment: float32 [8160, 2048], P(('seq', 'tok')), may hold values from -28.8 to 28.8
- second_moment: float32 [8160, 2048], P(('seq', 'tok')), may hold values from 0 to 901.12, as said below
Outputs:
- result: bfloat16 [4, 1024, 1024], P('seq', 'tok')
- grad_input: bfloat16 [4, 1024, 1024], P('seq', 'tok')
- reduced_grad: float32 [8160, 2048], P(('seq', 'tok'))
- new_first: float32 [8160, 2048], P(('seq', 'tok'))
- new_second: float32 [8160, 2048], P(('seq', 'tok'))
- new_master: float32 [8160, 2048], P(('seq', 'tok'))
Inputs may be any that keep to these rules, and one draw needn't show every extreme that they name: owners[b] is the device, indexed over seq then tok, that owns weight block b; no device owns more than 255 blocks and some device owns exactly 255. Entries of second_moment are positive.
All inputs are finite; a program needn't handle non-finite values.
Results may differ from a plain program's by a relative error of at most 0.012.
Values may be sent and summed in bfloat16 or wider, within the bound.
No kernel may reach another device: no remote copies, remote signals or barrier semaphores. Data moves between devices by JAX's collectives and lax.ppermute only.
A program may use at most 576 MiB of HBM per device.

v0:
```python
import math

import jax
import jax.numpy as jnp
from jax import lax
from jax.sharding import PartitionSpec as P


D = 1024
HEADS = 16
FD = 16
DV = 64
FF = 2752
STEP = 10
BLK = 2048

NORM_EPSILON = 1e-05
ADAM_EPSILON = 1e-08
BETA_ONE = 0.9
BETA_TWO = 0.95
DECAY_RATE = 0.1
BF = jnp.bfloat16
F32 = jnp.float32


MATRIX_BLOCKS = [
    D * HEADS * FD // BLK,
    D * HEADS * FD // BLK,
    D * HEADS * DV // BLK,
    HEADS * DV * D // BLK,
    D * FF // BLK,
    D * FF // BLK,
    FF * D // BLK,
]
MATRIX_STARTS = [1 + sum(MATRIX_BLOCKS[:k]) for k in range(len(MATRIX_BLOCKS))]
LIMITS = [1] + [MATRIX_STARTS[k] + MATRIX_BLOCKS[k] for k in range(len(MATRIX_BLOCKS))]
GROUPS = [(0, 1, 2, 3), (4, 5, 6)]


def product(left, right):
    return jnp.dot(left, right, preferred_element_type=F32)


def left_product(left, right):
    return lax.dot_general(left, right, (((0,), (0,)), ((), ())), preferred_element_type=F32)


def right_product(left, right):
    return lax.dot_general(left, right, (((1,), (1,)), ((), ())), preferred_element_type=F32)


def normalize(values):
    scale = lax.rsqrt(jnp.mean(values * values, axis=-1, keepdims=True) + NORM_EPSILON)
    return (values * scale, scale)


def norm_back(grad_hat, normed_rows, scale):
    return scale * (
        grad_hat - normed_rows * jnp.mean(grad_hat * normed_rows, axis=-1, keepdims=True)
    )


def swap(values, mask):
    return lax.ppermute(values, "tok", [(i, i ^ mask) for i in range(8)])


def exchange(values):
    return lax.all_to_all(values, "tok", 0, 0, tiled=True)


def gather_rows(rows, tok):
    if tok != 8:
        return lax.all_gather(rows, "tok", axis=1, tiled=False)
    half = rows.shape[2] // 2
    a, b = rows[:, :, :half], rows[:, :, half:]
    ax, by = swap(a, 2), swap(b, 4)
    a2, b2 = jnp.stack([a, ax], 1), jnp.stack([b, by], 1)
    ay, bx = swap(a2, 4), swap(b2, 2)
    first = jnp.concatenate([a2, ay], 1)
    second = jnp.stack([b, bx[:, 0], by, bx[:, 1]], 1)
    full = jnp.concatenate([first, second], -1)
    other = swap(full, 1)
    count = rows.shape[0]
    return jnp.stack([full, other], 2).reshape((count, 8) + rows.shape[1:])


def scatter_sum(parts, tok):
    if tok != 8:
        sent = lax.all_to_all(parts.astype(BF), "tok", 1, 1, tiled=True)
        return jnp.sum(sent.astype(F32), axis=1)
    many, _, count, width = parts.shape
    half = width // 2
    pairs = parts.reshape(many, 4, 2, count, width)
    mine = pairs[:, :, 0] + swap(pairs[:, :, 1].astype(BF), 1).astype(F32)
    a, b = mine[..., :half], mine[..., half:]
    got_a = swap(a[:, 2:].astype(BF), 4)
    got_b = swap(jnp.stack([b[:, 1], b[:, 3]], 1).astype(BF), 2)
    a = a[:, :2] + got_a.astype(F32)
    b = jnp.stack([b[:, 0], b[:, 2]], 1) + got_b.astype(F32)
    got_a = swap(a[:, 1].astype(BF), 2)
    got_b = swap(b[:, 1].astype(BF), 4)
    return jnp.concatenate([a[:, 0] + got_a.astype(F32), b[:, 0] + got_b.astype(F32)], -1)


def ff_share(tok):
    return round_up(FF / tok, 128)


def sharded(per_block, tok, group, fill):
    pieces = []
    if group == 0:
        pieces.append(jnp.broadcast_to(per_block[:1][None], (tok, 1)))
    for k in GROUPS[group]:
        piece = lax.slice_in_dim(per_block, MATRIX_STARTS[k], MATRIX_STARTS[k] + MATRIX_BLOCKS[k])
        if k == 6:
            missing = tok * ff_share(tok) * D // BLK - MATRIX_BLOCKS[k]
            piece = jnp.pad(piece, (0, missing), constant_values=fill)
        pieces.append(piece.reshape(tok, -1))
    return jnp.concatenate(pieces, axis=1)


def rotate(values, count):
    return lax.ppermute(values, "seq", [(i, (i + 1) % count) for i in range(count)])


def onehot(index, size):
    return (index[:, None] == jnp.arange(size, dtype=jnp.int32)[None, :]).astype(BF)


def before(size):
    rows = jnp.arange(size, dtype=jnp.int32)
    return (rows[:, None] < rows[None, :]).astype(BF)


def slot_ranks(owners, devices):
    count = owners.shape[0]
    chunks = -(-count // 128)
    padded = jnp.pad(owners, (0, chunks * 128 - count), constant_values=-1).reshape(chunks, 128)
    match = (
        padded[None] == jnp.arange(devices, dtype=jnp.int32)[:, None, None]
    ).astype(BF)
    within = jnp.einsum("ocl,lm->ocm", match, before(128), preferred_element_type=F32)
    totals = jnp.sum(match.astype(F32), axis=2)
    base = product(totals.astype(BF), before(chunks))
    ranks = jnp.sum(match.astype(F32) * (within + base[:, :, None]), axis=0)
    return ranks.reshape(-1)[:count].astype(jnp.int32)


def round_up(value, unit):
    return int(-(-value // unit) * unit)


class Route:
    def __init__(self, owners, slots, group, seq, tok, capacity):
        devices = seq * tok
        count = owners.shape[0]
        self.seq, self.tok, self.capacity, self.group = seq, tok, capacity, group
        owner = sharded(owners, tok, group, -1)
        slot = sharded(slots, tok, group, 0)
        size = owner.shape[1]
        self.size = size
        mean = capacity * size / count
        self.pair_cap = round_up(mean + 4.2 * math.sqrt(mean) + 1, 8)
        share = min(1.0, ((tok - 1) * count / devices + capacity) / count)
        mean = size * share
        self.row_cap = min(round_up(mean + 3.7 * math.sqrt(mean * (1 - share)), 8), round_up(size, 8))
        match = (owner[None] == jnp.arange(devices, dtype=jnp.int32)[:, None, None]).astype(BF)
        earlier = jnp.einsum("otl,lm->otm", match, before(size), preferred_element_type=F32)
        pair_rank = jnp.sum(match.astype(F32) * earlier, axis=0).astype(jnp.int32)
        owner_seq = jnp.where(owner >= 0, owner // tok, -1)
        earlier_seq = jnp.sum(earlier.reshape(seq, tok, tok, size), axis=1)
        match_seq = owner_seq[None] == jnp.arange(seq, dtype=jnp.int32)[:, None, None]
        row_rank = jnp.sum(jnp.where(match_seq, earlier_seq, 0.0), axis=0).astype(jnp.int32)
        self.fits = (jnp.max(pair_rank) < self.pair_cap) & (jnp.max(row_rank) < self.row_cap)
        me_seq, me_tok = lax.axis_index("seq"), lax.axis_index("tok")
        me = me_seq * tok + me_tok
        shard = jnp.arange(tok, dtype=jnp.int32)[:, None]
        place = jnp.where(pair_rank < self.pair_cap, shard * self.pair_cap + pair_rank, -1)
        self.own_slot = jnp.where(owner == me, slot, -1)
        self.has_gains = (owners[0] == me) & (jnp.arange(capacity, dtype=jnp.int32) == 0)
        once = 1 if group == 0 else 0
        own_slot = self.own_slot[:, once:].reshape(-1)
        hit = own_slot[None, :] == jnp.arange(capacity, dtype=jnp.int32)[:, None]
        target = (
            jnp.sum(jnp.where(hit, place[:, once:].reshape(-1)[None, :] + 1, 0), axis=1) - 1
        )
        columns = jnp.arange(tok * self.pair_cap, dtype=jnp.int32)[None, :]
        send = target[:, None] == columns
        if once:
            send = send | (self.has_gains[:, None] & (columns % self.pair_cap == 0))
        self.send = send.astype(BF)
        my_owner = lax.dynamic_index_in_dim(owner, me_tok, 0, keepdims=False)
        my_seq = lax.dynamic_index_in_dim(owner_seq, me_tok, 0, keepdims=False)
        my_pair = lax.dynamic_index_in_dim(pair_rank, me_tok, 0, keepdims=False)
        my_row = lax.dynamic_index_in_dim(row_rank, me_tok, 0, keepdims=False)
        arrive = jnp.where(
            (my_pair < self.pair_cap) & (my_owner >= 0),
            (my_owner % tok) * self.pair_cap + my_pair,
            -1,
        )
        from_pairs = onehot(arrive, tok * self.pair_cap)
        to_rows = onehot(jnp.where(my_seq == me_seq, my_row, -1), self.row_cap)
        self.compact = left_product(to_rows, from_pairs).astype(BF)
        self.place = onehot(
            jnp.where(
                (my_row < self.row_cap) & (my_owner >= 0),
                my_seq * self.row_cap + my_row,
                -1,
            ),
            seq * self.row_cap,
        )

    def fetch(self, rounded):
        packed = left_product(self.send, rounded).astype(BF)
        packed = exchange(packed)
        rows = product(self.compact, packed).astype(BF)
        rows = lax.all_gather(rows, "seq", axis=0, tiled=True)
        return product(self.place, rows).astype(BF)

    def fetch_any(self, rounded):
        width = rounded.shape[1]
        own = self.own_slot.reshape(-1)
        mine = jnp.where(
            (own >= 0)[:, None], jnp.take(rounded, jnp.maximum(own, 0), axis=0), 0
        ).astype(BF)
        mine = lax.all_to_all(mine.reshape(self.tok, self.size, width), "tok", 0, 0, tiled=True)
        mine = jnp.sum(mine, axis=0)
        total = mine
        for _ in range(self.seq - 1):
            mine = rotate(mine, self.seq)
            total = total + mine
        return total

    def give(self, grads):
        rows = left_product(self.place, grads).astype(BF)
        rows = lax.psum_scatter(rows, "seq", scatter_dimension=0, tiled=True)
        packed = left_product(self.compact, rows).astype(BF)
        packed = exchange(packed)
        return product(self.send, packed)

    def give_any(self, grads):
        width = grads.shape[1]
        total = grads.astype(F32)
        passing = grads
        for _ in range(self.seq - 1):
            passing = rotate(passing, self.seq)
            total = total + passing.astype(F32)
        every = jnp.broadcast_to(total.astype(BF)[None], (self.tok, self.size, width))
        every = lax.all_to_all(every, "tok", 0, 0, tiled=True)
        once = 1 if self.group == 0 else 0
        own = self.own_slot[:, once:].reshape(-1)
        hit = own[None, :] == jnp.arange(self.capacity, dtype=jnp.int32)[:, None]
        index = jnp.sum(
            jnp.where(hit, jnp.arange(1, own.shape[0] + 1, dtype=jnp.int32)[None, :], 0), axis=1
        )
        taken = jnp.take(
            every[:, once:].reshape(-1, width), jnp.maximum(index - 1, 0), axis=0
        ).astype(F32)
        taken = jnp.where((index > 0)[:, None], taken, 0.0)
        if once:
            gains = jnp.sum(every[:, 0].astype(F32), axis=0)
            taken = jnp.where(self.has_gains[:, None], gains[None, :], taken)
        return taken


def rates_for(kinds, seq_len):
    out_std = 1.0 / math.sqrt(max(1, D * 16 // seq_len))
    matrix_rate = 3.0 / math.sqrt(D)
    rate_list = [
        1.0,
        matrix_rate,
        matrix_rate,
        matrix_rate,
        3.0 * out_std,
        matrix_rate,
        matrix_rate,
        3.0 / math.sqrt(FF),
        0.0,
    ]
    decay_list = [0.0] + [DECAY_RATE] * 7 + [0.0]
    chosen = (kinds[:, None] == jnp.arange(9, dtype=jnp.int32)[None, :]).astype(F32)
    rate_values = jnp.sum(chosen * jnp.array(rate_list, F32)[None, :], axis=1)
    decay_values = jnp.sum(chosen * jnp.array(decay_list, F32)[None, :], axis=1)
    return (rate_values, decay_values)


def adam_update(grads, moment_one, moment_two, weights, rate_values, decay_values):
    first = BETA_ONE * moment_one + (1.0 - BETA_ONE) * grads
    second = BETA_TWO * moment_two + (1.0 - BETA_TWO) * grads * grads
    first_hat = first / (1.0 - BETA_ONE**STEP)
    second_hat = second / (1.0 - BETA_TWO**STEP)
    updated = weights - rate_values[:, None] * (
        first_hat / (jnp.sqrt(second_hat) + ADAM_EPSILON) + decay_values[:, None] * weights
    )
    return (first, second, updated)


def columns_out(rows, split):
    return rows.reshape(rows.shape[0], split, -1).transpose(1, 0, 2)


def step(tokens, cotangent, owners, master, first_moment, second_moment):
    seq = lax.axis_size("seq")
    tok = lax.axis_size("tok")
    capacity = master.shape[0]
    me = lax.axis_index("seq") * tok + lax.axis_index("tok")
    slots = slot_ranks(owners, seq * tok)
    routes = [Route(owners, slots, group, seq, tok, capacity) for group in range(2)]
    rounded = master.astype(BF)
    found = layer(tokens, cotangent, rounded, [(r.fetch, r.give) for r in routes])

    def any_owners(tokens, cotangent, rounded, *found):
        return layer(tokens, cotangent, rounded, [(r.fetch_any, r.give_any) for r in routes])

    result, grad_input, reduced = lax.cond(
        routes[0].fits & routes[1].fits,
        lambda tokens, cotangent, rounded, *found: found,
        any_owners,
        tokens,
        cotangent,
        rounded,
        *found,
    )
    mine = (owners == me)[None, :]
    numbers = jnp.arange(owners.shape[0], dtype=jnp.int32)[None, :]
    counts = jnp.sum(
        (mine & (numbers < jnp.array(LIMITS, jnp.int32)[:, None])).astype(jnp.int32), axis=1
    )
    kinds = jnp.sum(
        (jnp.arange(capacity, dtype=jnp.int32)[:, None] >= counts[None, :]).astype(jnp.int32), axis=1
    )
    rate_values, decay_values = rates_for(kinds, tokens.shape[1] * tok)
    first, second, updated = adam_update(
        reduced, first_moment, second_moment, master, rate_values, decay_values
    )
    return (result[None], grad_input[None], reduced, first, second, updated)


def layer(tokens, cotangent, rounded, routes):
    tok = lax.axis_size("tok")
    me_tok = lax.axis_index("tok")
    row_count = tokens.shape[1]
    seq_len = row_count * tok
    value_split = max(1, tok // HEADS)
    units = max(1, HEADS // tok)
    unit_width = DV // value_split
    slice_rows = D // tok
    ff_slice = ff_share(tok)
    qk_width = units * FD
    v_width = units * unit_width

    both = gather_rows(jnp.concatenate([tokens, cotangent]), tok)
    x_all, c_all = both[0].reshape(seq_len, D), both[1].reshape(seq_len, D)

    shard = routes[0][0](rounded)
    gain_one = shard[0, :D].astype(F32)
    gain_two = shard[0, D:].astype(F32)
    shard = shard[1:]
    a, b, c, _ = (MATRIX_BLOCKS[k] // tok for k in GROUPS[0])

    def spread(columns):
        wide = columns.reshape(slice_rows, tok // value_split, 1, qk_width)
        return jnp.broadcast_to(
            wide, (slice_rows, tok // value_split, value_split, qk_width)
        ).reshape(slice_rows, tok, qk_width)

    sent = jnp.concatenate(
        [
            spread(shard[:a].reshape(slice_rows, HEADS * FD)),
            spread(shard[a : a + b].reshape(slice_rows, HEADS * FD)),
            shard[a + b : a + b + c].reshape(slice_rows, tok, v_width),
        ],
        axis=-1,
    ).transpose(1, 0, 2)
    w_qkv = exchange(sent).reshape(D, -1)
    w_out = shard[a + b + c :].reshape(v_width, D)

    def padded(blocks):
        return jnp.pad(blocks.reshape(slice_rows, FF), ((0, 0), (0, tok * ff_slice - FF)))

    shard = routes[1][0](rounded)
    a = MATRIX_BLOCKS[4] // tok
    sent = jnp.concatenate(
        [
            columns_out(padded(shard[:a]), tok),
            columns_out(padded(shard[a : 2 * a]), tok),
        ],
        axis=-1,
    )
    w_gate_up = exchange(sent).reshape(D, -1)
    w_down = shard[2 * a :].reshape(ff_slice, D)

    normed_all, _ = normalize(x_all.astype(F32))
    hidden_one = (normed_all * gain_one).astype(BF)
    qkv = product(hidden_one, w_qkv).astype(BF)
    query = qkv[:, :qk_width].reshape(seq_len, units, FD).transpose(1, 0, 2)
    keys = qkv[:, qk_width : 2 * qk_width].reshape(seq_len, units, FD).transpose(1, 0, 2)
    values = qkv[:, 2 * qk_width :].reshape(seq_len, units, unit_width).transpose(1, 0, 2)
    place = jnp.arange(tok, dtype=jnp.int32)
    if tok == 8:
        place = place ^ me_tok
    index = (place[:, None] * row_count + jnp.arange(row_count, dtype=jnp.int32)[None, :]).reshape(-1)
    causal = (index[:, None] >= index[None, :])[None]
    inner = jnp.einsum("uif,ujf->uij", query, keys, preferred_element_type=F32) * (
        1.0 / math.sqrt(FD)
    )
    weight = jnp.where(causal, 1.0 + inner + 0.5 * inner * inner, 0.0)
    total = jnp.sum(weight, axis=2, keepdims=True)
    mixed_f = (
        jnp.einsum("uij,ujw->uiw", weight.astype(BF), values, preferred_element_type=F32) / total
    )
    mixed = mixed_f.astype(BF).transpose(1, 0, 2).reshape(seq_len, v_width)
    out = scatter_sum(product(mixed, w_out).reshape(1, tok, row_count, D), tok)[0]

    input_rows = tokens[0].astype(F32)
    middle = input_rows + out
    normed_two, scale_two = normalize(middle)
    hidden_two = gather_rows((normed_two * gain_two).astype(BF)[None], tok).reshape(seq_len, D)

    gate_up = product(hidden_two, w_gate_up)
    gate, up_proj = gate_up[:, :ff_slice], gate_up[:, ff_slice:]
    sigmoid = jax.nn.sigmoid(gate)
    activated = gate * sigmoid
    hidden = (activated * up_proj).astype(BF)
    grad_hidden = right_product(c_all, w_down)
    grad_gate = (grad_hidden * up_proj * sigmoid * (1.0 + gate * (1.0 - sigmoid))).astype(BF)
    grad_up = (grad_hidden * activated).astype(BF)
    grad_gate_up = jnp.concatenate([grad_gate, grad_up], axis=1)
    grad_two_terms = right_product(grad_gate_up, w_gate_up)
    grad_hidden_two = scatter_sum(grad_two_terms.reshape(1, tok, row_count, D), tok)[0]
    result_terms = product(hidden, w_down)

    grad_gain_two = jnp.sum(grad_hidden_two * normed_two, axis=0)
    grad_middle = cotangent[0].astype(F32) + norm_back(
        grad_hidden_two * gain_two, normed_two, scale_two
    )
    grad_mixer = gather_rows(grad_middle.astype(BF)[None], tok).reshape(seq_len, D)

    grad_w_down = left_product(hidden, c_all).astype(BF)
    grad_w_gate_up = left_product(hidden_two, grad_gate_up).astype(BF)
    back = exchange(grad_w_gate_up.reshape(tok, slice_rows, 2 * ff_slice))

    def flat(columns):
        rows = columns.transpose(1, 0, 2).reshape(slice_rows, tok * ff_slice)
        return rows[:, :FF].reshape(-1, BLK)

    back_gate, back_up = flat(back[..., :ff_slice]), flat(back[..., ff_slice:])
    reduced = routes[1][1](
        jnp.concatenate([back_gate, back_up, grad_w_down.reshape(-1, BLK)], axis=0)
    )

    grad_w_out = left_product(mixed, grad_mixer).astype(BF)
    grad_mixed = right_product(grad_mixer, w_out).astype(BF)
    grad_units = grad_mixed.reshape(seq_len, units, unit_width).transpose(1, 0, 2).astype(F32)
    grad_numer = (grad_units / total).astype(BF)
    grad_denom = -jnp.sum(grad_units * mixed_f, axis=-1, keepdims=True) / total
    grad_weight = (
        jnp.einsum("uiw,ujw->uij", grad_numer, values, preferred_element_type=F32) + grad_denom
    )
    grad_inner = (
        jnp.where(causal, grad_weight * (1.0 + inner), 0.0) * (1.0 / math.sqrt(FD))
    ).astype(BF)
    grad_query = jnp.einsum("uij,ujf->iuf", grad_inner, keys, preferred_element_type=F32)
    grad_keys = jnp.einsum("uij,uif->juf", grad_inner, query, preferred_element_type=F32)
    grad_values = jnp.einsum(
        "uij,uiw->juw", weight.astype(BF), grad_numer, preferred_element_type=F32
    )
    grad_qkv = jnp.concatenate(
        [
            grad_query.reshape(seq_len, -1),
            grad_keys.reshape(seq_len, -1),
            grad_values.reshape(seq_len, -1),
        ],
        axis=1,
    ).astype(BF)
    grad_w_qkv = left_product(hidden_one, grad_qkv).astype(BF)
    grad_one_terms = right_product(grad_qkv, w_qkv)
    terms = jnp.stack([result_terms, grad_one_terms]).reshape(2, tok, row_count, D)
    out_sum, grad_hidden_one = scatter_sum(terms, tok)
    result = (middle + out_sum).astype(BF)
    grad_gains = jnp.concatenate([jnp.sum(grad_one_terms * normed_all, axis=0), grad_gain_two])
    back = exchange(grad_w_qkv.reshape(tok, slice_rows, -1)).transpose(1, 0, 2)

    def gathered(columns):
        if value_split > 1:
            columns = jnp.sum(
                columns.reshape(slice_rows, tok // value_split, value_split, -1).astype(F32), axis=2
            ).astype(BF)
        return columns.reshape(-1, BLK)

    reduced = reduced + routes[0][1](
        jnp.concatenate(
            [
                grad_gains.astype(BF).reshape(1, BLK),
                gathered(back[..., :qk_width]),
                gathered(back[..., qk_width : 2 * qk_width]),
                back[..., 2 * qk_width :].reshape(-1, BLK),
                grad_w_out.reshape(-1, BLK),
            ],
            axis=0,
        )
    )

    normed_one, scale_one = normalize(input_rows)
    grad_input = grad_middle + norm_back(grad_hidden_one * gain_one, normed_one, scale_one)
    return result, grad_input.astype(BF), reduced


def solution(mesh):
    in_specs = (
        P("seq", "tok", None),
        P("seq", "tok", None),
        P(),
        P(("seq", "tok"), None),
        P(("seq", "tok"), None),
        P(("seq", "tok"), None),
    )
    out_specs = (
        P("seq", "tok", None),
        P("seq", "tok", None),
        P(("seq", "tok"), None),
        P(("seq", "tok"), None),
        P(("seq", "tok"), None),
        P(("seq", "tok"), None),
    )
    return jax.shard_map(step, mesh=mesh, in_specs=in_specs, out_specs=out_specs, check_vma=False)
```

profile of v0, /device:TPU:0, one launch (start us, length us, event | category | flops | bytes accessed | tf_op | source)
XLA Modules:
  0.0 463.7 jit_solution(18062239002089792864)
XLA Ops:
  19.0 5.2 %all-to-all-start.8 = ((bf16[8,24,2048]{2,1,0:T(8,128)(2,1)}), bf16[8,24,2048]{2,1,0:T(8,128)(2,1)S(1)}, u32[]{:S(2)}, u32[]{:S(2)}) async-start(bf16[8,24,2048]{2,1,0:T(8,128)(2,1)} %bitcast.121), calls=%async_computation.8 | async-start | bytes 1572864 | tf_op jit(solution)/shard_map/all_to_all | solution.py:68
  37.5 3.9 collective-permute-done.44
  47.2 9.1 %collective-permute-done.45 = bf16[2,2,128,512]{3,2,1,0:T(8,128)(2,1)} collective-permute-done((bf16[2,2,128,512]{3,2,1,0:T(8,128)(2,1)}, bf16[2,2,128,512]{3,2,1,0:T(8,128)(2,1)}, u32[]{:S(2)}, u32[]{:S(2)}) %collective-permute-start.45) | collective-permute-done | bytes 524320 | tf_op jit(solution)/shard_map/ppermute | solution.py:64
  63.2 9.1 %all-gather.3.cloned.1.call-done = bf16[256,2048]{1,0:T(8,128)(2,1)} async-done(((bf16[64,2048]{1,0:T(8,128)(2,1)}), bf16[256,2048]{1,0:T(8,128)(2,1)}) %all-gather.3.cloned.1.call-update) | async-done | bytes 1048592 | tf_op jit(solution)/shard_map/all_gather | solution.py:217
  87.8 4.1 all-to-all-start.9
  100.2 4.3 all-to-all-start.10
  107.3 4.9 %fusion.62 = (f32[2,1024]{1,0:T(2,128)S(1)}, bf16[2,1024,1024]{1,2,0:T(8,128)(2,1)S(1)}, f32[2,1024,1024]{1,2,0:T(8,128)}) fusion(pred[1024,1024]{0,1:T(8,128)(4,1)S(1)} %copy-done.79, bf16[2,1024,16]{1,2,0:T(8,128)(2,1)S(1)} %bitcast.730, bf16[2,1024,16]{1,2,0:T(8,128)(2,1)S(1)} %bitcast.722), kind=kOutput, calls=%fused_computation.206 | convolution fusion | flops 83884032 | bytes 13770752 | tf_op jit(solution)/shard_map/uif,ujf->uij/dot_general | solution.py:404
  132.1 5.8 %collective-permute-done.50 = bf16[1,2,128,512]{3,2,1,0:T(8,128)(2,1)S(1)} collective-permute-done((bf16[1,2,128,512]{3,2,1,0:T(8,128)(2,1)S(1)}, bf16[1,2,128,512]{3,2,1,0:T(8,128)(2,1)S(1)}, u32[]{:S(2)}, u32[]{:S(2)}) %collective-permute-start.50) | collective-permute-done | bytes 262176 | tf_op jit(solution)/shard_map/ppermute | solution.py:64
  145.8 4.5 collective-permute-done.54
  152.4 6.2 %collective-permute-done.52 = bf16[1,128,512]{2,1,0:T(8,128)(2,1)S(1)} collective-permute-done((bf16[1,128,512]{2,1,0:T(8,128)(2,1)S(1)}, bf16[1,128,512]{2,1,0:T(8,128)(2,1)S(1)}, u32[]{:S(2)}, u32[]{:S(2)}) %collective-permute-start.52) | collective-permute-done | bytes 131104 | tf_op jit(solution)/shard_map/ppermute | solution.py:64
  160.7 26.7 %all-gather.5.cloned.1.call-done = bf16[736,2048]{1,0:T(8,128)(2,1)} async-done(((bf16[184,2048]{1,0:T(8,128)(2,1)}), bf16[736,2048]{1,0:T(8,128)(2,1)}) %all-gather.5.cloned.1.call-update) | async-done | bytes 3014672 | tf_op jit(solution)/shard_map/all_gather | solution.py:217
  187.4 3.8 convolution_convert_fusion.10
  204.9 4.5 all-to-all-start.11
  218.4 12.1 %all-to-all-done.11 = bf16[8,128,768]{2,1,0:T(8,128)(2,1)} async-done(((bf16[8,128,768]{2,1,0:T(8,128)(2,1)}), bf16[8,128,768]{2,1,0:T(8,128)(2,1)}, u32[]{:S(2)}, u32[]{:S(2)}) %all-to-all-start.11) | async-done | bytes 1572896 | tf_op jit(solution)/shard_map/all_to_all | solution.py:68
  230.5 4.1 fusion.242
  248.4 7.1 %collective-permute-done.60 = bf16[1,2,128,512]{3,2,1,0:T(8,128)(2,1)S(1)} collective-permute-done((bf16[1,2,128,512]{3,2,1,0:T(8,128)(2,1)S(1)}, bf16[1,2,128,512]{3,2,1,0:T(8,128)(2,1)S(1)}, u32[]{:S(2)}, u32[]{:S(2)}) %collective-permute-start.60) | collective-permute-done | bytes 262176 | tf_op jit(solution)/shard_map/ppermute | solution.py:64
  270.5 3.7 collective-permute-done.65
  285.9 5.3 %multiply_convert_fusion.7 = bf16[2,1024,1024]{1,2,0:T(8,128)(2,1)S(1)} fusion(f32[2,1024,1024]{1,2,0:T(8,128)} %get-tuple-element.231, f32[2,1024]{1,0:T(2,128)S(1)} %negate_divide_fusion.1, pred[1024,1024]{0,1:T(8,128)(4,1)S(1)} %copy-done.80, bf16[2,1024,64]{1,2,0:T(8,128)(2,1)S(1)} %bitcast.739, f32[2,1024]{1,0:T(2,128)S(1)} %copy-done.133, ...), kind=kOutput, calls=%fused_computation.204 | convolution fusion | flops 283508736 | bytes 14172160 | tf_op jit(solution)/shard_map/uiw,ujw->uij/dot_general | solution.py:458
  294.0 4.0 multiply_convert_fusion.8
  299.4 4.1 all-to-all-start.14
  306.7 5.1 %all-to-all-done.14 = bf16[8,128,192]{1,2,0:T(8,128)(2,1)} async-done(((bf16[8,128,192]{1,2,0:T(8,128)(2,1)}), bf16[8,128,192]{1,2,0:T(8,128)(2,1)}, u32[]{:S(2)}, u32[]{:S(2)}) %all-to-all-start.14) | async-done | bytes 393248 | tf_op jit(solution)/shard_map/all_to_all | solution.py:68
  317.6 3.9 convolution_convert_fusion.19
  326.6 3.7 convolution_convert_fusion.20
  332.6 14.9 %all-to-all-done.12 = bf16[8,128,768]{1,2,0:T(8,128)(2,1)S(1)} async-done(((bf16[8,128,768]{1,2,0:T(8,128)(2,1)}), bf16[8,128,768]{1,2,0:T(8,128)(2,1)S(1)}, u32[]{:S(2)}, u32[]{:S(2)}) %all-to-all-start.12) | async-done | bytes 1572896 | tf_op jit(solution)/shard_map/all_to_all | solution.py:68
  352.3 5.4 %convolution_convert_fusion.9 = bf16[736,2048]{1,0:T(8,128)(2,1)} fusion(bf16[192,2048]{1,0:T(8,128)(2,1)S(1)} %copy-done.85, bf16[172,2048]{1,0:T(8,128)(2,1)} %reshape.1810, bf16[172,2048]{1,0:T(8,128)(2,1)S(1)} %reshape.1808, s32[536]{0:T(1024)S(1)} %copy-done.148), kind=kOutput, calls=%fused_computation.222 | convolution fusion | flops 1624343808 | bytes 5212256 | tf_op jit(solution)/shard_map/dot_general | solution.py:45
  369.6 3.7 fusion.198
  382.8 6.7 %collective-permute-done.70 = bf16[2,2,128,512]{3,2,0,1:T(8,128)(2,1)} collective-permute-done((bf16[2,2,128,512]{3,2,0,1:T(8,128)(2,1)}, bf16[2,2,128,512]{3,2,0,1:T(8,128)(2,1)}, u32[]{:S(2)}, u32[]{:S(2)}) %collective-permute-start.70) | collective-permute-done | bytes 524320 | tf_op jit(solution)/shard_map/ppermute | solution.py:64
  399.9 13.3 %reduce-scatter.3.cloned.1.call-done = bf16[184,2048]{1,0:T(8,128)(2,1)} async-done(((bf16[736,2048]{1,0:T(8,128)(2,1)}), bf16[184,2048]{1,0:T(8,128)(2,1)}) %reduce-scatter.3.cloned.1.call-update) | async-done | bytes 753680 | tf_op jit(solution)/shard_map/reduce_scatter | solution.py:236
  416.9 3.9 all-to-all-start.13
  426.7 15.1 %all-to-all-done.13 = bf16[8,48,2048]{2,1,0:T(8,128)(2,1)S(1)} async-done(((bf16[8,48,2048]{2,1,0:T(8,128)(2,1)}), bf16[8,48,2048]{2,1,0:T(8,128)(2,1)S(1)}, u32[]{:S(2)}, u32[]{:S(2)}) %all-to-all-start.13) | async-done | bytes 1572896 | tf_op jit(solution)/shard_map/all_to_all | solution.py:68
  443.9 5.3 %conditional.1 = (f32[255,2048]{1,0:T(8,128)S(1)}, bf16[1,128,1024]{2,1,0:T(8,128)(2,1)}, bf16[1,128,1024]{2,1,0:T(8,128)(2,1)}) conditional(s32[]{:T(128)} %convert_element_type.693, (s32[8,536]{1,0:T(8,128)S(1)}, bf16[1,128,1024]{2,1,0:T(8,128)(2,1)S(1)}, bf16[1,128,1024]{2,1,0:T(8,128)(2,1)S(1)}, s32[8,161]{1,0:T(8,128)S(1)}, ...), branch_computations={%region_25.40_spmd, %region_40.41_spmd} | conditional | flops 10486007808 | bytes 967106432 | solution.py:315
  449.2 7.8 %multiply_subtract_fusion = (f32[255,2048]{1,0:T(8,128)}, f32[255,2048]{1,0:T(8,128)}, f32[255,2048]{1,0:T(8,128)}) fusion(f32[255,2048]{1,0:T(8,128)} %param.14, f32[255]{0:T(256)} %get-tuple-element.57, f32[255]{0:T(256)} %get-tuple-element.56, f32[255,2048]{1,0:T(8,128)S(1)} %get-tuple-element.41, f32[255,2048]{1,0:T(8,128)} %param.16, f32[255,2048]{1,0:T(8,128)} %param.15), kind=kLoop, calls=%fused_computation.254 | loop fusion | flops 7833600 | bytes 14624760 | tf_op jit(solution)/shard_map/sub | solution.py:292
  (509 shorter events, 226.1 us)
Async XLA Ops:
  19.0 24.8 %all-to-all-start.8 = ((bf16[8,24,2048]{2,1,0:T(8,128)(2,1)}), bf16[8,24,2048]{2,1,0:T(8,128)(2,1)S(1)}, u32[]{:S(2)}, u32[]{:S(2)}) async-start(bf16[8,24,2048]{2,1,0:T(8,128)(2,1)} %bitcast.121), calls=%async_computation.8 | async-start | bytes 1572864 | tf_op jit(solution)/shard_map/all_to_all | solution.py:68
  24.2 48.1 %all-gather.3.cloned.1.call-start = ((), (), s32[]{:S(2)}) async-start(), calls=%async_computation.18 | async-start | bytes 1310720 | tf_op jit(solution)/shard_map/all_gather | solution.py:217
  25.2 16.2 %collective-permute-start.44 = (bf16[2,128,512]{2,1,0:T(8,128)(2,1)}, bf16[2,128,512]{2,1,0:T(8,128)(2,1)S(1)}, u32[]{:S(2)}, u32[]{:S(2)}) collective-permute-start(bf16[2,128,512]{2,1,0:T(8,128)(2,1)} %get-tuple-element.183), channel_id=1, source_target_pairs={{0,4},{1,5},{2,6},{3,7},{4,0},{5,1},{6,2},{7,3},{8,12},{9,13},{10,... | collective-permute-start | bytes 786440 | tf_op jit(solution)/shard_map/ppermute | solution.py:64
  27.2 17.6 %collective-permute-start.42 = (bf16[2,128,512]{2,1,0:T(8,128)(2,1)}, bf16[2,128,512]{2,1,0:T(8,128)(2,1)S(1)}, u32[]{:S(2)}, u32[]{:S(2)}) collective-permute-start(bf16[2,128,512]{2,1,0:T(8,128)(2,1)} %get-tuple-element.184), channel_id=1, source_target_pairs={{0,2},{1,3},{2,0},{3,1},{4,6},{5,7},{6,4},{7,5},{8,10},{9,11},{10,... | collective-permute-start | bytes 786440 | tf_op jit(solution)/shard_map/ppermute | solution.py:64
  42.3 13.9 %collective-permute-start.45 = (bf16[2,2,128,512]{3,2,1,0:T(8,128)(2,1)}, bf16[2,2,128,512]{3,2,1,0:T(8,128)(2,1)}, u32[]{:S(2)}, u32[]{:S(2)}) collective-permute-start(bf16[2,2,128,512]{3,2,1,0:T(8,128)(2,1)} %pad_maximum_fusion.34), channel_id=1, source_target_pairs={{0,2},{1,3},{2,0},{3,1},{4,6},{5,7},{6,4},{7,5},{8,10},{9,11},{10,... | collective-permute-start | bytes 1572872 | tf_op jit(solution)/shard_map/ppermute | solution.py:64
  44.9 13.7 %collective-permute-start.43 = (bf16[2,2,128,512]{3,2,0,1:T(8,128)(2,1)S(1)}, bf16[2,2,128,512]{3,2,0,1:T(8,128)(2,1)S(1)}, u32[]{:S(2)}, u32[]{:S(2)}) collective-permute-start(bf16[2,2,128,512]{3,2,0,1:T(8,128)(2,1)S(1)} %pad_maximum_fusion.33), channel_id=1, source_target_pairs={{0,4},{1,5},{2,6},{3,7},{4,0},{5,1},{6,2},{7,3},{8,12},{9,13},{10,... | collective-permute-start | bytes 1572872 | tf_op jit(solution)/shard_map/ppermute | solution.py:64
  60.0 32.6 %collective-permute-start.46 = (bf16[2,4,128,1024]{3,2,1,0:T(8,128)(2,1)}, bf16[2,4,128,1024]{3,2,1,0:T(8,128)(2,1)}, u32[]{:S(2)}, u32[]{:S(2)}) collective-permute-start(bf16[2,4,128,1024]{3,2,1,0:T(8,128)(2,1)} %maximum_maximum_fusion.3), channel_id=1, source_target_pairs={{0,1},{1,0},{2,3},{3,2},{4,5},{5,4},{6,7},{7,6},{8,9},{9,8},{10,11... | collective-permute-start | bytes 6291464 | tf_op jit(solution)/shard_map/ppermute | solution.py:64
  87.8 12.4 %all-to-all-start.9 = ((bf16[8,128,192]{1,2,0:T(8,128)(2,1)}), bf16[8,128,192]{1,2,0:T(8,128)(2,1)}, u32[]{:S(2)}, u32[]{:S(2)}) async-start(bf16[8,128,192]{1,2,0:T(8,128)(2,1)} %maximum_bitcast_fusion.1), calls=%async_computation.9 | async-start | bytes 786432 | tf_op jit(solution)/shard_map/all_to_all | solution.py:68
  100.2 25.3 %all-to-all-start.10 = ((bf16[8,48,2048]{2,1,0:T(8,128)(2,1)}), bf16[8,48,2048]{2,1,0:T(8,128)(2,1)}, u32[]{:S(2)}, u32[]{:S(2)}) async-start(bf16[8,48,2048]{2,1,0:T(8,128)(2,1)} %bitcast.637), calls=%async_computation.10 | async-start | bytes 3145728 | tf_op jit(solution)/shard_map/all_to_all | solution.py:68
  104.5 82.9 %all-gather.5.cloned.1.call-start = ((), (), s32[]{:S(2)}) async-start(), calls=%async_computation.19 | async-start | bytes 3768320 | tf_op jit(solution)/shard_map/all_gather | solution.py:217
  121.2 7.2 %collective-permute-start.47 = (bf16[1,4,128,1024]{3,2,1,0:T(8,128)(2,1)}, bf16[1,4,128,1024]{3,2,1,0:T(8,128)(2,1)}, u32[]{:S(2)}, u32[]{:S(2)}) collective-permute-start(bf16[1,4,128,1024]{3,2,1,0:T(8,128)(2,1)} %fusion.86), channel_id=1, source_target_pairs={{0,1},{1,0},{2,3},{3,2},{4,5},{5,4},{6,7},{7,6},{8,9},{9,8},{10,11... | collective-permute-start | bytes 3145736 | tf_op jit(solution)/shard_map/ppermute | solution.py:64
  130.8 7.1 %collective-permute-start.50 = (bf16[1,2,128,512]{3,2,1,0:T(8,128)(2,1)S(1)}, bf16[1,2,128,512]{3,2,1,0:T(8,128)(2,1)S(1)}, u32[]{:S(2)}, u32[]{:S(2)}) collective-permute-start(bf16[1,2,128,512]{3,2,1,0:T(8,128)(2,1)S(1)} %pad_maximum_fusion.39), channel_id=1, source_target_pairs={{0,2},{1,3},{2,0},{3,1},{4,6},{5,7},{6,4},{7,5},{8,10},{9,11},{10,... | collective-permute-start | bytes 786440 | tf_op jit(solution)/shard_map/ppermute | solution.py:64
  131.4 8.4 %collective-permute-start.48 = (bf16[1,2,128,512]{3,2,1,0:T(8,128)(2,1)S(1)}, bf16[1,2,128,512]{3,2,1,0:T(8,128)(2,1)S(1)}, u32[]{:S(2)}, u32[]{:S(2)}) collective-permute-start(bf16[1,2,128,512]{3,2,1,0:T(8,128)(2,1)S(1)} %slice.790), channel_id=1, source_target_pairs={{0,4},{1,5},{2,6},{3,7},{4,0},{5,1},{6,2},{7,3},{8,12},{9,13},{10,... | collective-permute-start | bytes 786440 | tf_op jit(solution)/shard_map/ppermute | solution.py:64
  150.3 9.6 %collective-permute-start.55 = (bf16[1,2,128,512]{3,2,1,0:T(8,128)(2,1)S(1)}, bf16[1,2,128,512]{3,2,1,0:T(8,128)(2,1)S(1)}, u32[]{:S(2)}, u32[]{:S(2)}) collective-permute-start(bf16[1,2,128,512]{3,2,1,0:T(8,128)(2,1)S(1)} %pad_maximum_fusion.41), channel_id=1, source_target_pairs={{0,2},{1,3},{2,0},{3,1},{4,6},{5,7},{6,4},{7,5},{8,10},{9,11},{10,... | collective-permute-start | bytes 786440 | tf_op jit(solution)/shard_map/ppermute | solution.py:64
  150.8 7.8 %collective-permute-start.52 = (bf16[1,128,512]{2,1,0:T(8,128)(2,1)S(1)}, bf16[1,128,512]{2,1,0:T(8,128)(2,1)S(1)}, u32[]{:S(2)}, u32[]{:S(2)}) collective-permute-start(bf16[1,128,512]{2,1,0:T(8,128)(2,1)S(1)} %get-tuple-element.200), channel_id=1, source_target_pairs={{0,2},{1,3},{2,0},{3,1},{4,6},{5,7},{6,4},{7,5},{8,10},{9,11},{10,... | collective-permute-start | bytes 393224 | tf_op jit(solution)/shard_map/ppermute | solution.py:64
  159.4 50.1 %collective-permute-start.53 = (bf16[1,2,128,512]{3,2,1,0:T(8,128)(2,1)}, bf16[1,2,128,512]{3,2,1,0:T(8,128)(2,1)}, u32[]{:S(2)}, u32[]{:S(2)}) collective-permute-start(bf16[1,2,128,512]{3,2,1,0:T(8,128)(2,1)} %pad_maximum_fusion.40), channel_id=1, source_target_pairs={{0,4},{1,5},{2,6},{3,7},{4,0},{5,1},{6,2},{7,3},{8,12},{9,13},{10,... | collective-permute-start | bytes 786440 | tf_op jit(solution)/shard_map/ppermute | solution.py:64
  204.9 25.5 %all-to-all-start.11 = ((bf16[8,128,768]{2,1,0:T(8,128)(2,1)}), bf16[8,128,768]{2,1,0:T(8,128)(2,1)}, u32[]{:S(2)}, u32[]{:S(2)}) async-start(bf16[8,128,768]{2,1,0:T(8,128)(2,1)} %pad_maximum_fusion.29), calls=%async_computation.11 | async-start | bytes 3145728 | tf_op jit(solution)/shard_map/all_to_all | solution.py:68
  247.1 8.4 %collective-permute-start.60 = (bf16[1,2,128,512]{3,2,1,0:T(8,128)(2,1)S(1)}, bf16[1,2,128,512]{3,2,1,0:T(8,128)(2,1)S(1)}, u32[]{:S(2)}, u32[]{:S(2)}) collective-permute-start(bf16[1,2,128,512]{3,2,1,0:T(8,128)(2,1)S(1)} %pad_maximum_fusion.42), channel_id=1, source_target_pairs={{0,2},{1,3},{2,0},{3,1},{4,6},{5,7},{6,4},{7,5},{8,10},{9,11},{10,... | collective-permute-start | bytes 786440 | tf_op jit(solution)/shard_map/ppermute | solution.py:64
  247.7 8.5 %collective-permute-start.58 = (bf16[1,2,128,512]{3,2,1,0:T(8,128)(2,1)S(1)}, bf16[1,2,128,512]{3,2,1,0:T(8,128)(2,1)S(1)}, u32[]{:S(2)}, u32[]{:S(2)}) collective-permute-start(bf16[1,2,128,512]{3,2,1,0:T(8,128)(2,1)S(1)} %slice.816), channel_id=1, source_target_pairs={{0,4},{1,5},{2,6},{3,7},{4,0},{5,1},{6,2},{7,3},{8,12},{9,13},{10,... | collective-permute-start | bytes 786440 | tf_op jit(solution)/shard_map/ppermute | solution.py:64
  264.0 6.4 %collective-permute-start.62 = (bf16[1,128,512]{2,1,0:T(8,128)(2,1)S(1)}, bf16[1,128,512]{2,1,0:T(8,128)(2,1)S(1)}, u32[]{:S(2)}, u32[]{:S(2)}) collective-permute-start(bf16[1,128,512]{2,1,0:T(8,128)(2,1)S(1)} %get-tuple-element.194), channel_id=1, source_target_pairs={{0,2},{1,3},{2,0},{3,1},{4,6},{5,7},{6,4},{7,5},{8,10},{9,11},{10,... | collective-permute-start | bytes 393224 | tf_op jit(solution)/shard_map/ppermute | solution.py:64
  267.6 6.7 %collective-permute-start.65 = (bf16[1,2,128,512]{3,2,1,0:T(8,128)(2,1)S(1)}, bf16[1,2,128,512]{3,2,1,0:T(8,128)(2,1)S(1)}, u32[]{:S(2)}, u32[]{:S(2)}) collective-permute-start(bf16[1,2,128,512]{3,2,1,0:T(8,128)(2,1)S(1)} %pad_maximum_fusion.44), channel_id=1, source_target_pairs={{0,2},{1,3},{2,0},{3,1},{4,6},{5,7},{6,4},{7,5},{8,10},{9,11},{10,... | collective-permute-start | bytes 786440 | tf_op jit(solution)/shard_map/ppermute | solution.py:64
  270.4 6.4 %collective-permute-start.63 = (bf16[1,2,128,512]{3,2,1,0:T(8,128)(2,1)S(1)}, bf16[1,2,128,512]{3,2,1,0:T(8,128)(2,1)S(1)}, u32[]{:S(2)}, u32[]{:S(2)}) collective-permute-start(bf16[1,2,128,512]{3,2,1,0:T(8,128)(2,1)S(1)} %pad_maximum_fusion.43), channel_id=1, source_target_pairs={{0,4},{1,5},{2,6},{3,7},{4,0},{5,1},{6,2},{7,3},{8,12},{9,13},{10,... | collective-permute-start | bytes 786440 | tf_op jit(solution)/shard_map/ppermute | solution.py:64
  299.4 12.4 %all-to-all-start.14 = ((bf16[8,128,192]{1,2,0:T(8,128)(2,1)}), bf16[8,128,192]{1,2,0:T(8,128)(2,1)}, u32[]{:S(2)}, u32[]{:S(2)}) async-start(bf16[8,128,192]{1,2,0:T(8,128)(2,1)} %bitcast.684), calls=%async_computation.15 | async-start | bytes 786432 | tf_op jit(solution)/shard_map/all_to_all | solution.py:68
  303.5 73.5 %reduce-scatter.5.cloned.1.call-start = ((), (), s32[]{:S(2)}) async-start(), calls=%async_computation.21 | async-start | bytes 1310720 | tf_op jit(solution)/shard_map/reduce_scatter | solution.py:236
  323.0 24.5 %all-to-all-start.12 = ((bf16[8,128,768]{1,2,0:T(8,128)(2,1)}), bf16[8,128,768]{1,2,0:T(8,128)(2,1)S(1)}, u32[]{:S(2)}, u32[]{:S(2)}) async-start(bf16[8,128,768]{1,2,0:T(8,128)(2,1)} %copy.273), calls=%async_computation.12 | async-start | bytes 3145728 | tf_op jit(solution)/shard_map/all_to_all | solution.py:68
  326.6 86.6 %reduce-scatter.3.cloned.1.call-start = ((), (), s32[]{:S(2)}) async-start(), calls=%async_computation.20 | async-start | bytes 3768320 | tf_op jit(solution)/shard_map/reduce_scatter | solution.py:236
  374.4 15.1 %collective-permute-start.70 = (bf16[2,2,128,512]{3,2,0,1:T(8,128)(2,1)}, bf16[2,2,128,512]{3,2,0,1:T(8,128)(2,1)}, u32[]{:S(2)}, u32[]{:S(2)}) collective-permute-start(bf16[2,2,128,512]{3,2,0,1:T(8,128)(2,1)} %pad_maximum_fusion.37), channel_id=1, source_target_pairs={{0,2},{1,3},{2,0},{3,1},{4,6},{5,7},{6,4},{7,5},{8,10},{9,11},{10,... | collective-permute-start | bytes 1572872 | tf_op jit(solution)/shard_map/ppermute | solution.py:64
  376.5 17.2 %collective-permute-start.68 = (bf16[2,2,128,512]{3,2,0,1:T(8,128)(2,1)}, bf16[2,2,128,512]{3,2,0,1:T(8,128)(2,1)}, u32[]{:S(2)}, u32[]{:S(2)}) collective-permute-start(bf16[2,2,128,512]{3,2,0,1:T(8,128)(2,1)} %slice.835), channel_id=1, source_target_pairs={{0,4},{1,5},{2,6},{3,7},{4,0},{5,1},{6,2},{7,3},{8,12},{9,13},{10,... | collective-permute-start | bytes 1572872 | tf_op jit(solution)/shard_map/ppermute | solution.py:64
  379.2 36.8 %all-to-all-start.15 = ((bf16[8,24,2048]{2,1,0:T(8,128)(2,1)}), bf16[8,24,2048]{2,1,0:T(8,128)(2,1)S(1)}, u32[]{:S(2)}, u32[]{:S(2)}) async-start(bf16[8,24,2048]{2,1,0:T(8,128)(2,1)} %bitcast.198), calls=%async_computation.17 | async-start | bytes 1572864 | tf_op jit(solution)/shard_map/all_to_all | solution.py:68
  392.5 28.4 %collective-permute-start.71 = (bf16[2,128,512]{2,1,0:T(8,128)(2,1)}, bf16[2,128,512]{2,1,0:T(8,128)(2,1)S(1)}, u32[]{:S(2)}, u32[]{:S(2)}) collective-permute-start(bf16[2,128,512]{2,1,0:T(8,128)(2,1)} %fusion.133), channel_id=1, source_target_pairs={{0,4},{1,5},{2,6},{3,7},{4,0},{5,1},{6,2},{7,3},{8,12},{9,13},{10,... | collective-permute-start | bytes 786440 | tf_op jit(solution)/shard_map/ppermute | solution.py:64
  397.0 25.1 %collective-permute-start.69 = (bf16[2,128,512]{2,1,0:T(8,128)(2,1)}, bf16[2,128,512]{2,1,0:T(8,128)(2,1)}, u32[]{:S(2)}, u32[]{:S(2)}) collective-permute-start(bf16[2,128,512]{2,1,0:T(8,128)(2,1)} %fusion.132), channel_id=1, source_target_pairs={{0,2},{1,3},{2,0},{3,1},{4,6},{5,7},{6,4},{7,5},{8,10},{9,11},{10,... | collective-permute-start | bytes 786440 | tf_op jit(solution)/shard_map/ppermute | solution.py:64
  416.9 24.8 %all-to-all-start.13 = ((bf16[8,48,2048]{2,1,0:T(8,128)(2,1)}), bf16[8,48,2048]{2,1,0:T(8,128)(2,1)S(1)}, u32[]{:S(2)}, u32[]{:S(2)}) async-start(bf16[8,48,2048]{2,1,0:T(8,128)(2,1)} %bitcast.639), calls=%async_computation.14 | async-start | bytes 3145728 | tf_op jit(solution)/shard_map/all_to_all | solution.py:68
  (115 other events, 808.3 us)
Sparse Core Ops, SparseCore 0:
  44.9 27.3 all-gather.2
  128.5 58.8 all-gather.4
  317.7 24.1 reduce-scatter.4
  357.9 55.2 reduce-scatter.2
where the time goes:
time: 473 us; the launch traced here: 464 us
  waiting for transfers between devices  170 us (36%)
  matrix products  77.6 us (16%)
  local copies, waits for them, and re-layouts  76.2 us (16%)
  other arithmetic  60.2 us (13%)
  starting transfers between devices  57.5 us (12%)
  between operations  19.2 us (4%)
    ppermute x30, waiting for transfers between devices, swap(): return lax.ppermute(values, 'tok', [(i, i ^ mask) for i in range(8)])  68.4 us
    all_to_all x8, waiting for transfers between devices, exchange(): return lax.all_to_all(values, 'tok', 0, 0, tiled=True)  52.6 us
    all_gather x2, waiting for transfers between devices, fetch(): rows = lax.all_gather(rows, 'seq', axis=0, tiled=True)  35.7 us
    all_to_all x8, starting transfers between devices, exchange(): return lax.all_to_all(values, 'tok', 0, 0, tiled=True)  33.2 us
    dot_general x12, matrix products, left_product(): lax.dot_general(left, right, (((0,), (0,)), ((), ())), preferred_element_...  26.4 us
    ppermute x30, starting transfers between devices, swap(): return lax.ppermute(values, 'tok', [(i, i ^ mask) for i in range(8)])  24 us
    dot_general x11, matrix products, product(): return jnp.dot(left, right, preferred_element_type=F32)  22.8 us
    unnamed x211, local copies, waits for them, and re-layouts  16.1 us
  transfers between devices with their start and end apart: 42, of which 28 were waited for; matrix products, arithmetic and copies ran while one was open for 30% of the time, Pallas kernels for 0%

commit v1 on v0

--- a/solution.py
+++ b/solution.py
@@ -3,6 +3,8 @@
 import jax
 import jax.numpy as jnp
 from jax import lax
+from jax.experimental import pallas as pl
+from jax.experimental.pallas import tpu as pltpu
 from jax.sharding import PartitionSpec as P
 
 
@@ -68,30 +70,33 @@
     return lax.all_to_all(values, "tok", 0, 0, tiled=True)
 
 
-def gather_rows(rows, tok):
-    if tok != 8:
-        return lax.all_gather(rows, "tok", axis=1, tiled=False)
-    half = rows.shape[2] // 2
+def gather_rows(rows):
+    return lax.all_gather(rows, "tok", axis=0, tiled=True)
+
+
+def scatter_sum(parts, tok):
+    sent = parts.astype(BF).reshape(tok, -1, parts.shape[1])
+    return jnp.sum(exchange(sent).astype(F32), axis=0)
+
+
+def gather_of_eight(rows):
+    count, height, width = rows.shape
+    half = width // 2
     a, b = rows[:, :, :half], rows[:, :, half:]
     ax, by = swap(a, 2), swap(b, 4)
     a2, b2 = jnp.stack([a, ax], 1), jnp.stack([b, by], 1)
     ay, bx = swap(a2, 4), swap(b2, 2)
     first = jnp.concatenate([a2, ay], 1)
     second = jnp.stack([b, bx[:, 0], by, bx[:, 1]], 1)
-    full = jnp.concatenate([first, second], -1)
-    other = swap(full, 1)
-    count = rows.shape[0]
-    return jnp.stack([full, other], 2).reshape((count, 8) + rows.shape[1:])
-
-
-def scatter_sum(parts, tok):
-    if tok != 8:
-        sent = lax.all_to_all(parts.astype(BF), "tok", 1, 1, tiled=True)
-        return jnp.sum(sent.astype(F32), axis=1)
-    many, _, count, width = parts.shape
+    near = jnp.concatenate([first, second], -1).reshape(count, 4 * height, width)
+    return near, swap(near, 1)
+
+
+def scatter_of_eight(keep, send):
+    many, height, width = keep.shape
     half = width // 2
-    pairs = parts.reshape(many, 4, 2, count, width)
-    mine = pairs[:, :, 0] + swap(pairs[:, :, 1].astype(BF), 1).astype(F32)
+    mine = keep.astype(F32) + swap(send, 1).astype(F32)
+    mine = mine.reshape(many, 4, height // 4, width)
     a, b = mine[..., :half], mine[..., half:]
     got_a = swap(a[:, 2:].astype(BF), 4)
     got_b = swap(jnp.stack([b[:, 1], b[:, 3]], 1).astype(BF), 2)
@@ -109,14 +114,35 @@
 def sharded(per_block, tok, group, fill):
     pieces = []
     if group == 0:
-        pieces.append(jnp.broadcast_to(per_block[:1][None], (tok, 1)))
+        first = jnp.broadcast_to(per_block[:1][None], (tok, 1))
+        pieces.append(jnp.pad(first, ((0, 0), (0, 7)), constant_values=fill))
     for k in GROUPS[group]:
         piece = lax.slice_in_dim(per_block, MATRIX_STARTS[k], MATRIX_STARTS[k] + MATRIX_BLOCKS[k])
         if k == 6:
             missing = tok * ff_share(tok) * D // BLK - MATRIX_BLOCKS[k]
             piece = jnp.pad(piece, (0, missing), constant_values=fill)
-        pieces.append(piece.reshape(tok, -1))
+        piece = piece.reshape(tok, -1)
+        missing = -piece.shape[1] % 8
+        pieces.append(jnp.pad(piece, ((0, 0), (0, missing)), constant_values=fill))
     return jnp.concatenate(pieces, axis=1)
+
+
+def piece_of(shard, tok, group, k):
+    offset = 0
+    for other in (-1,) * (group == 0) + GROUPS[group]:
+        if other == -1:
+            count = 1
+        elif other == 6:
+            count = ff_share(tok) * D // BLK
+        else:
+            count = MATRIX_BLOCKS[other] // tok
+        if other == k:
+            return shard[offset : offset + count]
+        offset += round_up(count, 8)
+
+
+def joined(pieces):
+    return jnp.concatenate([jnp.pad(p, ((0, -p.shape[0] % 8), (0, 0))) for p in pieces], axis=0)
 
 
 def rotate(values, count):
@@ -201,21 +227,20 @@
         from_pairs = onehot(arrive, tok * self.pair_cap)
         to_rows = onehot(jnp.where(my_seq == me_seq, my_row, -1), self.row_cap)
         self.compact = left_product(to_rows, from_pairs).astype(BF)
-        self.place = onehot(
-            jnp.where(
-                (my_row < self.row_cap) & (my_owner >= 0),
-                my_seq * self.row_cap + my_row,
-                -1,
-            ),
-            seq * self.row_cap,
+        my_place = jnp.where(
+            (my_row < self.row_cap) & (my_owner >= 0), my_seq * self.row_cap + my_row, -1
         )
+        self.place = onehot(my_place, seq * self.row_cap)
+        self.place_back = (
+            jnp.arange(seq * self.row_cap, dtype=jnp.int32)[:, None] == my_place[None, :]
+        ).astype(BF)
 
     def fetch(self, rounded):
         packed = left_product(self.send, rounded).astype(BF)
         packed = exchange(packed)
         rows = product(self.compact, packed).astype(BF)
         rows = lax.all_gather(rows, "seq", axis=0, tiled=True)
-        return product(self.place, rows).astype(BF)
+        return self.place, rows
 
     def fetch_any(self, rounded):
         width = rounded.shape[1]
@@ -229,19 +254,18 @@
         for _ in range(self.seq - 1):
             mine = rotate(mine, self.seq)
             total = total + mine
-        return total
-
-    def give(self, grads):
-        rows = left_product(self.place, grads).astype(BF)
+        return jnp.eye(self.size, dtype=BF), total
+
+    def give(self, rows):
         rows = lax.psum_scatter(rows, "seq", scatter_dimension=0, tiled=True)
         packed = left_product(self.compact, rows).astype(BF)
         packed = exchange(packed)
         return product(self.send, packed)
 
-    def give_any(self, grads):
-        width = grads.shape[1]
-        total = grads.astype(F32)
-        passing = grads
+    def give_any(self, rows):
+        width = rows.shape[1]
+        total = rows.astype(F32)
+        passing = rows
         for _ in range(self.seq - 1):
             passing = rotate(passing, self.seq)
             total = total + passing.astype(F32)
@@ -307,10 +331,14 @@
     slots = slot_ranks(owners, seq * tok)
     routes = [Route(owners, slots, group, seq, tok, capacity) for group in range(2)]
     rounded = master.astype(BF)
-    found = layer(tokens, cotangent, rounded, [(r.fetch, r.give) for r in routes])
+    layer = layer_of_eight if tok == 8 else layer_of_any
+    found = layer(
+        tokens, cotangent, rounded, [(r.fetch, r.place_back, r.give) for r in routes]
+    )
 
     def any_owners(tokens, cotangent, rounded, *found):
-        return layer(tokens, cotangent, rounded, [(r.fetch_any, r.give_any) for r in routes])
+        plain = [(r.fetch_any, jnp.eye(r.size, dtype=BF), r.give_any) for r in routes]
+        return layer(tokens, cotangent, rounded, plain)
 
     result, grad_input, reduced = lax.cond(
         routes[0].fits & routes[1].fits,
@@ -336,9 +364,300 @@
     return (result[None], grad_input[None], reduced, first, second, updated)
 
 
-def layer(tokens, cotangent, rounded, routes):
+def call(kernel, outs, scratch=(), scalars=0, operands=0, flops=0, nbytes=0):
+    return pl.pallas_call(
+        kernel,
+        out_shape=[jax.ShapeDtypeStruct(shape, kind) for shape, kind in outs],
+        in_specs=[pl.BlockSpec(memory_space=pltpu.SMEM)] * scalars
+        + [pl.BlockSpec(memory_space=pltpu.VMEM)] * (operands - scalars),
+        scratch_shapes=[pltpu.VMEM(shape, kind) for shape, kind in scratch],
+        compiler_params=pltpu.CompilerParams(vmem_limit_bytes=60 * 1024 * 1024),
+        cost_estimate=pl.CostEstimate(flops=flops, bytes_accessed=nbytes, transcendentals=0),
+    )
+
+
+def dot(left, right):
+    return jnp.dot(left, right, preferred_element_type=F32)
+
+
+def low_lanes(shape):
+    return lax.broadcasted_iota(jnp.int32, shape, 1) < 64
+
+
+def unpack_ff(place_ref, rows_ref, sent_ref, down_ref, flat, wide, tall):
+    for c in range(16):
+        lanes = pl.ds(128 * c, 128)
+        found = dot(place_ref[...], rows_ref[:, lanes])
+        flat[0, pl.ds(c, 176, stride=16), :] = found[:176]
+        flat[1, pl.ds(c, 176, stride=16), :] = found[176:352]
+        tall[c % 8, pl.ds(c // 8, 192, stride=2), :] = found[352:]
+    for k in range(8):
+        down_ref[:, pl.ds(128 * k, 128)] = tall[k].astype(BF)
+    low = low_lanes((64, 128))
+    zero = jnp.zeros((64, 128), F32)
+    for m in range(2):
+        for k in range(24):
+            if k > 21:
+                wide[k] = jnp.zeros((128, 128), F32)
+                continue
+            even = flat[m, pl.ds(k, 64, stride=43), :]
+            first = flat[m, pl.ds(21 + k, 64, stride=43), :]
+            second = flat[m, pl.ds(22 + k, 64, stride=43), :] if k < 21 else zero
+            if k == 21:
+                even = jnp.where(low, even, 0.0)
+            odd = pltpu.roll(jnp.where(low, second, first), 64, 1)
+            wide[k, pl.ds(0, 64, stride=2), :] = even
+            wide[k, pl.ds(1, 64, stride=2), :] = odd
+        for k in range(24):
+            sent_ref[k // 3, :, pl.ds(384 * m + 128 * (k % 3), 128)] = wide[k].astype(BF)
+
+
+def pack_ff(place_ref, back_ref, down_ref, rows_ref, flat, wide, tall):
+    low = low_lanes((64, 128))
+    for m in range(2):
+        flat[m, pl.ds(2752, 64), :] = jnp.zeros((64, 128), F32)
+        for k in range(22):
+            wide[k] = back_ref[k // 3, :, pl.ds(384 * m + 128 * (k % 3), 128)].astype(F32)
+
+        def turned(k):
+            return pltpu.roll(wide[k, pl.ds(1, 64, stride=2), :], 64, 1)
+
+        for k in range(21):
+            flat[m, pl.ds(k, 64, stride=43), :] = wide[k, pl.ds(0, 64, stride=2), :]
+        after = turned(0)
+        flat[m, pl.ds(21, 64, stride=43), :] = jnp.where(
+            low, wide[21, pl.ds(0, 64, stride=2), :], after
+        )
+        for k in range(21):
+            current, after = after, turned(k + 1)
+            flat[m, pl.ds(22 + k, 64, stride=43), :] = jnp.where(low, current, after)
+    for k in range(8):
+        tall[k] = down_ref[:, pl.ds(128 * k, 128)].astype(F32)
+    for c in range(16):
+        grads = jnp.concatenate(
+            [
+                flat[0, pl.ds(c, 176, stride=16), :],
+                flat[1, pl.ds(c, 176, stride=16), :],
+                tall[c % 8, pl.ds(c // 8, 192, stride=2), :],
+            ],
+            axis=0,
+        ).astype(BF)
+        rows_ref[:, pl.ds(128 * c, 128)] = dot(place_ref[...], grads).astype(BF)
+
+
+def unpack_mix(place_ref, rows_ref, gains_ref, sent_ref, out_ref, thin, tall):
+    for c in range(16):
+        lanes = pl.ds(128 * c, 128)
+        found = dot(place_ref[...], rows_ref[:, lanes])
+        gains_ref[:, lanes] = found[:8]
+        thin[c % 2, pl.ds(c // 2, 16, stride=8), :] = found[8:24]
+        thin[2 + c % 2, pl.ds(c // 2, 16, stride=8), :] = found[24:40]
+        tall[c % 8, pl.ds(c // 8, 64, stride=2), :] = found[40:104]
+        tall[8 + c % 8, pl.ds(c // 8, 64, stride=2), :] = found[104:]
+    lane = lax.broadcasted_iota(jnp.int32, (128, 128), 1)
+    for t in range(8):
+        sent_ref[t, :, pl.ds(0, 128)] = tall[t].astype(BF)
+        query, keys = thin[t // 4], thin[2 + t // 4]
+        if t % 4 != 0:
+            query = pltpu.roll(query, 128 - 32 * (t % 4), 1)
+        if t % 4 != 1:
+            keys = pltpu.roll(keys, (160 - 32 * (t % 4)) % 128, 1)
+        both = jnp.where(lane < 32, query, jnp.where(lane < 64, keys, 0.0))
+        sent_ref[t, :, pl.ds(128, 128)] = both.astype(BF)
+        out_ref[:, pl.ds(128 * t, 128)] = tall[8 + t].astype(BF)
+
+
+def pack_mix(place_ref, gains_ref, back_ref, out_ref, rows_ref, thin, tall):
+    lane = lax.broadcasted_iota(jnp.int32, (128, 128), 1)
+    for j in range(2):
+        query = jnp.zeros((128, 128), F32)
+        keys = jnp.zeros((128, 128), F32)
+        for u in range(4):
+            both = back_ref[4 * j + u, :, pl.ds(128, 128)].astype(F32)
+            here = (lane >= 32 * u) & (lane < 32 * u + 32)
+            moved = pltpu.roll(both, 32 * u, 1) if u else both
+            query = jnp.where(here, moved, query)
+            moved = pltpu.roll(both, (96 + 32 * u) % 128, 1) if u != 1 else both
+            keys = jnp.where(here, moved, keys)
+        thin[j] = query
+        thin[2 + j] = keys
+    for t in range(8):
+        tall[t] = back_ref[t, :, pl.ds(0, 128)].astype(F32)
+        tall[8 + t] = out_ref[:, pl.ds(128 * t, 128)].astype(F32)
+    for c in range(16):
+        lanes = pl.ds(128 * c, 128)
+        grads = jnp.concatenate(
+            [
+                gains_ref[:, lanes],
+                thin[c % 2, pl.ds(c // 2, 16, stride=8), :],
+                thin[2 + c % 2, pl.ds(c // 2, 16, stride=8), :],
+                tall[c % 8, pl.ds(c // 8, 64, stride=2), :],
+                tall[8 + c % 8, pl.ds(c // 8, 64, stride=2), :],
+            ],
+            axis=0,
+        ).astype(BF)
+        rows_ref[:, lanes] = dot(place_ref[...], grads).astype(BF)
+
+
+ROWS = 256
+
+
+def feed_forward(h0, h1, c0, c1, w_in, w_down, hidden_ref, grad_ref, keep, send, result_keep, result_send):
+    for half, (h_ref, c_ref, out, result) in enumerate(
+        ((h0, c0, keep, result_keep), (h1, c1, send, result_send))
+    ):
+
+        def block(i, carry, half=half, h_ref=h_ref, c_ref=c_ref, out=out, result=result):
+            here = pl.ds(pl.multiple_of(i * ROWS, ROWS), ROWS)
+            there = pl.ds(pl.multiple_of(i * ROWS + 512 * half, ROWS), ROWS)
+            gate_up = dot(h_ref[0, here, :], w_in[...])
+            gate, up = gate_up[:, :384], gate_up[:, 384:]
+            sigmoid = jax.nn.sigmoid(gate)
+            active = gate * sigmoid
+            hidden = (active * up).astype(BF)
+            hidden_ref[there, :] = hidden
+            grad_hidden = right_product(c_ref[1, here, :], w_down[...])
+            grad_gate = grad_hidden * up * sigmoid * (1.0 + gate * (1.0 - sigmoid))
+            grads = jnp.concatenate([grad_gate, grad_hidden * active], axis=1).astype(BF)
+            grad_ref[there, :] = grads
+            out[0, here, :] = right_product(grads, w_in[...]).astype(BF)
+            result[here, :] = dot(hidden, w_down[...]).astype(BF)
+            return carry
+
+        lax.fori_loop(0, 512 // ROWS, block, 0)
+
+
+def token_at(index, me):
+    group = index >> 7
+    far = ((group & 3) << 1) | (group >> 2)
+    return ((far ^ me) << 7) | (index & 127)
+
+
+def pair_weights(query, keys, first, me):
+    inner = right_product(query, keys) * (1.0 / math.sqrt(FD))
+    row = lax.broadcasted_iota(jnp.int32, inner.shape, 0) + first
+    column = lax.broadcasted_iota(jnp.int32, inner.shape, 1)
+    causal = token_at(row, me) >= token_at(column, me)
+    return inner, jnp.where(causal, 1.0 + inner + 0.5 * inner * inner, 0.0), causal
+
+
+def mix(me_ref, x0, x1, gain, w_in, w_out, hidden_ref, qkv, mixed_ref, mean_ref, total_ref, keep, send):
+    me = me_ref[0]
+    for half, x_ref in enumerate((x0, x1)):
+
+        def block(i, carry, half=half, x_ref=x_ref):
+            here = pl.ds(pl.multiple_of(i * ROWS, ROWS), ROWS)
+            there = pl.ds(pl.multiple_of(i * ROWS + 512 * half, ROWS), ROWS)
+            x = x_ref[0, here, :].astype(F32)
+            scale = lax.rsqrt(jnp.mean(x * x, axis=1, keepdims=True) + NORM_EPSILON)
+            hidden = (x * scale * gain[0:1, :]).astype(BF)
+            hidden_ref[there, :] = hidden
+            qkv[there, :] = dot(hidden, w_in[...]).astype(BF)
+            return carry
+
+        lax.fori_loop(0, 512 // ROWS, block, 0)
+    for half, out in enumerate((keep, send)):
+
+        def block(i, carry, half=half, out=out):
+            first = pl.multiple_of(i * ROWS + 512 * half, ROWS)
+            there = pl.ds(first, ROWS)
+            means, totals = [], []
+            for u in range(2):
+                query = qkv[there, pl.ds(128, 128)][:, 16 * u : 16 * u + 16]
+                keys = qkv[:, pl.ds(128, 128)][:, 32 + 16 * u : 48 + 16 * u]
+                values = qkv[:, pl.ds(0, 128)][:, 64 * u : 64 * u + 64]
+                _, weight, _ = pair_weights(query, keys, first, me)
+                total = jnp.sum(weight, axis=1, keepdims=True)
+                means.append(dot(weight.astype(BF), values) / total)
+                totals.append(jnp.broadcast_to(total, (ROWS, 64)))
+            mean = jnp.concatenate(means, axis=1)
+            mean_ref[there, :] = mean
+            total_ref[there, :] = jnp.concatenate(totals, axis=1)
+            mixed = mean.astype(BF)
+            mixed_ref[there, :] = mixed
+            here = pl.ds(pl.multiple_of(i * ROWS, ROWS), ROWS)
+            out[0, here, :] = dot(mixed, w_out[...]).astype(BF)
+            return carry
+
+        lax.fori_loop(0, 512 // ROWS, block, 0)
+
+
+def mix_back(
+    me_ref, m0, m1, x0, x1, w_in, w_out, qkv, mixed_ref, mean_ref, total_ref, result_keep, result_send,
+    grad_ref, keep, send, gain_ref, out_grad, numer, denom, back_keys, back_values, back_out,
+):
+    me = me_ref[0]
+    keep[0] = result_keep[...]
+    send[0] = result_send[...]
+    back_out[...] = jnp.zeros_like(back_out)
+    for half, m_ref in enumerate((m0, m1)):
+
+        def block(i, carry, half=half, m_ref=m_ref):
+            here = pl.ds(pl.multiple_of(i * ROWS, ROWS), ROWS)
+            there = pl.ds(pl.multiple_of(i * ROWS + 512 * half, ROWS), ROWS)
+            grad = right_product(m_ref[0, here, :], w_out[...]).astype(BF).astype(F32)
+            back_out[...] += left_product(mixed_ref[there, :], m_ref[0, here, :])
+            total = total_ref[there, :]
+            numer[there, :] = (grad / total).astype(BF)
+            lean = grad * mean_ref[there, :]
+            sums = [jnp.sum(lean[:, 64 * u : 64 * u + 64], axis=1, keepdims=True) for u in range(2)]
+            wide = jnp.concatenate([jnp.broadcast_to(s, (ROWS, 64)) for s in sums], axis=1)
+            denom[there, :] = -wide / total
+            return carry
+
+        lax.fori_loop(0, 512 // ROWS, block, 0)
+    out_grad[...] = back_out[...].astype(BF)
+    back_keys[...] = jnp.zeros_like(back_keys)
+    back_values[...] = jnp.zeros_like(back_values)
+
+    def pairs(i, carry):
+        first = pl.multiple_of(i * ROWS, ROWS)
+        there = pl.ds(first, ROWS)
+        query_grads = []
+        for u in range(2):
+            query = qkv[there, pl.ds(128, 128)][:, 16 * u : 16 * u + 16]
+            keys = qkv[:, pl.ds(128, 128)][:, 32 + 16 * u : 48 + 16 * u]
+            values = qkv[:, pl.ds(0, 128)][:, 64 * u : 64 * u + 64]
+            inner, weight, causal = pair_weights(query, keys, first, me)
+            down = numer[there, :][:, 64 * u : 64 * u + 64]
+            grad_weight = right_product(down, values) + denom[there, :][:, 64 * u : 64 * u + 1]
+            grad_inner = (
+                jnp.where(causal, grad_weight * (1.0 + inner), 0.0) * (1.0 / math.sqrt(FD))
+            ).astype(BF)
+            query_grads.append(dot(grad_inner, keys))
+            back_keys[u] += left_product(grad_inner, query)
+            back_values[u] += left_product(weight.astype(BF), down)
+        grad_ref[there, pl.ds(128, 128)] = jnp.concatenate(
+            query_grads + [jnp.zeros((ROWS, 96), F32)], axis=1
+        ).astype(BF)
+        return carry
+
+    lax.fori_loop(0, 1024 // ROWS, pairs, 0)
+    gain_ref[...] = jnp.zeros_like(gain_ref)
+    for half, (x_ref, out) in enumerate(((x0, keep), (x1, send))):
+
+        def block(i, carry, half=half, x_ref=x_ref, out=out):
+            here = pl.ds(pl.multiple_of(i * ROWS, ROWS), ROWS)
+            there = pl.ds(pl.multiple_of(i * ROWS + 512 * half, ROWS), ROWS)
+            query_grad = grad_ref[there, pl.ds(128, 128)][:, :32]
+            keys_grad = [back_keys[u, there, :].astype(BF) for u in range(2)]
+            values_grad = [back_values[u, there, :].astype(BF) for u in range(2)]
+            grads = jnp.concatenate(
+                values_grad + [query_grad] + keys_grad + [jnp.zeros((ROWS, 64), BF)], axis=1
+            )
+            grad_ref[there, :] = grads
+            terms = right_product(grads, w_in[...])
+            out[1, here, :] = terms.astype(BF)
+            x = x_ref[0, here, :].astype(F32)
+            scale = lax.rsqrt(jnp.mean(x * x, axis=1, keepdims=True) + NORM_EPSILON)
+            gain_ref[0:1, :] += jnp.sum(terms * (x * scale), axis=0, keepdims=True)
+            return carry
+
+        lax.fori_loop(0, 512 // ROWS, block, 0)
+
+
+def layer_of_any(tokens, cotangent, rounded, routes):
     tok = lax.axis_size("tok")
-    me_tok = lax.axis_index("tok")
     row_count = tokens.shape[1]
     seq_len = row_count * tok
     value_split = max(1, tok // HEADS)
@@ -349,14 +668,12 @@
     qk_width = units * FD
     v_width = units * unit_width
 
-    both = gather_rows(jnp.concatenate([tokens, cotangent]), tok)
-    x_all, c_all = both[0].reshape(seq_len, D), both[1].reshape(seq_len, D)
-
-    shard = routes[0][0](rounded)
+    x_all, c_all = gather_rows(tokens[0]), gather_rows(cotangent[0])
+
+    place, rows = routes[0][0](rounded)
+    shard = product(place, rows).astype(BF)
     gain_one = shard[0, :D].astype(F32)
     gain_two = shard[0, D:].astype(F32)
-    shard = shard[1:]
-    a, b, c, _ = (MATRIX_BLOCKS[k] // tok for k in GROUPS[0])
 
     def spread(columns):
         wide = columns.reshape(slice_rows, tok // value_split, 1, qk_width)
@@ -366,29 +683,29 @@
 
     sent = jnp.concatenate(
         [
-            spread(shard[:a].reshape(slice_rows, HEADS * FD)),
-            spread(shard[a : a + b].reshape(slice_rows, HEADS * FD)),
-            shard[a + b : a + b + c].reshape(slice_rows, tok, v_width),
+            spread(piece_of(shard, tok, 0, 0).reshape(slice_rows, HEADS * FD)),
+            spread(piece_of(shard, tok, 0, 1).reshape(slice_rows, HEADS * FD)),
+            piece_of(shard, tok, 0, 2).reshape(slice_rows, tok, v_width),
         ],
         axis=-1,
     ).transpose(1, 0, 2)
     w_qkv = exchange(sent).reshape(D, -1)
-    w_out = shard[a + b + c :].reshape(v_width, D)
+    w_out = piece_of(shard, tok, 0, 3).reshape(v_width, D)
 
     def padded(blocks):
         return jnp.pad(blocks.reshape(slice_rows, FF), ((0, 0), (0, tok * ff_slice - FF)))
 
-    shard = routes[1][0](rounded)
-    a = MATRIX_BLOCKS[4] // tok
+    place, rows = routes[1][0](rounded)
+    shard = product(place, rows).astype(BF)
     sent = jnp.concatenate(
         [
-            columns_out(padded(shard[:a]), tok),
-            columns_out(padded(shard[a : 2 * a]), tok),
+            columns_out(padded(piece_of(shard, tok, 1, 4)), tok),
+            columns_out(padded(piece_of(shard, tok, 1, 5)), tok),
         ],
         axis=-1,
     )
     w_gate_up = exchange(sent).reshape(D, -1)
-    w_down = shard[2 * a :].reshape(ff_slice, D)
+    w_down = piece_of(shard, tok, 1, 6).reshape(ff_slice, D)
 
     normed_all, _ = normalize(x_all.astype(F32))
     hidden_one = (normed_all * gain_one).astype(BF)
@@ -396,10 +713,7 @@
     query = qkv[:, :qk_width].reshape(seq_len, units, FD).transpose(1, 0, 2)
     keys = qkv[:, qk_width : 2 * qk_width].reshape(seq_len, units, FD).transpose(1, 0, 2)
     values = qkv[:, 2 * qk_width :].reshape(seq_len, units, unit_width).transpose(1, 0, 2)
-    place = jnp.arange(tok, dtype=jnp.int32)
-    if tok == 8:
-        place = place ^ me_tok
-    index = (place[:, None] * row_count + jnp.arange(row_count, dtype=jnp.int32)[None, :]).reshape(-1)
+    index = jnp.arange(seq_len, dtype=jnp.int32)
     causal = (index[:, None] >= index[None, :])[None]
     inner = jnp.einsum("uif,ujf->uij", query, keys, preferred_element_type=F32) * (
         1.0 / math.sqrt(FD)
@@ -410,12 +724,12 @@
         jnp.einsum("uij,ujw->uiw", weight.astype(BF), values, preferred_element_type=F32) / total
     )
     mixed = mixed_f.astype(BF).transpose(1, 0, 2).reshape(seq_len, v_width)
-    out = scatter_sum(product(mixed, w_out).reshape(1, tok, row_count, D), tok)[0]
+    out = scatter_sum(product(mixed, w_out), tok)
 
     input_rows = tokens[0].astype(F32)
     middle = input_rows + out
     normed_two, scale_two = normalize(middle)
-    hidden_two = gather_rows((normed_two * gain_two).astype(BF)[None], tok).reshape(seq_len, D)
+    hidden_two = gather_rows((normed_two * gain_two).astype(BF))
 
     gate_up = product(hidden_two, w_gate_up)
     gate, up_proj = gate_up[:, :ff_slice], gate_up[:, ff_slice:]
@@ -427,14 +741,14 @@
     grad_up = (grad_hidden * activated).astype(BF)
     grad_gate_up = jnp.concatenate([grad_gate, grad_up], axis=1)
     grad_two_terms = right_product(grad_gate_up, w_gate_up)
-    grad_hidden_two = scatter_sum(grad_two_terms.reshape(1, tok, row_count, D), tok)[0]
+    grad_hidden_two = scatter_sum(grad_two_terms, tok)
     result_terms = product(hidden, w_down)
 
     grad_gain_two = jnp.sum(grad_hidden_two * normed_two, axis=0)
     grad_middle = cotangent[0].astype(F32) + norm_back(
         grad_hidden_two * gain_two, normed_two, scale_two
     )
-    grad_mixer = gather_rows(grad_middle.astype(BF)[None], tok).reshape(seq_len, D)
+    grad_mixer = gather_rows(grad_middle.astype(BF))
 
     grad_w_down = left_product(hidden, c_all).astype(BF)
     grad_w_gate_up = left_product(hidden_two, grad_gate_up).astype(BF)
@@ -445,9 +759,8 @@
         return rows[:, :FF].reshape(-1, BLK)
 
     back_gate, back_up = flat(back[..., :ff_slice]), flat(back[..., ff_slice:])
-    reduced = routes[1][1](
-        jnp.concatenate([back_gate, back_up, grad_w_down.reshape(-1, BLK)], axis=0)
-    )
+    blocks = joined([back_gate, back_up, grad_w_down.reshape(-1, BLK)])
+    reduced = routes[1][2](product(routes[1][1], blocks).astype(BF))
 
     grad_w_out = left_product(mixed, grad_mixer).astype(BF)
     grad_mixed = right_product(grad_mixer, w_out).astype(BF)
@@ -475,9 +788,8 @@
     ).astype(BF)
     grad_w_qkv = left_product(hidden_one, grad_qkv).astype(BF)
     grad_one_terms = right_product(grad_qkv, w_qkv)
-    terms = jnp.stack([result_terms, grad_one_terms]).reshape(2, tok, row_count, D)
-    out_sum, grad_hidden_one = scatter_sum(terms, tok)
-    result = (middle + out_sum).astype(BF)
+    grad_hidden_one = scatter_sum(grad_one_terms, tok)
+    result = (middle + scatter_sum(result_terms, tok)).astype(BF)
     grad_gains = jnp.concatenate([jnp.sum(grad_one_terms * normed_all, axis=0), grad_gain_two])
     back = exchange(grad_w_qkv.reshape(tok, slice_rows, -1)).transpose(1, 0, 2)
 
@@ -488,21 +800,150 @@
             ).astype(BF)
         return columns.reshape(-1, BLK)
 
-    reduced = reduced + routes[0][1](
-        jnp.concatenate(
-            [
-                grad_gains.astype(BF).reshape(1, BLK),
-                gathered(back[..., :qk_width]),
-                gathered(back[..., qk_width : 2 * qk_width]),
-                back[..., 2 * qk_width :].reshape(-1, BLK),
-                grad_w_out.reshape(-1, BLK),
-            ],
-            axis=0,
-        )
-    )
+    blocks = joined(
+        [
+            grad_gains.astype(BF).reshape(1, BLK),
+            gathered(back[..., :qk_width]),
+            gathered(back[..., qk_width : 2 * qk_width]),
+            back[..., 2 * qk_width :].reshape(-1, BLK),
+            grad_w_out.reshape(-1, BLK),
+        ]
+    )
+    reduced = reduced + routes[0][2](product(routes[0][1], blocks).astype(BF))
 
     normed_one, scale_one = normalize(input_rows)
     grad_input = grad_middle + norm_back(grad_hidden_one * gain_one, normed_one, scale_one)
+    return result, grad_input.astype(BF), reduced
+
+
+def layer_of_eight(tokens, cotangent, rounded, routes):
+    me_tok = lax.axis_index("tok").astype(jnp.int32).reshape(1)
+    seq_len = 8 * tokens.shape[1]
+    half = seq_len // 2
+    x_near, x_far = gather_of_eight(jnp.concatenate([tokens, cotangent]))
+
+    place, rows = routes[0][0](rounded)
+    gains, sent, w_out = call(
+        unpack_mix,
+        [((8, BLK), F32), ((8, 128, 256), BF), ((128, D), BF)],
+        [((4, 128, 128), F32), ((16, 128, 128), F32)],
+        operands=2,
+        flops=2 * place.shape[0] * place.shape[1] * BLK,
+        nbytes=2 << 20,
+    )(place, rows)
+    w_qkv = exchange(sent).reshape(D, 256)
+    place, rows = routes[1][0](rounded)
+    sent, w_down = call(
+        unpack_ff,
+        [((8, 128, 768), BF), ((384, D), BF)],
+        [((2, 2816, 128), F32), ((24, 128, 128), F32), ((8, 384, 128), F32)],
+        operands=2,
+        flops=2 * place.shape[0] * place.shape[1] * BLK,
+        nbytes=6 << 20,
+    )(place, rows)
+    w_in = exchange(sent).reshape(D, 768)
+
+    hidden_one, qkv, mixed, mean, total, keep, send = call(
+        mix,
+        [
+            ((seq_len, D), BF),
+            ((seq_len, 256), BF),
+            ((seq_len, 128), BF),
+            ((seq_len, 128), F32),
+            ((seq_len, 128), F32),
+            ((1, half, D), BF),
+            ((1, half, D), BF),
+        ],
+        scalars=1,
+        operands=6,
+        flops=2 * seq_len * D * (256 + 128) + 4 * 2 * seq_len * seq_len * 256,
+        nbytes=10 << 20,
+    )(me_tok, x_near, x_far, gains[:, :D], w_qkv, w_out)
+    out = scatter_of_eight(keep, send)[0]
+
+    input_rows = tokens[0].astype(F32)
+    middle = input_rows + out
+    normed_two, scale_two = normalize(middle)
+    gain_two = gains[0, D:]
+    h_near, h_far = gather_of_eight((normed_two * gain_two).astype(BF)[None])
+
+    hidden, grad_gate_up, keep, send, result_keep, result_send = call(
+        feed_forward,
+        [
+            ((seq_len, 384), BF),
+            ((seq_len, 768), BF),
+            ((1, half, D), BF),
+            ((1, half, D), BF),
+            ((half, D), BF),
+            ((half, D), BF),
+        ],
+        operands=6,
+        flops=2 * seq_len * D * (768 * 2 + 384 * 2),
+        nbytes=14 << 20,
+    )(h_near, h_far, x_near, x_far, w_in, w_down)
+    grad_hidden_two = scatter_of_eight(keep, send)[0]
+    grad_gain_two = jnp.sum(grad_hidden_two * normed_two, axis=0)
+    grad_middle = cotangent[0].astype(F32) + norm_back(
+        grad_hidden_two * gain_two, normed_two, scale_two
+    )
+    m_near, m_far = gather_of_eight(grad_middle.astype(BF)[None])
+
+    grad_w_in = left_product(jnp.concatenate([h_near[0], h_far[0]]), grad_gate_up).astype(BF)
+    grad_w_down = left_product(hidden, jnp.concatenate([x_near[1], x_far[1]])).astype(BF)
+    back = exchange(grad_w_in.reshape(8, 128, 768))
+    (rows,) = call(
+        pack_ff,
+        [((routes[1][1].shape[0], BLK), BF)],
+        [((2, 2816, 128), F32), ((24, 128, 128), F32), ((8, 384, 128), F32)],
+        operands=3,
+        flops=2 * routes[1][1].size * BLK,
+        nbytes=6 << 20,
+    )(routes[1][1], back, grad_w_down)
+    reduced = routes[1][2](rows)
+
+    grad_qkv, keep, send, gain_terms, grad_w_out = call(
+        mix_back,
+        [
+            ((seq_len, 256), BF),
+            ((2, half, D), BF),
+            ((2, half, D), BF),
+            ((8, D), F32),
+            ((128, D), BF),
+        ],
+        [
+            ((seq_len, 128), BF),
+            ((seq_len, 128), F32),
+            ((2, seq_len, 16), F32),
+            ((2, seq_len, 64), F32),
+            ((128, D), F32),
+        ],
+        scalars=1,
+        operands=13,
+        flops=2 * seq_len * D * (256 + 256) + 10 * 2 * seq_len * seq_len * 256,
+        nbytes=20 << 20,
+    )(
+        me_tok, m_near, m_far, x_near, x_far, w_qkv, w_out, qkv, mixed, mean, total,
+        result_keep, result_send,
+    )
+    grad_w_qkv = left_product(hidden_one, grad_qkv).astype(BF)
+    back = exchange(grad_w_qkv.reshape(8, 128, 256))
+    out_sum, grad_hidden_one = scatter_of_eight(keep, send)
+    result = (middle + out_sum).astype(BF)
+    grad_gains = jnp.concatenate([gain_terms[0], grad_gain_two])
+    (rows,) = call(
+        pack_mix,
+        [((routes[0][1].shape[0], BLK), BF)],
+        [((4, 128, 128), F32), ((16, 128, 128), F32)],
+        operands=4,
+        flops=2 * routes[0][1].size * BLK,
+        nbytes=2 << 20,
+    )(routes[0][1], jnp.pad(grad_gains[None], ((0, 7), (0, 0))), back, grad_w_out)
+    reduced = reduced + routes[0][2](rows)
+
+    normed_one, scale_one = normalize(input_rows)
+    grad_input = grad_middle + norm_back(
+        grad_hidden_one * gains[0, :D], normed_one, scale_one
+    )
     return result, grad_input.astype(BF), reduced
 
 

time: 473 us -> 455 us (0.962)
  Pallas kernels: 0 us -> 66.3 us
  local copies, waits for them, and re-layouts: 76.2 us -> 26.3 us
  matrix products: 77.6 us -> 29 us
  waiting for transfers between devices: 170 us -> 200 us
  other arithmetic: 60.2 us -> 44.4 us
    pallas_call x0 -> x7, Pallas kernels: none -> 66.3 us  [the longest x1 19.7 us: layer_of_eight(): call(mix_back, [((seq_len, 256), BF), ((2, half, D), BF), ((2, half, D),...]
    dot_general x10 -> x0, matrix products: 26.6 us -> none  [the longest x4 11 us: right_product(): lax.dot_general(left, right, (((1,), (1,)), ((), ())), preferred_element_...]
    reshape x33 -> x14, local copies, waits for them, and re-layouts: 24.6 us -> 1.07 us  [sharded(): piece = piece.reshape(tok, -1)]
    dot_general x11 -> x5, matrix products: 22.8 us -> 7.82 us  [product(): return jnp.dot(left, right, preferred_element_type=F32)]
    another operation x18 -> x11, other arithmetic: 17.3 us -> 3.65 us  [the longest x6 2.45 us: gather_of_eight(): a2, b2 = (jnp.stack([a, ax], 1), jnp.stack([b, by], 1))]
    all_to_all x8, waiting for transfers between devices: 52.6 us -> 65.9 us  [exchange(): return lax.all_to_all(values, 'tok', 0, 0, tiled=True)]
    another operation x12 -> x3, local copies, waits for them, and re-layouts: 11.5 us -> 0.96 us  [gather_of_eight(): a2, b2 = (jnp.stack([a, ax], 1), jnp.stack([b, by], 1))]
    unnamed x211 -> x146, local copies, waits for them, and re-layouts: 16.1 us -> 7.97 us
  transfers between devices with their start and end apart: 42 -> 42, of which waited for: 28 -> 27; matrix products, arithmetic and copies ran while one was open for 30% -> 14% of each run, Pallas kernels for 0% -> 7%
where the time goes in v1:
time: 455 us; the launch traced here: 448 us
  waiting for transfers between devices  200 us (44%)
  Pallas kernels  66.3 us (15%)
  starting transfers between devices  60.8 us (13%)
  other arithmetic  44.4 us (10%)
  matrix products  29 us (6%)
  local copies, waits for them, and re-layouts  26.3 us (6%)
  between operations  18.9 us (4%)
    ppermute x30, waiting for transfers between devices, swap(): return lax.ppermute(values, 'tok', [(i, i ^ mask) for i in range(8)])  73.2 us
    all_to_all x8, waiting for transfers between devices, exchange(): return lax.all_to_all(values, 'tok', 0, 0, tiled=True)  65.9 us
    all_gather x2, waiting for transfers between devices, fetch(): rows = lax.all_gather(rows, 'seq', axis=0, tiled=True)  41.8 us
    all_to_all x8, starting transfers between devices, exchange(): return lax.all_to_all(values, 'tok', 0, 0, tiled=True)  34.5 us
    ppermute x30, starting transfers between devices, swap(): return lax.ppermute(values, 'tok', [(i, i ^ mask) for i in range(8)])  25.8 us
    pallas_call x1, Pallas kernels, layer_of_eight(): call(mix_back, [((seq_len, 256), BF), ((2, half, D), BF), ((2, half, D),...  19.7 us
    dot_general x9, matrix products, left_product(): lax.dot_general(left, right, (((0,), (0,)), ((), ())), preferred_element_...  19.4 us
    reduce_scatter x2, waiting for transfers between devices, give(): rows = lax.psum_scatter(rows, 'seq', scatter_dimension=0, tiled=True)  18.6 us
  transfers between devices with their start and end apart: 42, of which 27 were waited for; matrix products, arithmetic and copies ran while one was open for 14% of the time, Pallas kernels for 7%

profile of v1, /device:TPU:0, one launch (start us, length us, event | category | flops | bytes accessed | tf_op | source)
XLA Modules:
  0.0 448.0 jit_solution(7137958813808157711)
XLA Ops:
  18.5 5.2 %all-to-all-start.8 = ((bf16[8,24,2048]{2,1,0:T(8,128)(2,1)}), bf16[8,24,2048]{2,1,0:T(8,128)(2,1)S(1)}, u32[]{:S(2)}, u32[]{:S(2)}) async-start(bf16[8,24,2048]{2,1,0:T(8,128)(2,1)} %bitcast.70), calls=%async_computation.8 | async-start | bytes 1572864 | tf_op jit(solution)/shard_map/all_to_all | solution.py:70
  30.4 10.6 %collective-permute-done.44 = bf16[2,128,512]{2,1,0:T(8,128)(2,1)S(1)} collective-permute-done((bf16[2,128,512]{2,1,0:T(8,128)(2,1)}, bf16[2,128,512]{2,1,0:T(8,128)(2,1)S(1)}, u32[]{:S(2)}, u32[]{:S(2)}) %collective-permute-start.44) | collective-permute-done | bytes 262176 | tf_op jit(solution)/shard_map/ppermute | solution.py:66
  46.2 9.5 %collective-permute-done.45 = bf16[2,2,128,512]{3,2,0,1:T(8,128)(2,1)} collective-permute-done((bf16[2,2,128,512]{3,2,0,1:T(8,128)(2,1)}, bf16[2,2,128,512]{3,2,0,1:T(8,128)(2,1)}, u32[]{:S(2)}, u32[]{:S(2)}) %collective-permute-start.45) | collective-permute-done | bytes 524320 | tf_op jit(solution)/shard_map/ppermute | solution.py:66
  63.6 10.5 %all-gather.3.cloned.1.call-done.rows_ref = bf16[288,2048]{1,0:T(8,128)(2,1)} async-done(((bf16[72,2048]{1,0:T(8,128)(2,1)}), bf16[288,2048]{1,0:T(8,128)(2,1)}) %all-gather.3.cloned.1.call-update) | async-done | bytes 1179664 | tf_op jit(solution)/shard_map/all_gather | solution.py:242
  74.1 3.3 shard_map.136
  77.4 4.2 all-to-all-start.9
  83.4 7.9 %all-to-all-done.9 = bf16[8,128,256]{2,1,0:T(8,128)(2,1)} async-done(((bf16[8,128,256]{2,1,0:T(8,128)(2,1)}), bf16[8,128,256]{2,1,0:T(8,128)(2,1)}, u32[]{:S(2)}, u32[]{:S(2)}) %all-to-all-start.9) | async-done | bytes 524320 | tf_op jit(solution)/shard_map/all_to_all | solution.py:70
  91.3 4.3 all-to-all-start.10
  100.4 11.4 %shard_map.137 = (bf16[1024,1024]{1,0:T(8,128)(2,1)}, bf16[1024,256]{1,0:T(8,128)(2,1)}, bf16[1024,128]{1,0:T(8,128)(2,1)}, f32[1024,128]{1,0:T(8,128)}, f32[102...) custom-call(s32[1]{0:T(128)} %bitcast.60.me_ref, bf16[2,512,1024]{2,1,0:T(8,128)(2,1)} %bitcast.65.x0.c0, ...), custom_call_target="tpu_custom_call" | custom-call | flops 2952790016 | bytes 10485760 | tf_op jit(solution)/shard_map/pallas_call | solution.py:846
  112.1 4.5 %all-to-all-done.10 = bf16[8,48,2048]{2,1,0:T(8,128)(2,1)} async-done(((bf16[8,48,2048]{2,1,0:T(8,128)(2,1)}), bf16[8,48,2048]{2,1,0:T(8,128)(2,1)}, u32[]{:S(2)}, u32[]{:S(2)}) %all-to-all-start.10) | async-done | bytes 1572896 | tf_op jit(solution)/shard_map/all_to_all | solution.py:70
  124.3 5.1 %collective-permute-done.48 = bf16[1,2,128,512]{3,2,1,0:T(8,128)(2,1)S(1)} collective-permute-done((bf16[1,2,128,512]{3,2,1,0:T(8,128)(2,1)S(1)}, bf16[1,2,128,512]{3,2,1,0:T(8,128)(2,1)S(1)}, u32[]{:S(2)}, u32[]{:S(2)}) %collective-permute-start.48) | collective-permute-done | bytes 262176 | tf_op jit(solution)/shard_map/ppermute | solution.py:66
  147.1 31.2 %all-gather.5.cloned.1.call-done.rows_ref = bf16[736,2048]{1,0:T(8,128)(2,1)} async-done(((bf16[184,2048]{1,0:T(8,128)(2,1)}), bf16[736,2048]{1,0:T(8,128)(2,1)}) %all-gather.5.cloned.1.call-update) | async-done | bytes 3014672 | tf_op jit(solution)/shard_map/all_gather | solution.py:242
  178.3 8.0 %shard_map.138 = (bf16[8,128,768]{2,1,0:T(8,128)(2,1)}, bf16[384,1024]{1,0:T(8,128)(2,1)}) custom-call(bf16[544,736]{1,0:T(8,128)(2,1)} %fusion.61.place_ref, bf16[736,2048]{1,0:T(8,128)(2,1)} %all-gather.5.cloned.1.call-done.rows_ref), custom_call_target="tpu_custom_call" | custom-call | flops 1639972864 | bytes 6291456 | tf_op jit(solution)/shard_map/pallas_call | solution.py:836
  186.3 4.7 %all-to-all-start.11 = ((bf16[8,128,768]{2,1,0:T(8,128)(2,1)}), bf16[8,128,768]{2,1,0:T(8,128)(2,1)}, u32[]{:S(2)}, u32[]{:S(2)}) async-start(bf16[8,128,768]{2,1,0:T(8,128)(2,1)} %get-tuple-element.96), calls=%async_computation.11 | async-start | bytes 3145728 | tf_op jit(solution)/shard_map/all_to_all | solution.py:70
  197.1 14.9 %all-to-all-done.11 = bf16[8,128,768]{2,1,0:T(8,128)(2,1)} async-done(((bf16[8,128,768]{2,1,0:T(8,128)(2,1)}), bf16[8,128,768]{2,1,0:T(8,128)(2,1)}, u32[]{:S(2)}, u32[]{:S(2)}) %all-to-all-start.11) | async-done | bytes 1572896 | tf_op jit(solution)/shard_map/all_to_all | solution.py:70
  212.0 12.0 %shard_map.139 = (bf16[1024,384]{1,0:T(8,128)(2,1)}, bf16[1024,768]{1,0:T(8,128)(2,1)}, bf16[1,512,1024]{2,1,0:T(8,128)(2,1)}, bf16[1,512,1024]{2,1,0:T(8,128)(2...) custom-call(bf16[1,512,1024]{2,1,0:T(8,128)(2,1)} %bitcast.356, ...), custom_call_target="tpu_custom_call" | custom-call | flops 4831838208 | bytes 14680064 | tf_op jit(solution)/shard_map/pallas_call | solution.py:870
  230.1 7.0 %collective-permute-done.58 = bf16[1,2,128,512]{3,2,1,0:T(8,128)(2,1)S(1)} collective-permute-done((bf16[1,2,128,512]{3,2,1,0:T(8,128)(2,1)S(1)}, bf16[1,2,128,512]{3,2,1,0:T(8,128)(2,1)S(1)}, u32[]{:S(2)}, u32[]{:S(2)}) %collective-permute-start.58) | collective-permute-done | bytes 262176 | tf_op jit(solution)/shard_map/ppermute | solution.py:66
  252.0 3.4 collective-permute-done.65
  262.6 19.7 %shard_map.141 = (bf16[1024,256]{1,0:T(8,128)(2,1)}, bf16[2,512,1024]{2,1,0:T(8,128)(2,1)}, bf16[2,512,1024]{2,1,0:T(8,128)(2,1)}, f32[8,1024]{1,0:T(8,128)}, bf16[128,1024]{1,0:T(8,128)(2,1)}) custom-call(s32[1]{0:T(128)} %bitcast.60.me_ref, bf16[1,512,1024]{2,1,0:T(8,128)(2,1)} %bitcast.362, bf16[1,512,1024]{2,1,0:T(8,128)(2,1)} %copy-done.96, ...), custom_call_target="tpu_custom_call" | custom-call | flops 6442450944 | bytes 20971520 | tf_op jit(solution)/shard_map/pallas_call | solution.py:904
  285.5 4.1 all-to-all-start.14
  292.0 7.4 %all-to-all-done.14.back_ref = bf16[8,128,256]{2,1,0:T(8,128)(2,1)} async-done(((bf16[8,128,256]{2,1,0:T(8,128)(2,1)}), bf16[8,128,256]{2,1,0:T(8,128)(2,1)}, u32[]{:S(2)}, u32[]{:S(2)}) %all-to-all-start.14) | async-done | bytes 524320 | tf_op jit(solution)/shard_map/all_to_all | solution.py:70
  302.6 5.1 %fusion.58 = bf16[1024,768]{1,0:T(8,128)(2,1)} fusion(bf16[1024,768]{1,0:T(8,128)(2,1)} %get-tuple-element.98, bf16[512,1024]{1,0:T(8,128)(2,1)} %bitcast.87, bf16[512,1024]{1,0:T(8,128)(2,1)} %bitcast.357), kind=kOutput, calls=%fused_computation.169 | convolution fusion | flops 1615593472 | bytes 5242880 | tf_op jit(solution)/shard_map/dot_general | solution.py:47
  307.6 4.4 all-to-all-start.12
  317.0 16.0 %all-to-all-done.12.back_ref = bf16[8,128,768]{2,1,0:T(8,128)(2,1)} async-done(((bf16[8,128,768]{2,1,0:T(8,128)(2,1)}), bf16[8,128,768]{2,1,0:T(8,128)(2,1)}, u32[]{:S(2)}, u32[]{:S(2)}) %all-to-all-start.12) | async-done | bytes 1572896 | tf_op jit(solution)/shard_map/all_to_all | solution.py:70
  333.1 8.8 %shard_map.140 = bf16[736,2048]{1,0:T(8,128)(2,1)} custom-call(bf16[736,544]{1,0:T(8,128)(2,1)} %fusion.57.place_ref, bf16[8,128,768]{2,1,0:T(8,128)(2,1)} %all-to-all-done.12.back_ref, bf16[384,1024]{1,0:T(8,128)(2,1)} %fusion.62.down_ref), custom_call_target="tpu_custom_call" | custom-call | flops 1639972864 | bytes 6291456 | tf_op jit(solution)/shard_map/pallas_call | solution.py:894
  353.5 11.6 %collective-permute-done.68 = bf16[2,2,128,512]{3,2,0,1:T(8,128)(2,1)S(1)} collective-permute-done((bf16[2,2,128,512]{3,2,0,1:T(8,128)(2,1)S(1)}, bf16[2,2,128,512]{3,2,0,1:T(8,128)(2,1)S(1)}, u32[]{:S(2)}, u32[]{:S(2)}) %collective-permute-start.68) | collective-permute-done | bytes 524320 | tf_op jit(solution)/shard_map/ppermute | solution.py:66
  369.9 3.9 all-to-all-start.15
  378.7 18.6 %reduce-scatter.3.cloned.1.call-done = bf16[184,2048]{1,0:T(8,128)(2,1)} async-done(((bf16[736,2048]{1,0:T(8,128)(2,1)}), bf16[184,2048]{1,0:T(8,128)(2,1)}) %reduce-scatter.3.cloned.1.call-update) | async-done | bytes 753680 | tf_op jit(solution)/shard_map/reduce_scatter | solution.py:260
  401.1 3.7 all-to-all-start.13
  410.6 15.1 %all-to-all-done.13 = bf16[8,48,2048]{2,1,0:T(8,128)(2,1)S(1)} async-done(((bf16[8,48,2048]{2,1,0:T(8,128)(2,1)}), bf16[8,48,2048]{2,1,0:T(8,128)(2,1)S(1)}, u32[]{:S(2)}, u32[]{:S(2)}) %all-to-all-start.13) | async-done | bytes 1572896 | tf_op jit(solution)/shard_map/all_to_all | solution.py:70
  427.8 5.3 %conditional.1 = (f32[255,2048]{1,0:T(8,128)S(1)}, bf16[1,128,1024]{2,1,0:T(8,128)(2,1)}, bf16[1,128,1024]{2,1,0:T(8,128)(2,1)}) conditional(s32[]{:T(128)} %convert_element_type.519, (s32[8,544]{1,0:T(8,128)S(1)}, bf16[1,128,1024]{2,1,0:T(8,128)(2,1)S(1)}, bf16[1,128,1024]{2,1,0:T(8,128)(2,1)S(1)}, s32[8,168]{1,0:T(8,128)S(1)}, ...), branch_computations={%region_21.32_spmd, %region_32.33_spmd} | conditional | flops 19953197056 | bytes 725728768 | solution.py:343
  433.1 7.8 %multiply_subtract_fusion = (f32[255,2048]{1,0:T(8,128)}, f32[255,2048]{1,0:T(8,128)}, f32[255,2048]{1,0:T(8,128)}) fusion(f32[255,2048]{1,0:T(8,128)} %param.14, f32[255]{0:T(256)S(1)} %copy-done.85, f32[255]{0:T(256)S(1)} %copy-done.84, f32[255,2048]{1,0:T(8,128)S(1)} %get-tuple-element.87, f32[255,2048]{1,0:T(8,128)} %param.16, f32[255,2048]{1,0:T(8,128)} %param.15), kind=kLoop, calls=%fused_computation.163 | loop fusion | flops 7833600 | bytes 14624760 | tf_op jit(solution)/shard_map/sub | solution.py:316
  (374 shorter events, 142.4 us)
Async XLA Ops:
  18.5 24.8 %all-to-all-start.8 = ((bf16[8,24,2048]{2,1,0:T(8,128)(2,1)}), bf16[8,24,2048]{2,1,0:T(8,128)(2,1)S(1)}, u32[]{:S(2)}, u32[]{:S(2)}) async-start(bf16[8,24,2048]{2,1,0:T(8,128)(2,1)} %bitcast.70), calls=%async_computation.8 | async-start | bytes 1572864 | tf_op jit(solution)/shard_map/all_to_all | solution.py:70
  23.7 50.4 %all-gather.3.cloned.1.call-start = ((), (), s32[]{:S(2)}) async-start(), calls=%async_computation.18 | async-start | bytes 1474560 | tf_op jit(solution)/shard_map/all_gather | solution.py:242
  24.7 16.2 %collective-permute-start.44 = (bf16[2,128,512]{2,1,0:T(8,128)(2,1)}, bf16[2,128,512]{2,1,0:T(8,128)(2,1)S(1)}, u32[]{:S(2)}, u32[]{:S(2)}) collective-permute-start(bf16[2,128,512]{2,1,0:T(8,128)(2,1)} %get-tuple-element.201), channel_id=1, source_target_pairs={{0,4},{1,5},{2,6},{3,7},{4,0},{5,1},{6,2},{7,3},{8,12},{9,13},{10,... | collective-permute-start | bytes 786440 | tf_op jit(solution)/shard_map/ppermute | solution.py:66
  26.7 17.7 %collective-permute-start.42 = (bf16[2,128,512]{2,1,0:T(8,128)(2,1)}, bf16[2,128,512]{2,1,0:T(8,128)(2,1)S(1)}, u32[]{:S(2)}, u32[]{:S(2)}) collective-permute-start(bf16[2,128,512]{2,1,0:T(8,128)(2,1)} %get-tuple-element.202), channel_id=1, source_target_pairs={{0,2},{1,3},{2,0},{3,1},{4,6},{5,7},{6,4},{7,5},{8,10},{9,11},{10,... | collective-permute-start | bytes 786440 | tf_op jit(solution)/shard_map/ppermute | solution.py:66
  41.8 13.9 %collective-permute-start.45 = (bf16[2,2,128,512]{3,2,0,1:T(8,128)(2,1)}, bf16[2,2,128,512]{3,2,0,1:T(8,128)(2,1)}, u32[]{:S(2)}, u32[]{:S(2)}) collective-permute-start(bf16[2,2,128,512]{3,2,0,1:T(8,128)(2,1)} %pad_maximum_fusion.15), channel_id=1, source_target_pairs={{0,2},{1,3},{2,0},{3,1},{4,6},{5,7},{6,4},{7,5},{8,10},{9,11},{10,... | collective-permute-start | bytes 1572872 | tf_op jit(solution)/shard_map/ppermute | solution.py:66
  44.5 13.7 %collective-permute-start.43 = (bf16[2,2,128,512]{3,2,0,1:T(8,128)(2,1)S(1)}, bf16[2,2,128,512]{3,2,0,1:T(8,128)(2,1)S(1)}, u32[]{:S(2)}, u32[]{:S(2)}) collective-permute-start(bf16[2,2,128,512]{3,2,0,1:T(8,128)(2,1)S(1)} %pad_maximum_fusion.14), channel_id=1, source_target_pairs={{0,4},{1,5},{2,6},{3,7},{4,0},{5,1},{6,2},{7,3},{8,12},{9,13},{10,... | collective-permute-start | bytes 1572872 | tf_op jit(solution)/shard_map/ppermute | solution.py:66
  61.3 39.0 %collective-permute-start.46 = (bf16[2,512,1024]{2,1,0:T(8,128)(2,1)}, bf16[2,512,1024]{2,1,0:T(8,128)(2,1)}, u32[]{:S(2)}, u32[]{:S(2)}) collective-permute-start(bf16[2,512,1024]{2,1,0:T(8,128)(2,1)} %bitcast.65.x0.c0), channel_id=1, source_target_pairs={{0,1},{1,0},{2,3},{3,2},{4,5},{5,4},{6,7},{7,6},{8,9},{9,8},{10,11... | collective-permute-start | bytes 6291464 | tf_op jit(solution)/shard_map/ppermute | solution.py:66
  77.4 13.9 %all-to-all-start.9 = ((bf16[8,128,256]{2,1,0:T(8,128)(2,1)}), bf16[8,128,256]{2,1,0:T(8,128)(2,1)}, u32[]{:S(2)}, u32[]{:S(2)}) async-start(bf16[8,128,256]{2,1,0:T(8,128)(2,1)} %get-tuple-element.92), calls=%async_computation.9 | async-start | bytes 1048576 | tf_op jit(solution)/shard_map/all_to_all | solution.py:70
  91.3 25.3 %all-to-all-start.10 = ((bf16[8,48,2048]{2,1,0:T(8,128)(2,1)}), bf16[8,48,2048]{2,1,0:T(8,128)(2,1)}, u32[]{:S(2)}, u32[]{:S(2)}) async-start(bf16[8,48,2048]{2,1,0:T(8,128)(2,1)} %bitcast.348), calls=%async_computation.10 | async-start | bytes 3145728 | tf_op jit(solution)/shard_map/all_to_all | solution.py:70
  95.6 82.7 %all-gather.5.cloned.1.call-start = ((), (), s32[]{:S(2)}) async-start(), calls=%async_computation.19 | async-start | bytes 3768320 | tf_op jit(solution)/shard_map/all_gather | solution.py:242
  111.8 9.1 %collective-permute-start.47 = (bf16[1,512,1024]{2,1,0:T(8,128)(2,1)}, bf16[1,512,1024]{2,1,0:T(8,128)(2,1)}, u32[]{:S(2)}, u32[]{:S(2)}) collective-permute-start(bf16[1,512,1024]{2,1,0:T(8,128)(2,1)} %get-tuple-element.95), channel_id=1, source_target_pairs={{0,1},{1,0},{2,3},{3,2},{4,5},{5,4},{6,7},{7,6},{8,9},{9,8},{10,11... | collective-permute-start | bytes 3145736 | tf_op jit(solution)/shard_map/ppermute | solution.py:66
  123.0 6.4 %collective-permute-start.48 = (bf16[1,2,128,512]{3,2,1,0:T(8,128)(2,1)S(1)}, bf16[1,2,128,512]{3,2,1,0:T(8,128)(2,1)S(1)}, u32[]{:S(2)}, u32[]{:S(2)}) collective-permute-start(bf16[1,2,128,512]{3,2,1,0:T(8,128)(2,1)S(1)} %slice.577), channel_id=1, source_target_pairs={{0,4},{1,5},{2,6},{3,7},{4,0},{5,1},{6,2},{7,3},{8,12},{9,13},{10,... | collective-permute-start | bytes 786440 | tf_op jit(solution)/shard_map/ppermute | solution.py:66
  123.6 8.4 %collective-permute-start.50 = (bf16[1,2,128,512]{3,2,1,0:T(8,128)(2,1)S(1)}, bf16[1,2,128,512]{3,2,1,0:T(8,128)(2,1)S(1)}, u32[]{:S(2)}, u32[]{:S(2)}) collective-permute-start(bf16[1,2,128,512]{3,2,1,0:T(8,128)(2,1)S(1)} %pad_maximum_fusion.19), channel_id=1, source_target_pairs={{0,2},{1,3},{2,0},{3,1},{4,6},{5,7},{6,4},{7,5},{8,10},{9,11},{10,... | collective-permute-start | bytes 786440 | tf_op jit(solution)/shard_map/ppermute | solution.py:66
  137.5 7.8 %collective-permute-start.52 = (bf16[1,128,512]{2,1,0:T(8,128)(2,1)S(1)}, bf16[1,128,512]{2,1,0:T(8,128)(2,1)S(1)}, u32[]{:S(2)}, u32[]{:S(2)}) collective-permute-start(bf16[1,128,512]{2,1,0:T(8,128)(2,1)S(1)} %get-tuple-element.214), channel_id=1, source_target_pairs={{0,2},{1,3},{2,0},{3,1},{4,6},{5,7},{6,4},{7,5},{8,10},{9,11},{10,... | collective-permute-start | bytes 393224 | tf_op jit(solution)/shard_map/ppermute | solution.py:66
  143.4 47.6 %collective-permute-start.55 = (bf16[1,2,128,512]{3,2,1,0:T(8,128)(2,1)}, bf16[1,2,128,512]{3,2,1,0:T(8,128)(2,1)}, u32[]{:S(2)}, u32[]{:S(2)}) collective-permute-start(bf16[1,2,128,512]{3,2,1,0:T(8,128)(2,1)} %pad_maximum_fusion.21), channel_id=1, source_target_pairs={{0,2},{1,3},{2,0},{3,1},{4,6},{5,7},{6,4},{7,5},{8,10},{9,11},{10,... | collective-permute-start | bytes 786440 | tf_op jit(solution)/shard_map/ppermute | solution.py:66
  146.7 45.3 %collective-permute-start.53 = (bf16[1,2,128,512]{3,2,1,0:T(8,128)(2,1)}, bf16[1,2,128,512]{3,2,1,0:T(8,128)(2,1)}, u32[]{:S(2)}, u32[]{:S(2)}) collective-permute-start(bf16[1,2,128,512]{3,2,1,0:T(8,128)(2,1)} %pad_maximum_fusion.20), channel_id=1, source_target_pairs={{0,4},{1,5},{2,6},{3,7},{4,0},{5,1},{6,2},{7,3},{8,12},{9,13},{10,... | collective-permute-start | bytes 786440 | tf_op jit(solution)/shard_map/ppermute | solution.py:66
  186.3 25.7 %all-to-all-start.11 = ((bf16[8,128,768]{2,1,0:T(8,128)(2,1)}), bf16[8,128,768]{2,1,0:T(8,128)(2,1)}, u32[]{:S(2)}, u32[]{:S(2)}) async-start(bf16[8,128,768]{2,1,0:T(8,128)(2,1)} %get-tuple-element.96), calls=%async_computation.11 | async-start | bytes 3145728 | tf_op jit(solution)/shard_map/all_to_all | solution.py:70
  228.7 8.4 %collective-permute-start.58 = (bf16[1,2,128,512]{3,2,1,0:T(8,128)(2,1)S(1)}, bf16[1,2,128,512]{3,2,1,0:T(8,128)(2,1)S(1)}, u32[]{:S(2)}, u32[]{:S(2)}) collective-permute-start(bf16[1,2,128,512]{3,2,1,0:T(8,128)(2,1)S(1)} %slice.593), channel_id=1, source_target_pairs={{0,4},{1,5},{2,6},{3,7},{4,0},{5,1},{6,2},{7,3},{8,12},{9,13},{10,... | collective-permute-start | bytes 786440 | tf_op jit(solution)/shard_map/ppermute | solution.py:66
  229.4 8.5 %collective-permute-start.60 = (bf16[1,2,128,512]{3,2,1,0:T(8,128)(2,1)S(1)}, bf16[1,2,128,512]{3,2,1,0:T(8,128)(2,1)S(1)}, u32[]{:S(2)}, u32[]{:S(2)}) collective-permute-start(bf16[1,2,128,512]{3,2,1,0:T(8,128)(2,1)S(1)} %pad_maximum_fusion.22), channel_id=1, source_target_pairs={{0,2},{1,3},{2,0},{3,1},{4,6},{5,7},{6,4},{7,5},{8,10},{9,11},{10,... | collective-permute-start | bytes 786440 | tf_op jit(solution)/shard_map/ppermute | solution.py:66
  248.7 6.7 %collective-permute-start.65 = (bf16[1,2,128,512]{3,2,1,0:T(8,128)(2,1)S(1)}, bf16[1,2,128,512]{3,2,1,0:T(8,128)(2,1)S(1)}, u32[]{:S(2)}, u32[]{:S(2)}) collective-permute-start(bf16[1,2,128,512]{3,2,1,0:T(8,128)(2,1)S(1)} %pad_maximum_fusion.24), channel_id=1, source_target_pairs={{0,2},{1,3},{2,0},{3,1},{4,6},{5,7},{6,4},{7,5},{8,10},{9,11},{10,... | collective-permute-start | bytes 786440 | tf_op jit(solution)/shard_map/ppermute | solution.py:66
  251.3 6.4 %collective-permute-start.63 = (bf16[1,2,128,512]{3,2,1,0:T(8,128)(2,1)S(1)}, bf16[1,2,128,512]{3,2,1,0:T(8,128)(2,1)S(1)}, u32[]{:S(2)}, u32[]{:S(2)}) collective-permute-start(bf16[1,2,128,512]{3,2,1,0:T(8,128)(2,1)S(1)} %pad_maximum_fusion.23), channel_id=1, source_target_pairs={{0,4},{1,5},{2,6},{3,7},{4,0},{5,1},{6,2},{7,3},{8,12},{9,13},{10,... | collective-permute-start | bytes 786440 | tf_op jit(solution)/shard_map/ppermute | solution.py:66
  285.5 13.9 %all-to-all-start.14 = ((bf16[8,128,256]{2,1,0:T(8,128)(2,1)}), bf16[8,128,256]{2,1,0:T(8,128)(2,1)}, u32[]{:S(2)}, u32[]{:S(2)}) async-start(bf16[8,128,256]{2,1,0:T(8,128)(2,1)} %bitcast.373), calls=%async_computation.15 | async-start | bytes 1048576 | tf_op jit(solution)/shard_map/all_to_all | solution.py:70
  289.6 78.0 %reduce-scatter.5.cloned.1.call-start = ((), (), s32[]{:S(2)}) async-start(), calls=%async_computation.21 | async-start | bytes 1474560 | tf_op jit(solution)/shard_map/reduce_scatter | solution.py:260
  307.6 25.4 %all-to-all-start.12 = ((bf16[8,128,768]{2,1,0:T(8,128)(2,1)}), bf16[8,128,768]{2,1,0:T(8,128)(2,1)}, u32[]{:S(2)}, u32[]{:S(2)}) async-start(bf16[8,128,768]{2,1,0:T(8,128)(2,1)} %bitcast.354), calls=%async_computation.12 | async-start | bytes 3145728 | tf_op jit(solution)/shard_map/all_to_all | solution.py:70
  312.1 85.3 %reduce-scatter.3.cloned.1.call-start = ((), (), s32[]{:S(2)}) async-start(), calls=%async_computation.20 | async-start | bytes 3768320 | tf_op jit(solution)/shard_map/reduce_scatter | solution.py:260
  342.0 6.7 %collective-permute-start.67 = (bf16[2,512,1024]{2,1,0:T(8,128)(2,1)}, bf16[2,512,1024]{2,1,0:T(8,128)(2,1)}, u32[]{:S(2)}, u32[]{:S(2)}) collective-permute-start(bf16[2,512,1024]{2,1,0:T(8,128)(2,1)} %get-tuple-element.113), channel_id=1, source_target_pairs={{0,1},{1,0},{2,3},{3,2},{4,5},{5,4},{6,7},{7,6},{8,9},{9,8},{10,11... | collective-permute-start | bytes 6291464 | tf_op jit(solution)/shard_map/ppermute | solution.py:66
  351.3 13.8 %collective-permute-start.68 = (bf16[2,2,128,512]{3,2,0,1:T(8,128)(2,1)S(1)}, bf16[2,2,128,512]{3,2,0,1:T(8,128)(2,1)S(1)}, u32[]{:S(2)}, u32[]{:S(2)}) collective-permute-start(bf16[2,2,128,512]{3,2,0,1:T(8,128)(2,1)S(1)} %copy.62), channel_id=1, source_target_pairs={{0,4},{1,5},{2,6},{3,7},{4,0},{5,1},{6,2},{7,3},{8,12},{9,13},{10,... | collective-permute-start | bytes 1572872 | tf_op jit(solution)/shard_map/ppermute | solution.py:66
  352.8 21.0 %collective-permute-start.70 = (bf16[2,2,128,512]{3,2,0,1:T(8,128)(2,1)}, bf16[2,2,128,512]{3,2,0,1:T(8,128)(2,1)}, u32[]{:S(2)}, u32[]{:S(2)}) collective-permute-start(bf16[2,2,128,512]{3,2,0,1:T(8,128)(2,1)} %pad_maximum_fusion.18), channel_id=1, source_target_pairs={{0,2},{1,3},{2,0},{3,1},{4,6},{5,7},{6,4},{7,5},{8,10},{9,11},{10,... | collective-permute-start | bytes 1572872 | tf_op jit(solution)/shard_map/ppermute | solution.py:66
  367.0 37.8 %collective-permute-start.69 = (bf16[2,128,512]{2,1,0:T(8,128)(2,1)}, bf16[2,128,512]{2,1,0:T(8,128)(2,1)S(1)}, u32[]{:S(2)}, u32[]{:S(2)}) collective-permute-start(bf16[2,128,512]{2,1,0:T(8,128)(2,1)} %fusion.102), channel_id=1, source_target_pairs={{0,2},{1,3},{2,0},{3,1},{4,6},{5,7},{6,4},{7,5},{8,10},{9,11},{10,... | collective-permute-start | bytes 786440 | tf_op jit(solution)/shard_map/ppermute | solution.py:66
  369.9 30.3 %all-to-all-start.15 = ((bf16[8,24,2048]{2,1,0:T(8,128)(2,1)}), bf16[8,24,2048]{2,1,0:T(8,128)(2,1)S(1)}, u32[]{:S(2)}, u32[]{:S(2)}) async-start(bf16[8,24,2048]{2,1,0:T(8,128)(2,1)} %bitcast.111), calls=%async_computation.17 | async-start | bytes 1572864 | tf_op jit(solution)/shard_map/all_to_all | solution.py:70
  376.7 29.3 %collective-permute-start.71 = (bf16[2,128,512]{2,1,0:T(8,128)(2,1)}, bf16[2,128,512]{2,1,0:T(8,128)(2,1)}, u32[]{:S(2)}, u32[]{:S(2)}) collective-permute-start(bf16[2,128,512]{2,1,0:T(8,128)(2,1)} %fusion.103), channel_id=1, source_target_pairs={{0,4},{1,5},{2,6},{3,7},{4,0},{5,1},{6,2},{7,3},{8,12},{9,13},{10,... | collective-permute-start | bytes 786440 | tf_op jit(solution)/shard_map/ppermute | solution.py:66
  401.1 24.7 %all-to-all-start.13 = ((bf16[8,48,2048]{2,1,0:T(8,128)(2,1)}), bf16[8,48,2048]{2,1,0:T(8,128)(2,1)S(1)}, u32[]{:S(2)}, u32[]{:S(2)}) async-start(bf16[8,48,2048]{2,1,0:T(8,128)(2,1)} %bitcast.350), calls=%async_computation.14 | async-start | bytes 3145728 | tf_op jit(solution)/shard_map/all_to_all | solution.py:70
  (83 other events, 883.8 us)
Sparse Core Ops, SparseCore 0:
  44.4 29.6 all-gather.2
  119.6 58.7 all-gather.4
  302.7 26.1 reduce-scatter.4
  342.1 55.2 reduce-scatter.2

commit v2 on v1

--- a/solution.py
+++ b/solution.py
@@ -260,7 +260,7 @@
         rows = lax.psum_scatter(rows, "seq", scatter_dimension=0, tiled=True)
         packed = left_product(self.compact, rows).astype(BF)
         packed = exchange(packed)
-        return product(self.send, packed)
+        return packed
 
     def give_any(self, rows):
         width = rows.shape[1]
@@ -332,22 +332,8 @@
     routes = [Route(owners, slots, group, seq, tok, capacity) for group in range(2)]
     rounded = master.astype(BF)
     layer = layer_of_eight if tok == 8 else layer_of_any
-    found = layer(
+    result, grad_input, packed = layer(
         tokens, cotangent, rounded, [(r.fetch, r.place_back, r.give) for r in routes]
-    )
-
-    def any_owners(tokens, cotangent, rounded, *found):
-        plain = [(r.fetch_any, jnp.eye(r.size, dtype=BF), r.give_any) for r in routes]
-        return layer(tokens, cotangent, rounded, plain)
-
-    result, grad_input, reduced = lax.cond(
-        routes[0].fits & routes[1].fits,
-        lambda tokens, cotangent, rounded, *found: found,
-        any_owners,
-        tokens,
-        cotangent,
-        rounded,
-        *found,
     )
     mine = (owners == me)[None, :]
     numbers = jnp.arange(owners.shape[0], dtype=jnp.int32)[None, :]
@@ -355,12 +341,23 @@
         (mine & (numbers < jnp.array(LIMITS, jnp.int32)[:, None])).astype(jnp.int32), axis=1
     )
     kinds = jnp.sum(
-        (jnp.arange(capacity, dtype=jnp.int32)[:, None] >= counts[None, :]).astype(jnp.int32), axis=1
-    )
-    rate_values, decay_values = rates_for(kinds, tokens.shape[1] * tok)
-    first, second, updated = adam_update(
-        reduced, first_moment, second_moment, master, rate_values, decay_values
-    )
+        (jnp.arange(capacity, dtype=jnp.int32)[:, None] >= counts[None, :]).astype(jnp.int32),
+        axis=1,
+    )
+    rates = rates_for(kinds, tokens.shape[1] * tok)
+    held = (first_moment, second_moment, master)
+    found = (result, grad_input) + owned_update(routes, packed, held, rates)
+
+    def any_owners(carried):
+        plain = [(r.fetch_any, jnp.eye(r.size, dtype=BF), r.give_any) for r in routes]
+        result, grad_input, parts = layer(tokens, cotangent, rounded, plain)
+        reduced = parts[0] + parts[1]
+        updated = adam_update(reduced, *held, *rates)
+        return (jnp.int32(1), result, grad_input, reduced) + updated
+
+    missing = jnp.where(routes[0].fits & routes[1].fits, 1, 0).astype(jnp.int32)
+    found = lax.while_loop(lambda carried: carried[0] == 0, any_owners, (missing,) + found)
+    _, result, grad_input, reduced, first, second, updated = found
     return (result[None], grad_input[None], reduced, first, second, updated)
 
 
@@ -499,6 +496,44 @@
         rows_ref[:, lanes] = dot(place_ref[...], grads).astype(BF)
 
 
+def select_update(
+    send0, send1, near, far, first, second, weights, rates, decays, out0, out1, out2, out3
+):
+    grads = dot(send0[...], near[...]) + dot(send1[...], far[...])
+    out0[...] = grads
+    updated = adam_update(
+        grads, first[...], second[...], weights[...], rates[...][:, 0], decays[...][:, 0]
+    )
+    out1[...], out2[...], out3[...] = updated
+
+
+def owned_update(routes, packed, held, rates):
+    capacity, width = held[0].shape
+    columns = 256
+
+    def whole(array):
+        return pl.BlockSpec(array.shape, lambda i: (0, 0))
+
+    def part(array):
+        return pl.BlockSpec((array.shape[0], columns), lambda i: (0, i))
+
+    rates = [values[:, None] for values in rates]
+    return tuple(
+        pl.pallas_call(
+            select_update,
+            out_shape=[jax.ShapeDtypeStruct((capacity, width), F32)] * 4,
+            grid=(width // columns,),
+            in_specs=[whole(routes[0].send), whole(routes[1].send)]
+            + [part(array) for array in (*packed, *held)]
+            + [whole(rates[0]), whole(rates[1])],
+            out_specs=[part(held[0])] * 4,
+            cost_estimate=pl.CostEstimate(
+                flops=2 * capacity * width * 576, bytes_accessed=16 << 20, transcendentals=0
+            ),
+        )(routes[0].send, routes[1].send, *packed, *held, *rates)
+    )
+
+
 ROWS = 256
 
 
@@ -760,7 +795,7 @@
 
     back_gate, back_up = flat(back[..., :ff_slice]), flat(back[..., ff_slice:])
     blocks = joined([back_gate, back_up, grad_w_down.reshape(-1, BLK)])
-    reduced = routes[1][2](product(routes[1][1], blocks).astype(BF))
+    far = routes[1][2](product(routes[1][1], blocks).astype(BF))
 
     grad_w_out = left_product(mixed, grad_mixer).astype(BF)
     grad_mixed = right_product(grad_mixer, w_out).astype(BF)
@@ -809,11 +844,11 @@
             grad_w_out.reshape(-1, BLK),
         ]
     )
-    reduced = reduced + routes[0][2](product(routes[0][1], blocks).astype(BF))
+    near = routes[0][2](product(routes[0][1], blocks).astype(BF))
 
     normed_one, scale_one = normalize(input_rows)
     grad_input = grad_middle + norm_back(grad_hidden_one * gain_one, normed_one, scale_one)
-    return result, grad_input.astype(BF), reduced
+    return result, grad_input.astype(BF), (near, far)
 
 
 def layer_of_eight(tokens, cotangent, rounded, routes):
@@ -899,7 +934,7 @@
         flops=2 * routes[1][1].size * BLK,
         nbytes=6 << 20,
     )(routes[1][1], back, grad_w_down)
-    reduced = routes[1][2](rows)
+    far = routes[1][2](rows)
 
     grad_qkv, keep, send, gain_terms, grad_w_out = call(
         mix_back,
@@ -938,13 +973,13 @@
         flops=2 * routes[0][1].size * BLK,
         nbytes=2 << 20,
     )(routes[0][1], jnp.pad(grad_gains[None], ((0, 7), (0, 0))), back, grad_w_out)
-    reduced = reduced + routes[0][2](rows)
+    near = routes[0][2](rows)
 
     normed_one, scale_one = normalize(input_rows)
     grad_input = grad_middle + norm_back(
         grad_hidden_one * gains[0, :D], normed_one, scale_one
     )
-    return result, grad_input.astype(BF), reduced
+    return result, grad_input.astype(BF), (near, far)
 
 
 def solution(mesh):

time: 455 us -> 457 us (level)
  Pallas kernels: 66.3 us -> 76.4 us
  waiting for transfers between devices: 200 us -> 194 us
  other arithmetic: 44.4 us -> 38.8 us
    all_to_all x8, waiting for transfers between devices: 65.9 us -> 54.4 us  [exchange(): return lax.all_to_all(values, 'tok', 0, 0, tiled=True)]
    pallas_call x0 -> x1, Pallas kernels: none -> 10.3 us  [owned_update(): pl.pallas_call(select_update, out_shape=[jax.ShapeDtypeStruct((capacity,...]
    ppermute x30, waiting for transfers between devices: 73.2 us -> 81 us  [swap(): return lax.ppermute(values, 'tok', [(i, i ^ mask) for i in range(8)])]
    sub x1 -> x0, other arithmetic: 7.78 us -> none  [adam_update(): weights - rate_values[:, None] * (first_hat / (jnp.sqrt(second_hat) + ADA...]
  transfers between devices with their start and end apart: 42 -> 42, of which waited for: 27 -> 27; matrix products, arithmetic and copies ran while one was open for 14% -> 18% of each run, Pallas kernels for 7% -> 7%
where the time goes in v2:
time: 457 us; the launch traced here: 450 us
  waiting for transfers between devices  194 us (42%)
  Pallas kernels  76.4 us (17%)
  starting transfers between devices  63.8 us (14%)
  other arithmetic  38.8 us (8%)
  local copies, waits for them, and re-layouts  28.8 us (6%)
  matrix products  27.7 us (6%)
  between operations  18.3 us (4%)
    ppermute x30, waiting for transfers between devices, swap(): return lax.ppermute(values, 'tok', [(i, i ^ mask) for i in range(8)])  81 us
    all_to_all x8, waiting for transfers between devices, exchange(): return lax.all_to_all(values, 'tok', 0, 0, tiled=True)  54.4 us
    all_gather x2, waiting for transfers between devices, fetch(): rows = lax.all_gather(rows, 'seq', axis=0, tiled=True)  44 us
    all_to_all x8, starting transfers between devices, exchange(): return lax.all_to_all(values, 'tok', 0, 0, tiled=True)  34.6 us
    ppermute x30, starting transfers between devices, swap(): return lax.ppermute(values, 'tok', [(i, i ^ mask) for i in range(8)])  28.6 us
    dot_general x9, matrix products, left_product(): lax.dot_general(left, right, (((0,), (0,)), ((), ())), preferred_element_...  20.9 us
    pallas_call x1, Pallas kernels, layer_of_eight(): call(mix_back, [((seq_len, 256), BF), ((2, half, D), BF), ((2, half, D),...  19.7 us
    reduce_scatter x2, waiting for transfers between devices, give(): rows = lax.psum_scatter(rows, 'seq', scatter_dimension=0, tiled=True)  14.9 us
  transfers between devices with their start and end apart: 42, of which 27 were waited for; matrix products, arithmetic and copies ran while one was open for 18% of the time, Pallas kernels for 7%

profile of v2, /device:TPU:0, one launch (start us, length us, event | category | flops | bytes accessed | tf_op | source)
XLA Modules:
  0.0 449.5 jit_solution(12399836483960907910)
XLA Ops:
  25.1 4.2 all-to-all-start.8
  47.1 5.6 %collective-permute-done.45 = bf16[2,2,128,512]{3,2,0,1:T(8,128)(2,1)} collective-permute-done((bf16[2,2,128,512]{3,2,0,1:T(8,128)(2,1)}, bf16[2,2,128,512]{3,2,0,1:T(8,128)(2,1)}, u32[]{:S(2)}, u32[]{:S(2)}) %collective-permute-start.45) | collective-permute-done | bytes 524320 | tf_op jit(solution)/shard_map/ppermute | solution.py:66
  53.7 3.4 collective-permute-done.43
  62.9 10.9 %all-gather.3.cloned.1.call-done.rows_ref = bf16[288,2048]{1,0:T(8,128)(2,1)} async-done(((bf16[72,2048]{1,0:T(8,128)(2,1)}), bf16[288,2048]{1,0:T(8,128)(2,1)}) %all-gather.3.cloned.1.call-update) | async-done | bytes 1179664 | tf_op jit(solution)/shard_map/all_gather | solution.py:242
  73.8 3.3 shard_map.136
  77.1 4.2 all-to-all-start.9
  83.1 7.9 %all-to-all-done.9 = bf16[8,128,256]{2,1,0:T(8,128)(2,1)} async-done(((bf16[8,128,256]{2,1,0:T(8,128)(2,1)}), bf16[8,128,256]{2,1,0:T(8,128)(2,1)}, u32[]{:S(2)}, u32[]{:S(2)}) %all-to-all-start.9) | async-done | bytes 524320 | tf_op jit(solution)/shard_map/all_to_all | solution.py:70
  91.0 4.4 all-to-all-start.10
  98.4 11.3 %shard_map.137 = (bf16[1024,1024]{1,0:T(8,128)(2,1)}, bf16[1024,256]{1,0:T(8,128)(2,1)}, bf16[1024,128]{1,0:T(8,128)(2,1)}, f32[1024,128]{1,0:T(8,128)}, f32[102...) custom-call(s32[1]{0:T(128)} %bitcast.5.me_ref, bf16[2,512,1024]{2,1,0:T(8,128)(2,1)} %bitcast.10.x0.c0, ...), custom_call_target="tpu_custom_call" | custom-call | flops 2952790016 | bytes 10485760 | tf_op jit(solution)/shard_map/pallas_call | solution.py:881
  110.0 6.4 %all-to-all-done.10 = bf16[8,48,2048]{2,1,0:T(8,128)(2,1)} async-done(((bf16[8,48,2048]{2,1,0:T(8,128)(2,1)}), bf16[8,48,2048]{2,1,0:T(8,128)(2,1)}, u32[]{:S(2)}, u32[]{:S(2)}) %all-to-all-start.10) | async-done | bytes 1572896 | tf_op jit(solution)/shard_map/all_to_all | solution.py:70
  122.8 5.0 %collective-permute-done.48 = bf16[1,2,128,512]{3,2,1,0:T(8,128)(2,1)S(1)} collective-permute-done((bf16[1,2,128,512]{3,2,1,0:T(8,128)(2,1)S(1)}, bf16[1,2,128,512]{3,2,1,0:T(8,128)(2,1)S(1)}, u32[]{:S(2)}, u32[]{:S(2)}) %collective-permute-start.48) | collective-permute-done | bytes 262176 | tf_op jit(solution)/shard_map/ppermute | solution.py:66
  145.0 33.1 %all-gather.5.cloned.1.call-done.rows_ref = bf16[736,2048]{1,0:T(8,128)(2,1)} async-done(((bf16[184,2048]{1,0:T(8,128)(2,1)}), bf16[736,2048]{1,0:T(8,128)(2,1)}) %all-gather.5.cloned.1.call-update) | async-done | bytes 3014672 | tf_op jit(solution)/shard_map/all_gather | solution.py:242
  178.2 8.0 %shard_map.138 = (bf16[8,128,768]{2,1,0:T(8,128)(2,1)}, bf16[384,1024]{1,0:T(8,128)(2,1)}) custom-call(bf16[544,736]{1,0:T(8,128)(2,1)} %fusion.67.place_ref, bf16[736,2048]{1,0:T(8,128)(2,1)} %all-gather.5.cloned.1.call-done.rows_ref), custom_call_target="tpu_custom_call" | custom-call | flops 1639972864 | bytes 6291456 | tf_op jit(solution)/shard_map/pallas_call | solution.py:871
  186.1 4.8 %all-to-all-start.11 = ((bf16[8,128,768]{2,1,0:T(8,128)(2,1)}), bf16[8,128,768]{2,1,0:T(8,128)(2,1)}, u32[]{:S(2)}, u32[]{:S(2)}) async-start(bf16[8,128,768]{2,1,0:T(8,128)(2,1)} %get-tuple-element.151), calls=%async_computation.11 | async-start | bytes 3145728 | tf_op jit(solution)/shard_map/all_to_all | solution.py:70
  197.1 14.9 %all-to-all-done.11 = bf16[8,128,768]{2,1,0:T(8,128)(2,1)} async-done(((bf16[8,128,768]{2,1,0:T(8,128)(2,1)}), bf16[8,128,768]{2,1,0:T(8,128)(2,1)}, u32[]{:S(2)}, u32[]{:S(2)}) %all-to-all-start.11) | async-done | bytes 1572896 | tf_op jit(solution)/shard_map/all_to_all | solution.py:70
  212.0 12.0 %shard_map.139 = (bf16[1024,384]{1,0:T(8,128)(2,1)}, bf16[1024,768]{1,0:T(8,128)(2,1)}, bf16[1,512,1024]{2,1,0:T(8,128)(2,1)}, bf16[1,512,1024]{2,1,0:T(8,128)(2...) custom-call(bf16[1,512,1024]{2,1,0:T(8,128)(2,1)} %bitcast.409, ...), custom_call_target="tpu_custom_call" | custom-call | flops 4831838208 | bytes 14680064 | tf_op jit(solution)/shard_map/pallas_call | solution.py:905
  230.0 7.0 %collective-permute-done.58 = bf16[1,2,128,512]{3,2,1,0:T(8,128)(2,1)S(1)} collective-permute-done((bf16[1,2,128,512]{3,2,1,0:T(8,128)(2,1)S(1)}, bf16[1,2,128,512]{3,2,1,0:T(8,128)(2,1)S(1)}, u32[]{:S(2)}, u32[]{:S(2)}) %collective-permute-start.58) | collective-permute-done | bytes 262176 | tf_op jit(solution)/shard_map/ppermute | solution.py:66
  251.9 3.4 collective-permute-done.65
  262.4 19.7 %shard_map.140 = (bf16[1024,256]{1,0:T(8,128)(2,1)}, bf16[2,512,1024]{2,1,0:T(8,128)(2,1)}, bf16[2,512,1024]{2,1,0:T(8,128)(2,1)}, f32[8,1024]{1,0:T(8,128)}, bf16[128,1024]{1,0:T(8,128)(2,1)}) custom-call(s32[1]{0:T(128)} %bitcast.5.me_ref, bf16[1,512,1024]{2,1,0:T(8,128)(2,1)} %bitcast.412, bf16[1,512,1024]{2,1,0:T(8,128)(2,1)} %copy-done.80, ...), custom_call_target="tpu_custom_call" | custom-call | flops 6442450944 | bytes 20971520 | tf_op jit(solution)/shard_map/pallas_call | solution.py:939
  282.1 3.2 convolution_convert_fusion.7
  285.3 4.2 all-to-all-start.12
  291.8 7.4 %all-to-all-done.12.back_ref = bf16[8,128,256]{2,1,0:T(8,128)(2,1)} async-done(((bf16[8,128,256]{2,1,0:T(8,128)(2,1)}), bf16[8,128,256]{2,1,0:T(8,128)(2,1)}, u32[]{:S(2)}, u32[]{:S(2)}) %all-to-all-start.12) | async-done | bytes 524320 | tf_op jit(solution)/shard_map/all_to_all | solution.py:70
  302.4 5.1 %fusion.64 = bf16[1024,768]{1,0:T(8,128)(2,1)} fusion(bf16[1024,768]{1,0:T(8,128)(2,1)} %get-tuple-element.167, bf16[512,1024]{1,0:T(8,128)(2,1)} %bitcast.64, bf16[512,1024]{1,0:T(8,128)(2,1)} %bitcast.410), kind=kOutput, calls=%fused_computation.175 | convolution fusion | flops 1615593472 | bytes 5242880 | tf_op jit(solution)/shard_map/dot_general | solution.py:47
  307.5 4.3 all-to-all-start.14
  316.7 16.0 %all-to-all-done.14.back_ref = bf16[8,128,768]{2,1,0:T(8,128)(2,1)} async-done(((bf16[8,128,768]{2,1,0:T(8,128)(2,1)}), bf16[8,128,768]{2,1,0:T(8,128)(2,1)}, u32[]{:S(2)}, u32[]{:S(2)}) %all-to-all-start.14) | async-done | bytes 1572896 | tf_op jit(solution)/shard_map/all_to_all | solution.py:70
  332.8 8.7 %shard_map.142 = bf16[736,2048]{1,0:T(8,128)(2,1)} custom-call(bf16[736,544]{1,0:T(8,128)(2,1)} %fusion.63.place_ref, bf16[8,128,768]{2,1,0:T(8,128)(2,1)} %all-to-all-done.14.back_ref, bf16[384,1024]{1,0:T(8,128)(2,1)} %fusion.68.down_ref), custom_call_target="tpu_custom_call" | custom-call | flops 1639972864 | bytes 6291456 | tf_op jit(solution)/shard_map/pallas_call | solution.py:929
  357.5 10.7 %collective-permute-done.68 = bf16[2,2,128,512]{3,2,0,1:T(8,128)(2,1)S(1)} collective-permute-done((bf16[2,2,128,512]{3,2,0,1:T(8,128)(2,1)S(1)}, bf16[2,2,128,512]{3,2,0,1:T(8,128)(2,1)S(1)}, u32[]{:S(2)}, u32[]{:S(2)}) %collective-permute-start.68) | collective-permute-done | bytes 524320 | tf_op jit(solution)/shard_map/ppermute | solution.py:66
  371.6 4.2 all-to-all-start.13
  382.0 14.9 %reduce-scatter.5.cloned.1.call-done = bf16[184,2048]{1,0:T(8,128)(2,1)} async-done(((bf16[736,2048]{1,0:T(8,128)(2,1)}), bf16[184,2048]{1,0:T(8,128)(2,1)}) %reduce-scatter.5.cloned.1.call-update) | async-done | bytes 753680 | tf_op jit(solution)/shard_map/reduce_scatter | solution.py:260
  399.9 4.3 all-to-all-start.15
  408.6 21.2 %collective-permute-done.71 = bf16[2,128,512]{2,1,0:T(8,128)(2,1)S(1)} collective-permute-done((bf16[2,128,512]{2,1,0:T(8,128)(2,1)S(1)}, bf16[2,128,512]{2,1,0:T(8,128)(2,1)S(1)}, u32[]{:S(2)}, u32[]{:S(2)}) %collective-permute-start.71) | collective-permute-done | bytes 262176 | tf_op jit(solution)/shard_map/ppermute | solution.py:66
  431.3 10.3 %shard_map.143 = (f32[255,2048]{1,0:T(8,128)}, f32[255,2048]{1,0:T(8,128)}, f32[255,2048]{1,0:T(8,128)}, f32[255,2048]{1,0:T(8,128)}) custom-call(bf16[255,192]{1,0:T(8,128)(2,1)} %fusion.118.send0, bf16[255,384]{1,0:T(8,128)(2,1)} %fusion.103.send1, bf16[192,2048]{1,0:T(8,128)(2,1)} %bitcast.62.near, bf16[384,2048]{1,0:T(8,128)(2,1)} %bitcast.69.far, ...), custom_call_target="tpu_custom_call" | custom-call | flops 601620480 | bytes 16777216 | tf_op jit(solution)/shard_map/pallas_call | solution.py:522
  (321 shorter events, 147.3 us)
Async XLA Ops:
  10.2 26.2 %collective-permute-start.44 = (bf16[2,128,512]{2,1,0:T(8,128)(2,1)}, bf16[2,128,512]{2,1,0:T(8,128)(2,1)}, u32[]{:S(2)}, u32[]{:S(2)}) collective-permute-start(bf16[2,128,512]{2,1,0:T(8,128)(2,1)} %get-tuple-element.352), channel_id=1, source_target_pairs={{0,4},{1,5},{2,6},{3,7},{4,0},{5,1},{6,2},{7,3},{8,12},{9,13},{10,... | collective-permute-start | bytes 786440 | tf_op jit(solution)/shard_map/ppermute | solution.py:66
  13.2 30.9 %collective-permute-start.42 = (bf16[2,128,512]{2,1,0:T(8,128)(2,1)}, bf16[2,128,512]{2,1,0:T(8,128)(2,1)}, u32[]{:S(2)}, u32[]{:S(2)}) collective-permute-start(bf16[2,128,512]{2,1,0:T(8,128)(2,1)} %get-tuple-element.353), channel_id=1, source_target_pairs={{0,2},{1,3},{2,0},{3,1},{4,6},{5,7},{6,4},{7,5},{8,10},{9,11},{10,... | collective-permute-start | bytes 786440 | tf_op jit(solution)/shard_map/ppermute | solution.py:66
  25.1 16.8 %all-to-all-start.8 = ((bf16[8,24,2048]{2,1,0:T(8,128)(2,1)}), bf16[8,24,2048]{2,1,0:T(8,128)(2,1)}, u32[]{:S(2)}, u32[]{:S(2)}) async-start(bf16[8,24,2048]{2,1,0:T(8,128)(2,1)} %bitcast.401), calls=%async_computation.8 | async-start | bytes 1572864 | tf_op jit(solution)/shard_map/all_to_all | solution.py:70
  29.3 44.5 %all-gather.3.cloned.1.call-start = ((), (), s32[]{:S(2)}) async-start(), calls=%async_computation.18 | async-start | bytes 1474560 | tf_op jit(solution)/shard_map/all_gather | solution.py:242
  38.2 14.5 %collective-permute-start.45 = (bf16[2,2,128,512]{3,2,0,1:T(8,128)(2,1)}, bf16[2,2,128,512]{3,2,0,1:T(8,128)(2,1)}, u32[]{:S(2)}, u32[]{:S(2)}) collective-permute-start(bf16[2,2,128,512]{3,2,0,1:T(8,128)(2,1)} %pad_maximum_fusion.15), channel_id=1, source_target_pairs={{0,2},{1,3},{2,0},{3,1},{4,6},{5,7},{6,4},{7,5},{8,10},{9,11},{10,... | collective-permute-start | bytes 1572872 | tf_op jit(solution)/shard_map/ppermute | solution.py:66
  45.2 11.9 %collective-permute-start.43 = (bf16[2,2,128,512]{3,2,0,1:T(8,128)(2,1)S(1)}, bf16[2,2,128,512]{3,2,0,1:T(8,128)(2,1)S(1)}, u32[]{:S(2)}, u32[]{:S(2)}) collective-permute-start(bf16[2,2,128,512]{3,2,0,1:T(8,128)(2,1)S(1)} %pad_maximum_fusion.14), channel_id=1, source_target_pairs={{0,4},{1,5},{2,6},{3,7},{4,0},{5,1},{6,2},{7,3},{8,12},{9,13},{10,... | collective-permute-start | bytes 1572872 | tf_op jit(solution)/shard_map/ppermute | solution.py:66
  60.6 37.8 %collective-permute-start.46 = (bf16[2,512,1024]{2,1,0:T(8,128)(2,1)}, bf16[2,512,1024]{2,1,0:T(8,128)(2,1)}, u32[]{:S(2)}, u32[]{:S(2)}) collective-permute-start(bf16[2,512,1024]{2,1,0:T(8,128)(2,1)} %bitcast.10.x0.c0), channel_id=1, source_target_pairs={{0,1},{1,0},{2,3},{3,2},{4,5},{5,4},{6,7},{7,6},{8,9},{9,8},{10,11... | collective-permute-start | bytes 6291464 | tf_op jit(solution)/shard_map/ppermute | solution.py:66
  77.1 13.9 %all-to-all-start.9 = ((bf16[8,128,256]{2,1,0:T(8,128)(2,1)}), bf16[8,128,256]{2,1,0:T(8,128)(2,1)}, u32[]{:S(2)}, u32[]{:S(2)}) async-start(bf16[8,128,256]{2,1,0:T(8,128)(2,1)} %get-tuple-element.147), calls=%async_computation.9 | async-start | bytes 1048576 | tf_op jit(solution)/shard_map/all_to_all | solution.py:70
  91.0 25.4 %all-to-all-start.10 = ((bf16[8,48,2048]{2,1,0:T(8,128)(2,1)}), bf16[8,48,2048]{2,1,0:T(8,128)(2,1)}, u32[]{:S(2)}, u32[]{:S(2)}) async-start(bf16[8,48,2048]{2,1,0:T(8,128)(2,1)} %bitcast.399), calls=%async_computation.10 | async-start | bytes 3145728 | tf_op jit(solution)/shard_map/all_to_all | solution.py:70
  95.4 82.7 %all-gather.5.cloned.1.call-start = ((), (), s32[]{:S(2)}) async-start(), calls=%async_computation.19 | async-start | bytes 3768320 | tf_op jit(solution)/shard_map/all_gather | solution.py:242
  109.7 9.6 %collective-permute-start.47 = (bf16[1,512,1024]{2,1,0:T(8,128)(2,1)}, bf16[1,512,1024]{2,1,0:T(8,128)(2,1)}, u32[]{:S(2)}, u32[]{:S(2)}) collective-permute-start(bf16[1,512,1024]{2,1,0:T(8,128)(2,1)} %get-tuple-element.150), channel_id=1, source_target_pairs={{0,1},{1,0},{2,3},{3,2},{4,5},{5,4},{6,7},{7,6},{8,9},{9,8},{10,11... | collective-permute-start | bytes 3145736 | tf_op jit(solution)/shard_map/ppermute | solution.py:66
  121.4 6.4 %collective-permute-start.48 = (bf16[1,2,128,512]{3,2,1,0:T(8,128)(2,1)S(1)}, bf16[1,2,128,512]{3,2,1,0:T(8,128)(2,1)S(1)}, u32[]{:S(2)}, u32[]{:S(2)}) collective-permute-start(bf16[1,2,128,512]{3,2,1,0:T(8,128)(2,1)S(1)} %slice.625), channel_id=1, source_target_pairs={{0,4},{1,5},{2,6},{3,7},{4,0},{5,1},{6,2},{7,3},{8,12},{9,13},{10,... | collective-permute-start | bytes 786440 | tf_op jit(solution)/shard_map/ppermute | solution.py:66
  122.1 8.4 %collective-permute-start.50 = (bf16[1,2,128,512]{3,2,1,0:T(8,128)(2,1)S(1)}, bf16[1,2,128,512]{3,2,1,0:T(8,128)(2,1)S(1)}, u32[]{:S(2)}, u32[]{:S(2)}) collective-permute-start(bf16[1,2,128,512]{3,2,1,0:T(8,128)(2,1)S(1)} %pad_maximum_fusion.19), channel_id=1, source_target_pairs={{0,2},{1,3},{2,0},{3,1},{4,6},{5,7},{6,4},{7,5},{8,10},{9,11},{10,... | collective-permute-start | bytes 786440 | tf_op jit(solution)/shard_map/ppermute | solution.py:66
  136.0 7.8 %collective-permute-start.52 = (bf16[1,128,512]{2,1,0:T(8,128)(2,1)S(1)}, bf16[1,128,512]{2,1,0:T(8,128)(2,1)S(1)}, u32[]{:S(2)}, u32[]{:S(2)}) collective-permute-start(bf16[1,128,512]{2,1,0:T(8,128)(2,1)S(1)} %get-tuple-element.365), channel_id=1, source_target_pairs={{0,2},{1,3},{2,0},{3,1},{4,6},{5,7},{6,4},{7,5},{8,10},{9,11},{10,... | collective-permute-start | bytes 393224 | tf_op jit(solution)/shard_map/ppermute | solution.py:66
  141.9 49.1 %collective-permute-start.55 = (bf16[1,2,128,512]{3,2,1,0:T(8,128)(2,1)}, bf16[1,2,128,512]{3,2,1,0:T(8,128)(2,1)}, u32[]{:S(2)}, u32[]{:S(2)}) collective-permute-start(bf16[1,2,128,512]{3,2,1,0:T(8,128)(2,1)} %pad_maximum_fusion.21), channel_id=1, source_target_pairs={{0,2},{1,3},{2,0},{3,1},{4,6},{5,7},{6,4},{7,5},{8,10},{9,11},{10,... | collective-permute-start | bytes 786440 | tf_op jit(solution)/shard_map/ppermute | solution.py:66
  144.6 47.4 %collective-permute-start.53 = (bf16[1,2,128,512]{3,2,1,0:T(8,128)(2,1)}, bf16[1,2,128,512]{3,2,1,0:T(8,128)(2,1)}, u32[]{:S(2)}, u32[]{:S(2)}) collective-permute-start(bf16[1,2,128,512]{3,2,1,0:T(8,128)(2,1)} %pad_maximum_fusion.20), channel_id=1, source_target_pairs={{0,4},{1,5},{2,6},{3,7},{4,0},{5,1},{6,2},{7,3},{8,12},{9,13},{10,... | collective-permute-start | bytes 786440 | tf_op jit(solution)/shard_map/ppermute | solution.py:66
  186.1 25.8 %all-to-all-start.11 = ((bf16[8,128,768]{2,1,0:T(8,128)(2,1)}), bf16[8,128,768]{2,1,0:T(8,128)(2,1)}, u32[]{:S(2)}, u32[]{:S(2)}) async-start(bf16[8,128,768]{2,1,0:T(8,128)(2,1)} %get-tuple-element.151), calls=%async_computation.11 | async-start | bytes 3145728 | tf_op jit(solution)/shard_map/all_to_all | solution.py:70
  228.6 8.4 %collective-permute-start.58 = (bf16[1,2,128,512]{3,2,1,0:T(8,128)(2,1)S(1)}, bf16[1,2,128,512]{3,2,1,0:T(8,128)(2,1)S(1)}, u32[]{:S(2)}, u32[]{:S(2)}) collective-permute-start(bf16[1,2,128,512]{3,2,1,0:T(8,128)(2,1)S(1)} %slice.642), channel_id=1, source_target_pairs={{0,4},{1,5},{2,6},{3,7},{4,0},{5,1},{6,2},{7,3},{8,12},{9,13},{10,... | collective-permute-start | bytes 786440 | tf_op jit(solution)/shard_map/ppermute | solution.py:66
  229.3 8.5 %collective-permute-start.60 = (bf16[1,2,128,512]{3,2,1,0:T(8,128)(2,1)S(1)}, bf16[1,2,128,512]{3,2,1,0:T(8,128)(2,1)S(1)}, u32[]{:S(2)}, u32[]{:S(2)}) collective-permute-start(bf16[1,2,128,512]{3,2,1,0:T(8,128)(2,1)S(1)} %pad_maximum_fusion.22), channel_id=1, source_target_pairs={{0,2},{1,3},{2,0},{3,1},{4,6},{5,7},{6,4},{7,5},{8,10},{9,11},{10,... | collective-permute-start | bytes 786440 | tf_op jit(solution)/shard_map/ppermute | solution.py:66
  248.6 6.7 %collective-permute-start.65 = (bf16[1,2,128,512]{3,2,1,0:T(8,128)(2,1)S(1)}, bf16[1,2,128,512]{3,2,1,0:T(8,128)(2,1)S(1)}, u32[]{:S(2)}, u32[]{:S(2)}) collective-permute-start(bf16[1,2,128,512]{3,2,1,0:T(8,128)(2,1)S(1)} %pad_maximum_fusion.24), channel_id=1, source_target_pairs={{0,2},{1,3},{2,0},{3,1},{4,6},{5,7},{6,4},{7,5},{8,10},{9,11},{10,... | collective-permute-start | bytes 786440 | tf_op jit(solution)/shard_map/ppermute | solution.py:66
  251.2 6.4 %collective-permute-start.63 = (bf16[1,2,128,512]{3,2,1,0:T(8,128)(2,1)S(1)}, bf16[1,2,128,512]{3,2,1,0:T(8,128)(2,1)S(1)}, u32[]{:S(2)}, u32[]{:S(2)}) collective-permute-start(bf16[1,2,128,512]{3,2,1,0:T(8,128)(2,1)S(1)} %pad_maximum_fusion.23), channel_id=1, source_target_pairs={{0,4},{1,5},{2,6},{3,7},{4,0},{5,1},{6,2},{7,3},{8,12},{9,13},{10,... | collective-permute-start | bytes 786440 | tf_op jit(solution)/shard_map/ppermute | solution.py:66
  285.3 13.9 %all-to-all-start.12 = ((bf16[8,128,256]{2,1,0:T(8,128)(2,1)}), bf16[8,128,256]{2,1,0:T(8,128)(2,1)}, u32[]{:S(2)}, u32[]{:S(2)}) async-start(bf16[8,128,256]{2,1,0:T(8,128)(2,1)} %bitcast.416), calls=%async_computation.12 | async-start | bytes 1048576 | tf_op jit(solution)/shard_map/all_to_all | solution.py:70
  289.5 79.9 %reduce-scatter.3.cloned.1.call-start = ((), (), s32[]{:S(2)}) async-start(), calls=%async_computation.20 | async-start | bytes 1474560 | tf_op jit(solution)/shard_map/reduce_scatter | solution.py:260
  307.5 25.3 %all-to-all-start.14 = ((bf16[8,128,768]{2,1,0:T(8,128)(2,1)}), bf16[8,128,768]{2,1,0:T(8,128)(2,1)}, u32[]{:S(2)}, u32[]{:S(2)}) async-start(bf16[8,128,768]{2,1,0:T(8,128)(2,1)} %bitcast.407), calls=%async_computation.15 | async-start | bytes 3145728 | tf_op jit(solution)/shard_map/all_to_all | solution.py:70
  311.8 85.2 %reduce-scatter.5.cloned.1.call-start = ((), (), s32[]{:S(2)}) async-start(), calls=%async_computation.21 | async-start | bytes 3768320 | tf_op jit(solution)/shard_map/reduce_scatter | solution.py:260
  341.5 9.5 %collective-permute-start.67 = (bf16[2,512,1024]{2,1,0:T(8,128)(2,1)}, bf16[2,512,1024]{2,1,0:T(8,128)(2,1)}, u32[]{:S(2)}, u32[]{:S(2)}) collective-permute-start(bf16[2,512,1024]{2,1,0:T(8,128)(2,1)} %get-tuple-element.162), channel_id=1, source_target_pairs={{0,1},{1,0},{2,3},{3,2},{4,5},{5,4},{6,7},{7,6},{8,9},{9,8},{10,11... | collective-permute-start | bytes 6291464 | tf_op jit(solution)/shard_map/ppermute | solution.py:66
  354.4 13.8 %collective-permute-start.68 = (bf16[2,2,128,512]{3,2,0,1:T(8,128)(2,1)S(1)}, bf16[2,2,128,512]{3,2,0,1:T(8,128)(2,1)S(1)}, u32[]{:S(2)}, u32[]{:S(2)}) collective-permute-start(bf16[2,2,128,512]{3,2,0,1:T(8,128)(2,1)S(1)} %copy.66), channel_id=1, source_target_pairs={{0,4},{1,5},{2,6},{3,7},{4,0},{5,1},{6,2},{7,3},{8,12},{9,13},{10,... | collective-permute-start | bytes 1572872 | tf_op jit(solution)/shard_map/ppermute | solution.py:66
  355.8 23.7 %collective-permute-start.70 = (bf16[2,2,128,512]{3,2,0,1:T(8,128)(2,1)}, bf16[2,2,128,512]{3,2,0,1:T(8,128)(2,1)}, u32[]{:S(2)}, u32[]{:S(2)}) collective-permute-start(bf16[2,2,128,512]{3,2,0,1:T(8,128)(2,1)} %pad_maximum_fusion.18), channel_id=1, source_target_pairs={{0,2},{1,3},{2,0},{3,1},{4,6},{5,7},{6,4},{7,5},{8,10},{9,11},{10,... | collective-permute-start | bytes 1572872 | tf_op jit(solution)/shard_map/ppermute | solution.py:66
  371.6 28.3 %all-to-all-start.13 = ((bf16[8,24,2048]{2,1,0:T(8,128)(2,1)}), bf16[8,24,2048]{2,1,0:T(8,128)(2,1)}, u32[]{:S(2)}, u32[]{:S(2)}) async-start(bf16[8,24,2048]{2,1,0:T(8,128)(2,1)} %bitcast.402), calls=%async_computation.14 | async-start | bytes 1572864 | tf_op jit(solution)/shard_map/all_to_all | solution.py:70
  377.6 29.8 %collective-permute-start.69 = (bf16[2,128,512]{2,1,0:T(8,128)(2,1)}, bf16[2,128,512]{2,1,0:T(8,128)(2,1)}, u32[]{:S(2)}, u32[]{:S(2)}) collective-permute-start(bf16[2,128,512]{2,1,0:T(8,128)(2,1)} %fusion.108), channel_id=1, source_target_pairs={{0,2},{1,3},{2,0},{3,1},{4,6},{5,7},{6,4},{7,5},{8,10},{9,11},{10,... | collective-permute-start | bytes 786440 | tf_op jit(solution)/shard_map/ppermute | solution.py:66
  399.9 31.4 %all-to-all-start.15 = ((bf16[8,48,2048]{2,1,0:T(8,128)(2,1)}), bf16[8,48,2048]{2,1,0:T(8,128)(2,1)}, u32[]{:S(2)}, u32[]{:S(2)}) async-start(bf16[8,48,2048]{2,1,0:T(8,128)(2,1)} %bitcast.400), calls=%async_computation.17 | async-start | bytes 3145728 | tf_op jit(solution)/shard_map/all_to_all | solution.py:70
  405.4 24.3 %collective-permute-start.71 = (bf16[2,128,512]{2,1,0:T(8,128)(2,1)S(1)}, bf16[2,128,512]{2,1,0:T(8,128)(2,1)S(1)}, u32[]{:S(2)}, u32[]{:S(2)}) collective-permute-start(bf16[2,128,512]{2,1,0:T(8,128)(2,1)S(1)} %fusion.109), channel_id=1, source_target_pairs={{0,4},{1,5},{2,6},{3,7},{4,0},{5,1},{6,2},{7,3},{8,12},{9,13},{10,... | collective-permute-start | bytes 786440 | tf_op jit(solution)/shard_map/ppermute | solution.py:66
  (56 other events, 517.6 us)
Sparse Core Ops, SparseCore 0:
  44.1 29.6 all-gather.2
  119.4 58.7 all-gather.4
  302.5 26.1 reduce-scatter.2
  341.7 55.2 reduce-scatter.4

commit v3 on v2

--- a/solution.py
+++ b/solution.py
@@ -145,6 +145,14 @@
     return jnp.concatenate([jnp.pad(p, ((0, -p.shape[0] % 8), (0, 0))) for p in pieces], axis=0)
 
 
+def selected(places, blocks):
+    found, at = [], 0
+    for place in places:
+        found.append(product(place, blocks[at : at + place.shape[1]]).astype(BF))
+        at += place.shape[1]
+    return found
+
+
 def rotate(values, count):
     return lax.ppermute(values, "seq", [(i, (i + 1) % count) for i in range(count)])
 
@@ -188,16 +196,28 @@
         mean = capacity * size / count
         self.pair_cap = round_up(mean + 4.2 * math.sqrt(mean) + 1, 8)
         share = min(1.0, ((tok - 1) * count / devices + capacity) / count)
-        mean = size * share
-        self.row_cap = min(round_up(mean + 3.7 * math.sqrt(mean * (1 - share)), 8), round_up(size, 8))
+        cuts = [0, size] if group == 0 else [0, size - ff_share(tok) * D // BLK, size]
+        self.cuts = list(zip(cuts[:-1], cuts[1:], strict=True))
+        self.row_caps = []
+        for start, end in self.cuts:
+            mean = (end - start) * share
+            cap = round_up(mean + 3.7 * math.sqrt(mean * (1 - share)), 8)
+            self.row_caps.append(min(cap, end - start))
         match = (owner[None] == jnp.arange(devices, dtype=jnp.int32)[:, None, None]).astype(BF)
         earlier = jnp.einsum("otl,lm->otm", match, before(size), preferred_element_type=F32)
         pair_rank = jnp.sum(match.astype(F32) * earlier, axis=0).astype(jnp.int32)
         owner_seq = jnp.where(owner >= 0, owner // tok, -1)
         earlier_seq = jnp.sum(earlier.reshape(seq, tok, tok, size), axis=1)
         match_seq = owner_seq[None] == jnp.arange(seq, dtype=jnp.int32)[:, None, None]
-        row_rank = jnp.sum(jnp.where(match_seq, earlier_seq, 0.0), axis=0).astype(jnp.int32)
-        self.fits = (jnp.max(pair_rank) < self.pair_cap) & (jnp.max(row_rank) < self.row_cap)
+        self.fits = jnp.max(pair_rank) < self.pair_cap
+        row_ranks = []
+        for (start, end), cap in zip(self.cuts, self.row_caps, strict=True):
+            part = earlier_seq[:, :, start:end] - earlier_seq[:, :, start : start + 1]
+            rank = jnp.sum(jnp.where(match_seq[:, :, start:end], part, 0.0), axis=0)
+            rank = rank.astype(jnp.int32)
+            self.fits = self.fits & (jnp.max(rank) < cap)
+            row_ranks.append(jnp.where(rank < cap, rank, -1))
+        row_rank = jnp.concatenate(row_ranks, axis=1)
         me_seq, me_tok = lax.axis_index("seq"), lax.axis_index("tok")
         me = me_seq * tok + me_tok
         shard = jnp.arange(tok, dtype=jnp.int32)[:, None]
@@ -225,22 +245,35 @@
             -1,
         )
         from_pairs = onehot(arrive, tok * self.pair_cap)
-        to_rows = onehot(jnp.where(my_seq == me_seq, my_row, -1), self.row_cap)
+        offset = [sum(self.row_caps[:k]) for k in range(len(self.row_caps))]
+        shift = jnp.concatenate(
+            [
+                jnp.full((end - start,), at, jnp.int32)
+                for (start, end), at in zip(self.cuts, offset, strict=True)
+            ]
+        )
+        to_rows = onehot(
+            jnp.where((my_seq == me_seq) & (my_row >= 0), my_row + shift, -1), sum(self.row_caps)
+        )
         self.compact = left_product(to_rows, from_pairs).astype(BF)
-        my_place = jnp.where(
-            (my_row < self.row_cap) & (my_owner >= 0), my_seq * self.row_cap + my_row, -1
-        )
-        self.place = onehot(my_place, seq * self.row_cap)
-        self.place_back = (
-            jnp.arange(seq * self.row_cap, dtype=jnp.int32)[:, None] == my_place[None, :]
-        ).astype(BF)
+        self.places, self.places_back = [], []
+        for (start, end), cap in zip(self.cuts, self.row_caps, strict=True):
+            row, owner_of = my_row[start:end], my_owner[start:end]
+            at = jnp.where((row >= 0) & (owner_of >= 0), my_seq[start:end] * cap + row, -1)
+            self.places.append(onehot(at, seq * cap))
+            every = jnp.arange(seq * cap, dtype=jnp.int32)[:, None]
+            self.places_back.append((every == at[None, :]).astype(BF))
 
     def fetch(self, rounded):
         packed = left_product(self.send, rounded).astype(BF)
         packed = exchange(packed)
         rows = product(self.compact, packed).astype(BF)
-        rows = lax.all_gather(rows, "seq", axis=0, tiled=True)
-        return self.place, rows
+        fetched, at = [], 0
+        for place, cap in zip(self.places, self.row_caps, strict=True):
+            part = lax.all_gather(rows[at : at + cap], "seq", axis=0, tiled=True)
+            fetched.append((place, part))
+            at += cap
+        return fetched
 
     def fetch_any(self, rounded):
         width = rounded.shape[1]
@@ -254,15 +287,22 @@
         for _ in range(self.seq - 1):
             mine = rotate(mine, self.seq)
             total = total + mine
-        return jnp.eye(self.size, dtype=BF), total
+        return [(jnp.eye(end - start, dtype=BF), total[start:end]) for start, end in self.cuts]
+
+    def plain(self):
+        eyes = [jnp.eye(end - start, dtype=BF) for start, end in self.cuts]
+        return (self.fetch_any, eyes, self.give_any)
 
     def give(self, rows):
-        rows = lax.psum_scatter(rows, "seq", scatter_dimension=0, tiled=True)
+        rows = jnp.concatenate(
+            [lax.psum_scatter(part, "seq", scatter_dimension=0, tiled=True) for part in rows]
+        )
         packed = left_product(self.compact, rows).astype(BF)
         packed = exchange(packed)
         return packed
 
     def give_any(self, rows):
+        rows = jnp.concatenate(rows)
         width = rows.shape[1]
         total = rows.astype(F32)
         passing = rows
@@ -333,7 +373,7 @@
     rounded = master.astype(BF)
     layer = layer_of_eight if tok == 8 else layer_of_any
     result, grad_input, packed = layer(
-        tokens, cotangent, rounded, [(r.fetch, r.place_back, r.give) for r in routes]
+        tokens, cotangent, rounded, [(r.fetch, r.places_back, r.give) for r in routes]
     )
     mine = (owners == me)[None, :]
     numbers = jnp.arange(owners.shape[0], dtype=jnp.int32)[None, :]
@@ -349,8 +389,9 @@
     found = (result, grad_input) + owned_update(routes, packed, held, rates)
 
     def any_owners(carried):
-        plain = [(r.fetch_any, jnp.eye(r.size, dtype=BF), r.give_any) for r in routes]
-        result, grad_input, parts = layer(tokens, cotangent, rounded, plain)
+        result, grad_input, parts = layer(
+            tokens, cotangent, rounded, [route.plain() for route in routes]
+        )
         reduced = parts[0] + parts[1]
         updated = adam_update(reduced, *held, *rates)
         return (jnp.int32(1), result, grad_input, reduced) + updated
@@ -381,15 +422,13 @@
     return lax.broadcasted_iota(jnp.int32, shape, 1) < 64
 
 
-def unpack_ff(place_ref, rows_ref, sent_ref, down_ref, flat, wide, tall):
-    for c in range(16):
-        lanes = pl.ds(128 * c, 128)
-        found = dot(place_ref[...], rows_ref[:, lanes])
-        flat[0, pl.ds(c, 176, stride=16), :] = found[:176]
-        flat[1, pl.ds(c, 176, stride=16), :] = found[176:352]
-        tall[c % 8, pl.ds(c // 8, 192, stride=2), :] = found[352:]
-    for k in range(8):
-        down_ref[:, pl.ds(128 * k, 128)] = tall[k].astype(BF)
+def unpack_ff(place_ref, rows_ref, sent_ref, flat, wide):
+    for c in range(0, 16, 2):
+        found = dot(place_ref[...], rows_ref[:, pl.ds(128 * c, 256)])
+        for m in range(2):
+            half = found[176 * m : 176 * m + 176]
+            flat[m, pl.ds(c, 176, stride=16), :] = half[:, :128]
+            flat[m, pl.ds(c + 1, 176, stride=16), :] = half[:, 128:]
     low = low_lanes((64, 128))
     zero = jnp.zeros((64, 128), F32)
     for m in range(2):
@@ -409,7 +448,16 @@
             sent_ref[k // 3, :, pl.ds(384 * m + 128 * (k % 3), 128)] = wide[k].astype(BF)
 
 
-def pack_ff(place_ref, back_ref, down_ref, rows_ref, flat, wide, tall):
+def unpack_down(place_ref, rows_ref, down_ref, tall):
+    for c in range(0, 16, 2):
+        found = dot(place_ref[...], rows_ref[:, pl.ds(128 * c, 256)])
+        tall[c % 8, pl.ds(c // 8, 192, stride=2), :] = found[:, :128]
+        tall[c % 8 + 1, pl.ds(c // 8, 192, stride=2), :] = found[:, 128:]
+    for k in range(8):
+        down_ref[:, pl.ds(128 * k, 128)] = tall[k].astype(BF)
+
+
+def pack_ff(place_ref, back_ref, rows_ref, flat, wide):
     low = low_lanes((64, 128))
     for m in range(2):
         flat[m, pl.ds(2752, 64), :] = jnp.zeros((64, 128), F32)
@@ -428,18 +476,25 @@
         for k in range(21):
             current, after = after, turned(k + 1)
             flat[m, pl.ds(22 + k, 64, stride=43), :] = jnp.where(low, current, after)
+    for c in range(0, 16, 2):
+        grads = jnp.concatenate(
+            [
+                jnp.concatenate([flat[m, pl.ds(c + h, 176, stride=16), :] for m in range(2)], axis=0)
+                for h in range(2)
+            ],
+            axis=1,
+        ).astype(BF)
+        rows_ref[:, pl.ds(128 * c, 256)] = dot(place_ref[...], grads).astype(BF)
+
+
+def pack_down(place_ref, down_ref, rows_ref, tall):
     for k in range(8):
         tall[k] = down_ref[:, pl.ds(128 * k, 128)].astype(F32)
-    for c in range(16):
+    for c in range(0, 16, 2):
         grads = jnp.concatenate(
-            [
-                flat[0, pl.ds(c, 176, stride=16), :],
-                flat[1, pl.ds(c, 176, stride=16), :],
-                tall[c % 8, pl.ds(c // 8, 192, stride=2), :],
-            ],
-            axis=0,
+            [tall[c % 8 + h, pl.ds(c // 8, 192, stride=2), :] for h in range(2)], axis=1
         ).astype(BF)
-        rows_ref[:, pl.ds(128 * c, 128)] = dot(place_ref[...], grads).astype(BF)
+        rows_ref[:, pl.ds(128 * c, 256)] = dot(place_ref[...], grads).astype(BF)
 
 
 def unpack_mix(place_ref, rows_ref, gains_ref, sent_ref, out_ref, thin, tall):
@@ -570,8 +625,8 @@
 
 def pair_weights(query, keys, first, me):
     inner = right_product(query, keys) * (1.0 / math.sqrt(FD))
-    row = lax.broadcasted_iota(jnp.int32, inner.shape, 0) + first
-    column = lax.broadcasted_iota(jnp.int32, inner.shape, 1)
+    row = lax.broadcasted_iota(jnp.int32, (inner.shape[0], 1), 0) + first
+    column = lax.broadcasted_iota(jnp.int32, (1, inner.shape[1]), 1)
     causal = token_at(row, me) >= token_at(column, me)
     return inner, jnp.where(causal, 1.0 + inner + 0.5 * inner * inner, 0.0), causal
 
@@ -705,8 +760,7 @@
 
     x_all, c_all = gather_rows(tokens[0]), gather_rows(cotangent[0])
 
-    place, rows = routes[0][0](rounded)
-    shard = product(place, rows).astype(BF)
+    shard = jnp.concatenate([product(*part).astype(BF) for part in routes[0][0](rounded)])
     gain_one = shard[0, :D].astype(F32)
     gain_two = shard[0, D:].astype(F32)
 
@@ -730,8 +784,7 @@
     def padded(blocks):
         return jnp.pad(blocks.reshape(slice_rows, FF), ((0, 0), (0, tok * ff_slice - FF)))
 
-    place, rows = routes[1][0](rounded)
-    shard = product(place, rows).astype(BF)
+    shard = jnp.concatenate([product(*part).astype(BF) for part in routes[1][0](rounded)])
     sent = jnp.concatenate(
         [
             columns_out(padded(piece_of(shard, tok, 1, 4)), tok),
@@ -795,7 +848,7 @@
 
     back_gate, back_up = flat(back[..., :ff_slice]), flat(back[..., ff_slice:])
     blocks = joined([back_gate, back_up, grad_w_down.reshape(-1, BLK)])
-    far = routes[1][2](product(routes[1][1], blocks).astype(BF))
+    far = routes[1][2](selected(routes[1][1], blocks))
 
     grad_w_out = left_product(mixed, grad_mixer).astype(BF)
     grad_mixed = right_product(grad_mixer, w_out).astype(BF)
@@ -844,7 +897,7 @@
             grad_w_out.reshape(-1, BLK),
         ]
     )
-    near = routes[0][2](product(routes[0][1], blocks).astype(BF))
+    near = routes[0][2](selected(routes[0][1], blocks))
 
     normed_one, scale_one = normalize(input_rows)
     grad_input = grad_middle + norm_back(grad_hidden_one * gain_one, normed_one, scale_one)
@@ -857,7 +910,7 @@
     half = seq_len // 2
     x_near, x_far = gather_of_eight(jnp.concatenate([tokens, cotangent]))
 
-    place, rows = routes[0][0](rounded)
+    ((place, rows),) = routes[0][0](rounded)
     gains, sent, w_out = call(
         unpack_mix,
         [((8, BLK), F32), ((8, 128, 256), BF), ((128, D), BF)],
@@ -867,15 +920,23 @@
         nbytes=2 << 20,
     )(place, rows)
     w_qkv = exchange(sent).reshape(D, 256)
-    place, rows = routes[1][0](rounded)
-    sent, w_down = call(
+    (place, rows), (down_place, down_rows) = routes[1][0](rounded)
+    (sent,) = call(
         unpack_ff,
-        [((8, 128, 768), BF), ((384, D), BF)],
-        [((2, 2816, 128), F32), ((24, 128, 128), F32), ((8, 384, 128), F32)],
+        [((8, 128, 768), BF)],
+        [((2, 2816, 128), F32), ((24, 128, 128), F32)],
         operands=2,
-        flops=2 * place.shape[0] * place.shape[1] * BLK,
-        nbytes=6 << 20,
+        flops=2 * place.size * BLK,
+        nbytes=4 << 20,
     )(place, rows)
+    (w_down,) = call(
+        unpack_down,
+        [((384, D), BF)],
+        [((8, 384, 128), F32)],
+        operands=2,
+        flops=2 * down_place.size * BLK,
+        nbytes=2 << 20,
+    )(down_place, down_rows)
     w_in = exchange(sent).reshape(D, 768)
 
     hidden_one, qkv, mixed, mean, total, keep, send = call(
@@ -923,18 +984,28 @@
     )
     m_near, m_far = gather_of_eight(grad_middle.astype(BF)[None])
 
-    grad_w_in = left_product(jnp.concatenate([h_near[0], h_far[0]]), grad_gate_up).astype(BF)
-    grad_w_down = left_product(hidden, jnp.concatenate([x_near[1], x_far[1]])).astype(BF)
+    all_rows = jnp.concatenate([h_near[0], h_far[0]])
+    grad_w_in = left_product(all_rows, grad_gate_up).astype(BF)
+    all_rows = jnp.concatenate([x_near[1], x_far[1]])
+    grad_w_down = left_product(hidden, all_rows).astype(BF)
     back = exchange(grad_w_in.reshape(8, 128, 768))
     (rows,) = call(
         pack_ff,
-        [((routes[1][1].shape[0], BLK), BF)],
-        [((2, 2816, 128), F32), ((24, 128, 128), F32), ((8, 384, 128), F32)],
-        operands=3,
-        flops=2 * routes[1][1].size * BLK,
-        nbytes=6 << 20,
-    )(routes[1][1], back, grad_w_down)
-    far = routes[1][2](rows)
+        [((routes[1][1][0].shape[0], BLK), BF)],
+        [((2, 2816, 128), F32), ((24, 128, 128), F32)],
+        operands=2,
+        flops=2 * routes[1][1][0].size * BLK,
+        nbytes=4 << 20,
+    )(routes[1][1][0], back)
+    (down_rows,) = call(
+        pack_down,
+        [((routes[1][1][1].shape[0], BLK), BF)],
+        [((8, 384, 128), F32)],
+        operands=2,
+        flops=2 * routes[1][1][1].size * BLK,
+        nbytes=2 << 20,
+    )(routes[1][1][1], grad_w_down)
+    far = routes[1][2]([rows, down_rows])
 
     grad_qkv, keep, send, gain_terms, grad_w_out = call(
         mix_back,
@@ -967,13 +1038,13 @@
     grad_gains = jnp.concatenate([gain_terms[0], grad_gain_two])
     (rows,) = call(
         pack_mix,
-        [((routes[0][1].shape[0], BLK), BF)],
+        [((routes[0][1][0].shape[0], BLK), BF)],
         [((4, 128, 128), F32), ((16, 128, 128), F32)],
         operands=4,
-        flops=2 * routes[0][1].size * BLK,
+        flops=2 * routes[0][1][0].size * BLK,
         nbytes=2 << 20,
-    )(routes[0][1], jnp.pad(grad_gains[None], ((0, 7), (0, 0))), back, grad_w_out)
-    near = routes[0][2](rows)
+    )(routes[0][1][0], jnp.pad(grad_gains[None], ((0, 7), (0, 0))), back, grad_w_out)
+    near = routes[0][2]([rows])
 
     normed_one, scale_one = normalize(input_rows)
     grad_input = grad_middle + norm_back(

time: 457 us -> 455 us (level)
  starting transfers between devices: 63.8 us -> 68.6 us
    all_to_all x8, waiting for transfers between devices: 54.4 us -> 45.1 us  [exchange(): return lax.all_to_all(values, 'tok', 0, 0, tiled=True)]
    reduce_scatter x2 -> x3, waiting for transfers between devices: 14.9 us -> 24.1 us  [give(): lax.psum_scatter(part, 'seq', scatter_dimension=0, tiled=True)]
    ppermute x30, waiting for transfers between devices: 81 us -> 72.7 us  [swap(): return lax.ppermute(values, 'tok', [(i, i ^ mask) for i in range(8)])]
    all_gather x2 -> x3, waiting for transfers between devices: 44 us -> 47.7 us  [fetch(): part = lax.all_gather(rows[at:at + cap], 'seq', axis=0, tiled=True)]
    pallas_call x3 -> x5, Pallas kernels: 19.9 us -> 18.8 us  [the longest x1 5.03 us: layer_of_eight(): call(pack_ff, [((routes[1][1][0].shape[0], BLK), BF)], [((2, 2816, 128),...]
  transfers between devices with their start and end apart: 42 -> 44, of which waited for: 27 -> 25; matrix products, arithmetic and copies ran while one was open for 18% -> 18% of each run, Pallas kernels for 7% -> 7%
where the time goes in v3:
time: 455 us; the launch traced here: 448 us
  waiting for transfers between devices  190 us (42%)
  Pallas kernels  75.6 us (17%)
  starting transfers between devices  68.6 us (15%)
  other arithmetic  40.7 us (9%)
  local copies, waits for them, and re-layouts  27.4 us (6%)
  matrix products  25.6 us (6%)
  between operations  19.3 us (4%)
    ppermute x30, waiting for transfers between devices, swap(): return lax.ppermute(values, 'tok', [(i, i ^ mask) for i in range(8)])  72.7 us
    all_gather x3, waiting for transfers between devices, fetch(): part = lax.all_gather(rows[at:at + cap], 'seq', axis=0, tiled=True)  47.7 us
    all_to_all x8, waiting for transfers between devices, exchange(): return lax.all_to_all(values, 'tok', 0, 0, tiled=True)  45.1 us
    all_to_all x8, starting transfers between devices, exchange(): return lax.all_to_all(values, 'tok', 0, 0, tiled=True)  34.7 us
    ppermute x30, starting transfers between devices, swap(): return lax.ppermute(values, 'tok', [(i, i ^ mask) for i in range(8)])  33.1 us
    reduce_scatter x3, waiting for transfers between devices, give(): lax.psum_scatter(part, 'seq', scatter_dimension=0, tiled=True)  24.1 us
    pallas_call x1, Pallas kernels, layer_of_eight(): call(mix_back, [((seq_len, 256), BF), ((2, half, D), BF), ((2, half, D),...  19.7 us
    dot_general x9, matrix products, left_product(): lax.dot_general(left, right, (((0,), (0,)), ((), ())), preferred_element_...  19.5 us
  transfers between devices with their start and end apart: 44, of which 25 were waited for; matrix products, arithmetic and copies ran while one was open for 18% of the time, Pallas kernels for 7%

profile of v3, /device:TPU:0, one launch (start us, length us, event | category | flops | bytes accessed | tf_op | source)
XLA Modules:
  0.0 448.0 jit_solution(4773622382840437298)
XLA Ops:
  23.9 4.2 all-to-all-start.8
  37.3 4.1 all-to-all-done.8
  43.6 7.4 %collective-permute-done.45 = bf16[2,2,128,512]{3,2,0,1:T(8,128)(2,1)} collective-permute-done((bf16[2,2,128,512]{3,2,0,1:T(8,128)(2,1)}, bf16[2,2,128,512]{3,2,0,1:T(8,128)(2,1)}, u32[]{:S(2)}, u32[]{:S(2)}) %collective-permute-start.45) | collective-permute-done | bytes 524320 | tf_op jit(solution)/shard_map/ppermute | solution.py:66
  57.2 16.1 %all-gather.4.cloned.1.call-done.rows_ref = bf16[288,2048]{1,0:T(8,128)(2,1)} async-done(((bf16[72,2048]{1,0:T(8,128)(2,1)}), bf16[288,2048]{1,0:T(8,128)(2,1)}) %all-gather.4.cloned.1.call-update) | async-done | bytes 1179664 | tf_op jit(solution)/shard_map/all_gather | solution.py:273
  73.3 3.3 shard_map.136
  76.6 4.1 all-to-all-start.9
  82.7 7.7 %all-to-all-done.9 = bf16[8,128,256]{2,1,0:T(8,128)(2,1)} async-done(((bf16[8,128,256]{2,1,0:T(8,128)(2,1)}), bf16[8,128,256]{2,1,0:T(8,128)(2,1)}, u32[]{:S(2)}, u32[]{:S(2)}) %all-to-all-start.9) | async-done | bytes 524320 | tf_op jit(solution)/shard_map/all_to_all | solution.py:70
  90.5 4.3 all-to-all-start.10
  96.9 11.4 %shard_map.137 = (bf16[1024,1024]{1,0:T(8,128)(2,1)}, bf16[1024,256]{1,0:T(8,128)(2,1)}, bf16[1024,128]{1,0:T(8,128)(2,1)}, f32[1024,128]{1,0:T(8,128)}, f32[102...) custom-call(s32[1]{0:T(128)} %bitcast.5.me_ref, bf16[2,512,1024]{2,1,0:T(8,128)(2,1)} %bitcast.10.x0.c0, ...), custom_call_target="tpu_custom_call" | custom-call | flops 2952790016 | bytes 10485760 | tf_op jit(solution)/shard_map/pallas_call | solution.py:942
  109.4 6.3 %all-to-all-done.10 = bf16[8,48,2048]{2,1,0:T(8,128)(2,1)} async-done(((bf16[8,48,2048]{2,1,0:T(8,128)(2,1)}), bf16[8,48,2048]{2,1,0:T(8,128)(2,1)}, u32[]{:S(2)}, u32[]{:S(2)}) %all-to-all-start.10) | async-done | bytes 1572896 | tf_op jit(solution)/shard_map/all_to_all | solution.py:70
  123.2 5.0 %collective-permute-done.48 = bf16[1,2,128,512]{3,2,1,0:T(8,128)(2,1)S(1)} collective-permute-done((bf16[1,2,128,512]{3,2,1,0:T(8,128)(2,1)S(1)}, bf16[1,2,128,512]{3,2,1,0:T(8,128)(2,1)S(1)}, u32[]{:S(2)}, u32[]{:S(2)}) %collective-permute-start.48) | collective-permute-done | bytes 262176 | tf_op jit(solution)/shard_map/ppermute | solution.py:66
  150.3 12.6 %all-gather.6.cloned.1.call-done.rows_ref = bf16[512,2048]{1,0:T(8,128)(2,1)} async-done(((bf16[128,2048]{1,0:T(8,128)(2,1)}), bf16[512,2048]{1,0:T(8,128)(2,1)}) %all-gather.6.cloned.1.call-update) | async-done | bytes 2097168 | tf_op jit(solution)/shard_map/all_gather | solution.py:273
  162.8 4.7 %shard_map.138 = bf16[8,128,768]{2,1,0:T(8,128)(2,1)} custom-call(bf16[352,512]{1,0:T(8,128)(2,1)} %fusion.80.place_ref, bf16[512,2048]{1,0:T(8,128)(2,1)} %all-gather.6.cloned.1.call-done.rows_ref), custom_call_target="tpu_custom_call" | custom-call | flops 738197504 | bytes 4194304 | tf_op jit(solution)/shard_map/pallas_call | solution.py:924
  167.6 4.5 %all-to-all-start.11 = ((bf16[8,128,768]{2,1,0:T(8,128)(2,1)}), bf16[8,128,768]{2,1,0:T(8,128)(2,1)}, u32[]{:S(2)}, u32[]{:S(2)}) async-start(bf16[8,128,768]{2,1,0:T(8,128)(2,1)} %shard_map.138), calls=%async_computation.11 | async-start | bytes 3145728 | tf_op jit(solution)/shard_map/all_to_all | solution.py:70
  176.7 19.1 %all-gather.8.cloned.1.call-done.rows_ref = bf16[320,2048]{1,0:T(8,128)(2,1)} async-done(((bf16[80,2048]{1,0:T(8,128)(2,1)}), bf16[320,2048]{1,0:T(8,128)(2,1)}) %all-gather.8.cloned.1.call-update) | async-done | bytes 1310736 | tf_op jit(solution)/shard_map/all_gather | solution.py:273
  198.7 12.0 %shard_map.140 = (bf16[1024,384]{1,0:T(8,128)(2,1)}, bf16[1024,768]{1,0:T(8,128)(2,1)}, bf16[1,512,1024]{2,1,0:T(8,128)(2,1)}, bf16[1,512,1024]{2,1,0:T(8,128)(2...) custom-call(bf16[1,512,1024]{2,1,0:T(8,128)(2,1)} %bitcast.33.h0, ...), custom_call_target="tpu_custom_call" | custom-call | flops 4831838208 | bytes 14680064 | tf_op jit(solution)/shard_map/pallas_call | solution.py:966
  218.6 5.2 %collective-permute-done.58 = bf16[1,2,128,512]{3,2,1,0:T(8,128)(2,1)S(1)} collective-permute-done((bf16[1,2,128,512]{3,2,1,0:T(8,128)(2,1)S(1)}, bf16[1,2,128,512]{3,2,1,0:T(8,128)(2,1)S(1)}, u32[]{:S(2)}, u32[]{:S(2)}) %collective-permute-start.58) | collective-permute-done | bytes 262176 | tf_op jit(solution)/shard_map/ppermute | solution.py:66
  239.3 3.7 collective-permute-done.65
  250.5 19.7 %shard_map.141 = (bf16[1024,256]{1,0:T(8,128)(2,1)}, bf16[2,512,1024]{2,1,0:T(8,128)(2,1)}, bf16[2,512,1024]{2,1,0:T(8,128)(2,1)}, f32[8,1024]{1,0:T(8,128)}, bf16[128,1024]{1,0:T(8,128)(2,1)}) custom-call(s32[1]{0:T(128)} %bitcast.5.me_ref, bf16[1,512,1024]{2,1,0:T(8,128)(2,1)} %bitcast.405, bf16[1,512,1024]{2,1,0:T(8,128)(2,1)} %copy-done.80, ...), custom_call_target="tpu_custom_call" | custom-call | flops 6442450944 | bytes 20971520 | tf_op jit(solution)/shard_map/pallas_call | solution.py:1010
  273.5 4.1 all-to-all-start.12
  280.2 7.2 %all-to-all-done.12.back_ref = bf16[8,128,256]{2,1,0:T(8,128)(2,1)} async-done(((bf16[8,128,256]{2,1,0:T(8,128)(2,1)}), bf16[8,128,256]{2,1,0:T(8,128)(2,1)}, u32[]{:S(2)}, u32[]{:S(2)}) %all-to-all-start.12) | async-done | bytes 524320 | tf_op jit(solution)/shard_map/all_to_all | solution.py:70
  287.4 3.3 shard_map.142
  297.9 5.1 %fusion.64 = bf16[1024,768]{1,0:T(8,128)(2,1)} fusion(bf16[1024,768]{1,0:T(8,128)(2,1)} %get-tuple-element.161, bf16[512,1024]{1,0:T(8,128)(2,1)} %bitcast.65, bf16[512,1024]{1,0:T(8,128)(2,1)} %bitcast.64), kind=kOutput, calls=%fused_computation.176 | convolution fusion | flops 1615593472 | bytes 5242880 | tf_op jit(solution)/shard_map/dot_general | solution.py:47
  303.0 4.3 all-to-all-start.14
  308.5 19.8 %all-to-all-done.14.back_ref = bf16[8,128,768]{2,1,0:T(8,128)(2,1)} async-done(((bf16[8,128,768]{2,1,0:T(8,128)(2,1)}), bf16[8,128,768]{2,1,0:T(8,128)(2,1)}, u32[]{:S(2)}, u32[]{:S(2)}) %all-to-all-start.14) | async-done | bytes 1572896 | tf_op jit(solution)/shard_map/all_to_all | solution.py:70
  328.3 5.0 %shard_map.143 = bf16[512,2048]{1,0:T(8,128)(2,1)} custom-call(bf16[512,352]{1,0:T(8,128)(2,1)} %fusion.79.place_ref, bf16[8,128,768]{2,1,0:T(8,128)(2,1)} %all-to-all-done.14.back_ref), custom_call_target="tpu_custom_call" | custom-call | flops 738197504 | bytes 4194304 | tf_op jit(solution)/shard_map/pallas_call | solution.py:992
  348.0 7.6 %collective-permute-done.68 = bf16[2,2,128,512]{3,2,0,1:T(8,128)(2,1)S(1)} collective-permute-done((bf16[2,2,128,512]{3,2,0,1:T(8,128)(2,1)S(1)}, bf16[2,2,128,512]{3,2,0,1:T(8,128)(2,1)S(1)}, u32[]{:S(2)}, u32[]{:S(2)}) %collective-permute-start.68) | collective-permute-done | bytes 524320 | tf_op jit(solution)/shard_map/ppermute | solution.py:66
  359.0 4.9 %all-to-all-start.13 = ((bf16[8,24,2048]{2,1,0:T(8,128)(2,1)}), bf16[8,24,2048]{2,1,0:T(8,128)(2,1)}, u32[]{:S(2)}, u32[]{:S(2)}) async-start(bf16[8,24,2048]{2,1,0:T(8,128)(2,1)} %bitcast.398), calls=%async_computation.14 | async-start | bytes 1572864 | tf_op jit(solution)/shard_map/all_to_all | solution.py:70
  371.1 24.1 %reduce-scatter.6.cloned.1.call-done = bf16[128,2048]{1,0:T(8,128)(2,1)} async-done(((bf16[512,2048]{1,0:T(8,128)(2,1)}), bf16[128,2048]{1,0:T(8,128)(2,1)}) %reduce-scatter.6.cloned.1.call-update) | async-done | bytes 524304 | tf_op jit(solution)/shard_map/reduce_scatter | solution.py:298
  398.2 4.3 all-to-all-start.15
  406.9 21.2 %collective-permute-done.71 = bf16[2,128,512]{2,1,0:T(8,128)(2,1)S(1)} collective-permute-done((bf16[2,128,512]{2,1,0:T(8,128)(2,1)S(1)}, bf16[2,128,512]{2,1,0:T(8,128)(2,1)S(1)}, u32[]{:S(2)}, u32[]{:S(2)}) %collective-permute-start.71) | collective-permute-done | bytes 262176 | tf_op jit(solution)/shard_map/ppermute | solution.py:66
  429.6 10.3 %shard_map.145 = (f32[255,2048]{1,0:T(8,128)}, f32[255,2048]{1,0:T(8,128)}, f32[255,2048]{1,0:T(8,128)}, f32[255,2048]{1,0:T(8,128)}) custom-call(bf16[255,192]{1,0:T(8,128)(2,1)} %fusion.124.send0, bf16[255,384]{1,0:T(8,128)(2,1)} %fusion.107.send1, bf16[192,2048]{1,0:T(8,128)(2,1)} %bitcast.63.near, bf16[384,2048]{1,0:T(8,128)(2,1)} %bitcast.70.far, ...), custom_call_target="tpu_custom_call" | custom-call | flops 601620480 | bytes 16777216 | tf_op jit(solution)/shard_map/pallas_call | solution.py:577
  (337 shorter events, 152.0 us)
Async XLA Ops:
  10.3 18.6 %collective-permute-start.44 = (bf16[2,128,512]{2,1,0:T(8,128)(2,1)}, bf16[2,128,512]{2,1,0:T(8,128)(2,1)}, u32[]{:S(2)}, u32[]{:S(2)}) collective-permute-start(bf16[2,128,512]{2,1,0:T(8,128)(2,1)} %get-tuple-element.381), channel_id=1, source_target_pairs={{0,4},{1,5},{2,6},{3,7},{4,0},{5,1},{6,2},{7,3},{8,12},{9,13},{10,... | collective-permute-start | bytes 786440 | tf_op jit(solution)/shard_map/ppermute | solution.py:66
  13.3 20.6 %collective-permute-start.42 = (bf16[2,128,512]{2,1,0:T(8,128)(2,1)}, bf16[2,128,512]{2,1,0:T(8,128)(2,1)}, u32[]{:S(2)}, u32[]{:S(2)}) collective-permute-start(bf16[2,128,512]{2,1,0:T(8,128)(2,1)} %get-tuple-element.382), channel_id=1, source_target_pairs={{0,2},{1,3},{2,0},{3,1},{4,6},{5,7},{6,4},{7,5},{8,10},{9,11},{10,... | collective-permute-start | bytes 786440 | tf_op jit(solution)/shard_map/ppermute | solution.py:66
  23.9 17.4 %all-to-all-start.8 = ((bf16[8,24,2048]{2,1,0:T(8,128)(2,1)}), bf16[8,24,2048]{2,1,0:T(8,128)(2,1)}, u32[]{:S(2)}, u32[]{:S(2)}) async-start(bf16[8,24,2048]{2,1,0:T(8,128)(2,1)} %bitcast.397), calls=%async_computation.8 | async-start | bytes 1572864 | tf_op jit(solution)/shard_map/all_to_all | solution.py:70
  28.2 45.1 %all-gather.4.cloned.1.call-start = ((), (), s32[]{:S(2)}) async-start(), calls=%async_computation.19 | async-start | bytes 1474560 | tf_op jit(solution)/shard_map/all_gather | solution.py:273
  30.8 20.3 %collective-permute-start.45 = (bf16[2,2,128,512]{3,2,0,1:T(8,128)(2,1)}, bf16[2,2,128,512]{3,2,0,1:T(8,128)(2,1)}, u32[]{:S(2)}, u32[]{:S(2)}) collective-permute-start(bf16[2,2,128,512]{3,2,0,1:T(8,128)(2,1)} %pad_maximum_fusion.16), channel_id=1, source_target_pairs={{0,2},{1,3},{2,0},{3,1},{4,6},{5,7},{6,4},{7,5},{8,10},{9,11},{10,... | collective-permute-start | bytes 1572872 | tf_op jit(solution)/shard_map/ppermute | solution.py:66
  35.8 16.3 %collective-permute-start.43 = (bf16[2,2,128,512]{3,2,0,1:T(8,128)(2,1)}, bf16[2,2,128,512]{3,2,0,1:T(8,128)(2,1)}, u32[]{:S(2)}, u32[]{:S(2)}) collective-permute-start(bf16[2,2,128,512]{3,2,0,1:T(8,128)(2,1)} %pad_maximum_fusion.15), channel_id=1, source_target_pairs={{0,4},{1,5},{2,6},{3,7},{4,0},{5,1},{6,2},{7,3},{8,12},{9,13},{10,... | collective-permute-start | bytes 1572872 | tf_op jit(solution)/shard_map/ppermute | solution.py:66
  55.7 41.2 %collective-permute-start.46 = (bf16[2,512,1024]{2,1,0:T(8,128)(2,1)}, bf16[2,512,1024]{2,1,0:T(8,128)(2,1)}, u32[]{:S(2)}, u32[]{:S(2)}) collective-permute-start(bf16[2,512,1024]{2,1,0:T(8,128)(2,1)} %bitcast.10.x0.c0), channel_id=1, source_target_pairs={{0,1},{1,0},{2,3},{3,2},{4,5},{5,4},{6,7},{7,6},{8,9},{9,8},{10,11... | collective-permute-start | bytes 6291464 | tf_op jit(solution)/shard_map/ppermute | solution.py:66
  76.6 13.9 %all-to-all-start.9 = ((bf16[8,128,256]{2,1,0:T(8,128)(2,1)}), bf16[8,128,256]{2,1,0:T(8,128)(2,1)}, u32[]{:S(2)}, u32[]{:S(2)}) async-start(bf16[8,128,256]{2,1,0:T(8,128)(2,1)} %get-tuple-element.143), calls=%async_computation.9 | async-start | bytes 1048576 | tf_op jit(solution)/shard_map/all_to_all | solution.py:70
  90.5 25.3 %all-to-all-start.10 = ((bf16[8,48,2048]{2,1,0:T(8,128)(2,1)}), bf16[8,48,2048]{2,1,0:T(8,128)(2,1)}, u32[]{:S(2)}, u32[]{:S(2)}) async-start(bf16[8,48,2048]{2,1,0:T(8,128)(2,1)} %bitcast.395), calls=%async_computation.10 | async-start | bytes 3145728 | tf_op jit(solution)/shard_map/all_to_all | solution.py:70
  94.8 68.1 %all-gather.6.cloned.1.call-start = ((), (), s32[]{:S(2)}) async-start(), calls=%async_computation.20 | async-start | bytes 2621440 | tf_op jit(solution)/shard_map/all_gather | solution.py:273
  108.3 11.3 %collective-permute-start.47 = (bf16[1,512,1024]{2,1,0:T(8,128)(2,1)}, bf16[1,512,1024]{2,1,0:T(8,128)(2,1)}, u32[]{:S(2)}, u32[]{:S(2)}) collective-permute-start(bf16[1,512,1024]{2,1,0:T(8,128)(2,1)} %get-tuple-element.146), channel_id=1, source_target_pairs={{0,1},{1,0},{2,3},{3,2},{4,5},{5,4},{6,7},{7,6},{8,9},{9,8},{10,11... | collective-permute-start | bytes 3145736 | tf_op jit(solution)/shard_map/ppermute | solution.py:66
  119.6 76.2 %all-gather.8.cloned.1.call-start = ((), (), s32[]{:S(2)}) async-start(), calls=%async_computation.21 | async-start | bytes 1638400 | tf_op jit(solution)/shard_map/all_gather | solution.py:273
  122.4 8.4 %collective-permute-start.50 = (bf16[1,2,128,512]{3,2,1,0:T(8,128)(2,1)S(1)}, bf16[1,2,128,512]{3,2,1,0:T(8,128)(2,1)S(1)}, u32[]{:S(2)}, u32[]{:S(2)}) collective-permute-start(bf16[1,2,128,512]{3,2,1,0:T(8,128)(2,1)S(1)} %pad_maximum_fusion.20), channel_id=1, source_target_pairs={{0,2},{1,3},{2,0},{3,1},{4,6},{5,7},{6,4},{7,5},{8,10},{9,11},{10,... | collective-permute-start | bytes 786440 | tf_op jit(solution)/shard_map/ppermute | solution.py:66
  144.5 27.6 %collective-permute-start.55 = (bf16[1,2,128,512]{3,2,1,0:T(8,128)(2,1)}, bf16[1,2,128,512]{3,2,1,0:T(8,128)(2,1)}, u32[]{:S(2)}, u32[]{:S(2)}) collective-permute-start(bf16[1,2,128,512]{3,2,1,0:T(8,128)(2,1)} %pad_maximum_fusion.22), channel_id=1, source_target_pairs={{0,2},{1,3},{2,0},{3,1},{4,6},{5,7},{6,4},{7,5},{8,10},{9,11},{10,... | collective-permute-start | bytes 786440 | tf_op jit(solution)/shard_map/ppermute | solution.py:66
  147.7 25.4 %collective-permute-start.53 = (bf16[1,2,128,512]{3,2,1,0:T(8,128)(2,1)}, bf16[1,2,128,512]{3,2,1,0:T(8,128)(2,1)}, u32[]{:S(2)}, u32[]{:S(2)}) collective-permute-start(bf16[1,2,128,512]{3,2,1,0:T(8,128)(2,1)} %pad_maximum_fusion.21), channel_id=1, source_target_pairs={{0,4},{1,5},{2,6},{3,7},{4,0},{5,1},{6,2},{7,3},{8,12},{9,13},{10,... | collective-permute-start | bytes 786440 | tf_op jit(solution)/shard_map/ppermute | solution.py:66
  167.6 31.1 %all-to-all-start.11 = ((bf16[8,128,768]{2,1,0:T(8,128)(2,1)}), bf16[8,128,768]{2,1,0:T(8,128)(2,1)}, u32[]{:S(2)}, u32[]{:S(2)}) async-start(bf16[8,128,768]{2,1,0:T(8,128)(2,1)} %shard_map.138), calls=%async_computation.11 | async-start | bytes 3145728 | tf_op jit(solution)/shard_map/all_to_all | solution.py:70
  175.4 23.3 %collective-permute-start.56 = (bf16[1,512,1024]{2,1,0:T(8,128)(2,1)}, bf16[1,512,1024]{2,1,0:T(8,128)(2,1)}, u32[]{:S(2)}, u32[]{:S(2)}) collective-permute-start(bf16[1,512,1024]{2,1,0:T(8,128)(2,1)} %bitcast.33.h0), channel_id=1, source_target_pairs={{0,1},{1,0},{2,3},{3,2},{4,5},{5,4},{6,7},{7,6},{8,9},{9,8},{10,11... | collective-permute-start | bytes 3145736 | tf_op jit(solution)/shard_map/ppermute | solution.py:66
  215.4 8.4 %collective-permute-start.58 = (bf16[1,2,128,512]{3,2,1,0:T(8,128)(2,1)S(1)}, bf16[1,2,128,512]{3,2,1,0:T(8,128)(2,1)S(1)}, u32[]{:S(2)}, u32[]{:S(2)}) collective-permute-start(bf16[1,2,128,512]{3,2,1,0:T(8,128)(2,1)S(1)} %slice.729), channel_id=1, source_target_pairs={{0,4},{1,5},{2,6},{3,7},{4,0},{5,1},{6,2},{7,3},{8,12},{9,13},{10,... | collective-permute-start | bytes 786440 | tf_op jit(solution)/shard_map/ppermute | solution.py:66
  217.0 8.5 %collective-permute-start.60 = (bf16[1,2,128,512]{3,2,1,0:T(8,128)(2,1)S(1)}, bf16[1,2,128,512]{3,2,1,0:T(8,128)(2,1)S(1)}, u32[]{:S(2)}, u32[]{:S(2)}) collective-permute-start(bf16[1,2,128,512]{3,2,1,0:T(8,128)(2,1)S(1)} %pad_maximum_fusion.23), channel_id=1, source_target_pairs={{0,2},{1,3},{2,0},{3,1},{4,6},{5,7},{6,4},{7,5},{8,10},{9,11},{10,... | collective-permute-start | bytes 786440 | tf_op jit(solution)/shard_map/ppermute | solution.py:66
  236.4 6.7 %collective-permute-start.65 = (bf16[1,2,128,512]{3,2,1,0:T(8,128)(2,1)S(1)}, bf16[1,2,128,512]{3,2,1,0:T(8,128)(2,1)S(1)}, u32[]{:S(2)}, u32[]{:S(2)}) collective-permute-start(bf16[1,2,128,512]{3,2,1,0:T(8,128)(2,1)S(1)} %pad_maximum_fusion.25), channel_id=1, source_target_pairs={{0,2},{1,3},{2,0},{3,1},{4,6},{5,7},{6,4},{7,5},{8,10},{9,11},{10,... | collective-permute-start | bytes 786440 | tf_op jit(solution)/shard_map/ppermute | solution.py:66
  273.5 13.9 %all-to-all-start.12 = ((bf16[8,128,256]{2,1,0:T(8,128)(2,1)}), bf16[8,128,256]{2,1,0:T(8,128)(2,1)}, u32[]{:S(2)}, u32[]{:S(2)}) async-start(bf16[8,128,256]{2,1,0:T(8,128)(2,1)} %bitcast.409), calls=%async_computation.12 | async-start | bytes 1048576 | tf_op jit(solution)/shard_map/all_to_all | solution.py:70
  277.6 79.1 %reduce-scatter.4.cloned.1.call-start = ((), (), s32[]{:S(2)}) async-start(), calls=%async_computation.22 | async-start | bytes 1474560 | tf_op jit(solution)/shard_map/reduce_scatter | solution.py:298
  290.6 80.4 %reduce-scatter.8.cloned.1.call-start = ((), (), s32[]{:S(2)}) async-start(), calls=%async_computation.24 | async-start | bytes 1638400 | tf_op jit(solution)/shard_map/reduce_scatter | solution.py:298
  303.0 25.3 %all-to-all-start.14 = ((bf16[8,128,768]{2,1,0:T(8,128)(2,1)}), bf16[8,128,768]{2,1,0:T(8,128)(2,1)}, u32[]{:S(2)}, u32[]{:S(2)}) async-start(bf16[8,128,768]{2,1,0:T(8,128)(2,1)} %bitcast.403), calls=%async_computation.15 | async-start | bytes 3145728 | tf_op jit(solution)/shard_map/all_to_all | solution.py:70
  307.3 87.9 %reduce-scatter.6.cloned.1.call-start = ((), (), s32[]{:S(2)}) async-start(), calls=%async_computation.23 | async-start | bytes 2621440 | tf_op jit(solution)/shard_map/reduce_scatter | solution.py:298
  308.2 33.3 %collective-permute-start.67 = (bf16[2,512,1024]{2,1,0:T(8,128)(2,1)}, bf16[2,512,1024]{2,1,0:T(8,128)(2,1)}, u32[]{:S(2)}, u32[]{:S(2)}) collective-permute-start(bf16[2,512,1024]{2,1,0:T(8,128)(2,1)} %get-tuple-element.156), channel_id=1, source_target_pairs={{0,1},{1,0},{2,3},{3,2},{4,5},{5,4},{6,7},{7,6},{8,9},{9,8},{10,11... | collective-permute-start | bytes 6291464 | tf_op jit(solution)/shard_map/ppermute | solution.py:66
  344.7 10.8 %collective-permute-start.68 = (bf16[2,2,128,512]{3,2,0,1:T(8,128)(2,1)S(1)}, bf16[2,2,128,512]{3,2,0,1:T(8,128)(2,1)S(1)}, u32[]{:S(2)}, u32[]{:S(2)}) collective-permute-start(bf16[2,2,128,512]{3,2,0,1:T(8,128)(2,1)S(1)} %copy.191), channel_id=1, source_target_pairs={{0,4},{1,5},{2,6},{3,7},{4,0},{5,1},{6,2},{7,3},{8,12},{9,13},{10,... | collective-permute-start | bytes 1572872 | tf_op jit(solution)/shard_map/ppermute | solution.py:66
  346.3 22.3 %collective-permute-start.70 = (bf16[2,2,128,512]{3,2,0,1:T(8,128)(2,1)}, bf16[2,2,128,512]{3,2,0,1:T(8,128)(2,1)}, u32[]{:S(2)}, u32[]{:S(2)}) collective-permute-start(bf16[2,2,128,512]{3,2,0,1:T(8,128)(2,1)} %pad_maximum_fusion.19), channel_id=1, source_target_pairs={{0,2},{1,3},{2,0},{3,1},{4,6},{5,7},{6,4},{7,5},{8,10},{9,11},{10,... | collective-permute-start | bytes 1572872 | tf_op jit(solution)/shard_map/ppermute | solution.py:66
  359.0 39.1 %all-to-all-start.13 = ((bf16[8,24,2048]{2,1,0:T(8,128)(2,1)}), bf16[8,24,2048]{2,1,0:T(8,128)(2,1)}, u32[]{:S(2)}, u32[]{:S(2)}) async-start(bf16[8,24,2048]{2,1,0:T(8,128)(2,1)} %bitcast.398), calls=%async_computation.14 | async-start | bytes 1572864 | tf_op jit(solution)/shard_map/all_to_all | solution.py:70
  365.7 40.0 %collective-permute-start.69 = (bf16[2,128,512]{2,1,0:T(8,128)(2,1)}, bf16[2,128,512]{2,1,0:T(8,128)(2,1)}, u32[]{:S(2)}, u32[]{:S(2)}) collective-permute-start(bf16[2,128,512]{2,1,0:T(8,128)(2,1)} %fusion.114), channel_id=1, source_target_pairs={{0,2},{1,3},{2,0},{3,1},{4,6},{5,7},{6,4},{7,5},{8,10},{9,11},{10,... | collective-permute-start | bytes 786440 | tf_op jit(solution)/shard_map/ppermute | solution.py:66
  398.2 31.4 %all-to-all-start.15 = ((bf16[8,48,2048]{2,1,0:T(8,128)(2,1)}), bf16[8,48,2048]{2,1,0:T(8,128)(2,1)}, u32[]{:S(2)}, u32[]{:S(2)}) async-start(bf16[8,48,2048]{2,1,0:T(8,128)(2,1)} %bitcast.396), calls=%async_computation.18 | async-start | bytes 3145728 | tf_op jit(solution)/shard_map/all_to_all | solution.py:70
  403.7 24.3 %collective-permute-start.71 = (bf16[2,128,512]{2,1,0:T(8,128)(2,1)S(1)}, bf16[2,128,512]{2,1,0:T(8,128)(2,1)S(1)}, u32[]{:S(2)}, u32[]{:S(2)}) collective-permute-start(bf16[2,128,512]{2,1,0:T(8,128)(2,1)S(1)} %fusion.115), channel_id=1, source_target_pairs={{0,4},{1,5},{2,6},{3,7},{4,0},{5,1},{6,2},{7,3},{8,12},{9,13},{10,... | collective-permute-start | bytes 786440 | tf_op jit(solution)/shard_map/ppermute | solution.py:66
  (57 other events, 546.9 us)
Sparse Core Ops, SparseCore 0:
  43.6 29.6 all-gather.3
  119.7 43.0 all-gather.5
  164.4 31.3 all-gather.7
  290.8 26.6 reduce-scatter.3
  320.2 29.9 reduce-scatter.7
  352.8 42.3 reduce-scatter.5

commit v4 on v3

--- a/solution.py
+++ b/solution.py
@@ -151,6 +151,26 @@
         found.append(product(place, blocks[at : at + place.shape[1]]).astype(BF))
         at += place.shape[1]
     return found
+
+
+def line(count, step):
+    return [(i, i + step) for i in range(count) if 0 <= i + step < count]
+
+
+def shift(values, step, seq):
+    return lax.ppermute(values, "seq", line(seq, step))
+
+
+def sum_line(pieces, seq):
+    pieces = pieces.reshape(seq, -1, pieces.shape[1])
+    up = down = None
+    for k in range(1, seq):
+        own_up, own_down = pieces[seq - k], pieces[k]
+        up = own_up if up is None else (own_up.astype(F32) + up.astype(F32)).astype(BF)
+        down = own_down if down is None else (own_down.astype(F32) + down.astype(F32)).astype(BF)
+        up = shift(up, 1, seq)
+        down = shift(down, -1, seq)
+    return pieces[0].astype(F32) + up.astype(F32) + down.astype(F32)
 
 
 def rotate(values, count):
@@ -261,6 +281,9 @@
             row, owner_of = my_row[start:end], my_owner[start:end]
             at = jnp.where((row >= 0) & (owner_of >= 0), my_seq[start:end] * cap + row, -1)
             self.places.append(onehot(at, seq * cap))
+            if group == 0:
+                away = (my_seq[start:end] - me_seq + seq) % seq
+                at = jnp.where((row >= 0) & (owner_of >= 0), away * cap + row, -1)
             every = jnp.arange(seq * cap, dtype=jnp.int32)[:, None]
             self.places_back.append((every == at[None, :]).astype(BF))
 
@@ -294,12 +317,11 @@
         return (self.fetch_any, eyes, self.give_any)
 
     def give(self, rows):
-        rows = jnp.concatenate(
+        if self.group == 0:
+            return sum_line(rows[0], self.seq).astype(BF)
+        return jnp.concatenate(
             [lax.psum_scatter(part, "seq", scatter_dimension=0, tiled=True) for part in rows]
         )
-        packed = left_product(self.compact, rows).astype(BF)
-        packed = exchange(packed)
-        return packed
 
     def give_any(self, rows):
         rows = jnp.concatenate(rows)
@@ -372,9 +394,22 @@
     routes = [Route(owners, slots, group, seq, tok, capacity) for group in range(2)]
     rounded = master.astype(BF)
     layer = layer_of_eight if tok == 8 else layer_of_any
-    result, grad_input, packed = layer(
+    result, grad_input, sums = layer(
         tokens, cotangent, rounded, [(r.fetch, r.places_back, r.give) for r in routes]
     )
+    rows = sum(sum(r.row_caps) for r in routes)
+    wide = [r.compact.reshape(-1, tok, r.pair_cap) for r in routes]
+    compact = jnp.concatenate(
+        [
+            jnp.pad(wide[0], ((0, 0), (0, 0), (0, routes[1].pair_cap))),
+            jnp.pad(wide[1], ((0, 0), (0, 0), (routes[0].pair_cap, 0))),
+        ]
+    ).reshape(rows, -1)
+    send = jnp.concatenate(
+        [r.send.reshape(capacity, tok, r.pair_cap) for r in routes], axis=2
+    ).reshape(capacity, -1)
+    packed = left_product(compact, jnp.concatenate(sums)).astype(BF)
+    packed = exchange(packed)
     mine = (owners == me)[None, :]
     numbers = jnp.arange(owners.shape[0], dtype=jnp.int32)[None, :]
     counts = jnp.sum(
@@ -386,7 +421,7 @@
     )
     rates = rates_for(kinds, tokens.shape[1] * tok)
     held = (first_moment, second_moment, master)
-    found = (result, grad_input) + owned_update(routes, packed, held, rates)
+    found = (result, grad_input) + owned_update(send, packed, held, rates)
 
     def any_owners(carried):
         result, grad_input, parts = layer(
@@ -551,10 +586,8 @@
         rows_ref[:, lanes] = dot(place_ref[...], grads).astype(BF)
 
 
-def select_update(
-    send0, send1, near, far, first, second, weights, rates, decays, out0, out1, out2, out3
-):
-    grads = dot(send0[...], near[...]) + dot(send1[...], far[...])
+def select_update(send, rows, first, second, weights, rates, decays, out0, out1, out2, out3):
+    grads = dot(send[...], rows[...])
     out0[...] = grads
     updated = adam_update(
         grads, first[...], second[...], weights[...], rates[...][:, 0], decays[...][:, 0]
@@ -562,7 +595,7 @@
     out1[...], out2[...], out3[...] = updated
 
 
-def owned_update(routes, packed, held, rates):
+def owned_update(send, rows, held, rates):
     capacity, width = held[0].shape
     columns = 256
 
@@ -578,14 +611,14 @@
             select_update,
             out_shape=[jax.ShapeDtypeStruct((capacity, width), F32)] * 4,
             grid=(width // columns,),
-            in_specs=[whole(routes[0].send), whole(routes[1].send)]
-            + [part(array) for array in (*packed, *held)]
+            in_specs=[whole(send)]
+            + [part(array) for array in (rows, *held)]
             + [whole(rates[0]), whole(rates[1])],
             out_specs=[part(held[0])] * 4,
             cost_estimate=pl.CostEstimate(
-                flops=2 * capacity * width * 576, bytes_accessed=16 << 20, transcendentals=0
+                flops=2 * send.size * width, bytes_accessed=16 << 20, transcendentals=0
             ),
-        )(routes[0].send, routes[1].send, *packed, *held, *rates)
+        )(send, rows, *held, *rates)
     )
 
 

time: 455 us -> 457 us (level)
  waiting for transfers between devices: 190 us -> 165 us
  starting transfers between devices: 68.6 us -> 80.4 us
  other arithmetic: 40.7 us -> 51.9 us
    ppermute x0 -> x6, waiting for transfers between devices: none -> 32.2 us  [shift(): return lax.ppermute(values, 'seq', line(seq, step))]
    all_to_all x8 -> x7, waiting for transfers between devices: 45.1 us -> 17.6 us  [exchange(): return lax.all_to_all(values, 'tok', 0, 0, tiled=True)]
    reduce_scatter x3 -> x2, waiting for transfers between devices: 24.1 us -> 0.01 us  [give(): lax.psum_scatter(part, 'seq', scatter_dimension=0, tiled=True)]
    ppermute x0 -> x6, starting transfers between devices: none -> 15.3 us  [shift(): return lax.ppermute(values, 'seq', line(seq, step))]
    ppermute x30, waiting for transfers between devices: 72.7 us -> 67.7 us  [swap(): return lax.ppermute(values, 'tok', [(i, i ^ mask) for i in range(8)])]
    convert_element_type x2 -> x3, other arithmetic: 1.56 us -> 6.31 us  [the longest x2 4.35 us: sum_line(): (own_up.astype(F32) + up.astype(F32)).astype(BF)]
    all_to_all x8 -> x7, starting transfers between devices: 34.7 us -> 30.2 us  [exchange(): return lax.all_to_all(values, 'tok', 0, 0, tiled=True)]
    dot_general x9 -> x8, matrix products: 19.5 us -> 18 us  [left_product(): lax.dot_general(left, right, (((0,), (0,)), ((), ())), preferred_element_...]
  transfers between devices with their start and end apart: 44 -> 48, of which waited for: 25 -> 24; matrix products, arithmetic and copies ran while one was open for 18% -> 22% of each run, Pallas kernels for 7% -> 12%
where the time goes in v4:
time: 457 us; the launch traced here: 449 us
  waiting for transfers between devices  165 us (36%)
  starting transfers between devices  80.4 us (18%)
  Pallas kernels  75.2 us (16%)
  other arithmetic  51.9 us (11%)
  local copies, waits for them, and re-layouts  31.3 us (7%)
  matrix products  24 us (5%)
  between operations  19.6 us (4%)
    ppermute x30, waiting for transfers between devices, swap(): return lax.ppermute(values, 'tok', [(i, i ^ mask) for i in range(8)])  67.7 us
    all_gather x3, waiting for transfers between devices, fetch(): part = lax.all_gather(rows[at:at + cap], 'seq', axis=0, tiled=True)  47.7 us
    ppermute x30, starting transfers between devices, swap(): return lax.ppermute(values, 'tok', [(i, i ^ mask) for i in range(8)])  33.9 us
    ppermute x6, waiting for transfers between devices, shift(): return lax.ppermute(values, 'seq', line(seq, step))  32.2 us
    all_to_all x7, starting transfers between devices, exchange(): return lax.all_to_all(values, 'tok', 0, 0, tiled=True)  30.2 us
    pallas_call x1, Pallas kernels, layer_of_eight(): call(mix_back, [((seq_len, 256), BF), ((2, half, D), BF), ((2, half, D),...  19.8 us
    dot_general x8, matrix products, left_product(): lax.dot_general(left, right, (((0,), (0,)), ((), ())), preferred_element_...  18 us
    all_to_all x7, waiting for transfers between devices, exchange(): return lax.all_to_all(values, 'tok', 0, 0, tiled=True)  17.6 us
  transfers between devices with their start and end apart: 48, of which 24 were waited for; matrix products, arithmetic and copies ran while one was open for 22% of the time, Pallas kernels for 12%

profile of v4, /device:TPU:0, one launch (start us, length us, event | category | flops | bytes accessed | tf_op | source)
XLA Modules:
  0.0 449.0 jit_solution(4758956043269958819)
XLA Ops:
  24.0 4.2 all-to-all-start.8
  37.4 4.0 all-to-all-done.8
  43.7 7.4 %collective-permute-done.45 = bf16[2,2,128,512]{3,2,0,1:T(8,128)(2,1)} collective-permute-done((bf16[2,2,128,512]{3,2,0,1:T(8,128)(2,1)}, bf16[2,2,128,512]{3,2,0,1:T(8,128)(2,1)}, u32[]{:S(2)}, u32[]{:S(2)}) %collective-permute-start.45) | collective-permute-done | bytes 524320 | tf_op jit(solution)/shard_map/ppermute | solution.py:66
  57.3 16.1 %all-gather.4.cloned.1.call-done.rows_ref = bf16[288,2048]{1,0:T(8,128)(2,1)} async-done(((bf16[72,2048]{1,0:T(8,128)(2,1)}), bf16[288,2048]{1,0:T(8,128)(2,1)}) %all-gather.4.cloned.1.call-update) | async-done | bytes 1179664 | tf_op jit(solution)/shard_map/all_gather | solution.py:296
  76.7 4.2 all-to-all-start.9
  82.8 7.7 %all-to-all-done.9 = bf16[8,128,256]{2,1,0:T(8,128)(2,1)} async-done(((bf16[8,128,256]{2,1,0:T(8,128)(2,1)}), bf16[8,128,256]{2,1,0:T(8,128)(2,1)}, u32[]{:S(2)}, u32[]{:S(2)}) %all-to-all-start.9) | async-done | bytes 524320 | tf_op jit(solution)/shard_map/all_to_all | solution.py:70
  90.5 4.3 all-to-all-start.10
  97.5 11.4 %shard_map.137 = (bf16[1024,1024]{1,0:T(8,128)(2,1)}, bf16[1024,256]{1,0:T(8,128)(2,1)}, bf16[1024,128]{1,0:T(8,128)(2,1)}, f32[1024,128]{1,0:T(8,128)}, f32[102...) custom-call(s32[1]{0:T(128)} %bitcast.5.me_ref, bf16[2,512,1024]{2,1,0:T(8,128)(2,1)} %bitcast.10.x0.c0, ...), custom_call_target="tpu_custom_call" | custom-call | flops 2952790016 | bytes 10485760 | tf_op jit(solution)/shard_map/pallas_call | solution.py:975
  110.0 5.9 %all-to-all-done.10 = bf16[8,48,2048]{2,1,0:T(8,128)(2,1)} async-done(((bf16[8,48,2048]{2,1,0:T(8,128)(2,1)}), bf16[8,48,2048]{2,1,0:T(8,128)(2,1)}, u32[]{:S(2)}, u32[]{:S(2)}) %all-to-all-start.10) | async-done | bytes 1572896 | tf_op jit(solution)/shard_map/all_to_all | solution.py:70
  123.3 5.0 %collective-permute-done.48 = bf16[1,2,128,512]{3,2,1,0:T(8,128)(2,1)S(1)} collective-permute-done((bf16[1,2,128,512]{3,2,1,0:T(8,128)(2,1)S(1)}, bf16[1,2,128,512]{3,2,1,0:T(8,128)(2,1)S(1)}, u32[]{:S(2)}, u32[]{:S(2)}) %collective-permute-start.48) | collective-permute-done | bytes 262176 | tf_op jit(solution)/shard_map/ppermute | solution.py:66
  150.5 12.5 %all-gather.6.cloned.1.call-done.rows_ref = bf16[512,2048]{1,0:T(8,128)(2,1)} async-done(((bf16[128,2048]{1,0:T(8,128)(2,1)}), bf16[512,2048]{1,0:T(8,128)(2,1)}) %all-gather.6.cloned.1.call-update) | async-done | bytes 2097168 | tf_op jit(solution)/shard_map/all_gather | solution.py:296
  162.9 4.7 %shard_map.138 = bf16[8,128,768]{2,1,0:T(8,128)(2,1)} custom-call(bf16[352,512]{1,0:T(8,128)(2,1)} %fusion.84.place_ref, bf16[512,2048]{1,0:T(8,128)(2,1)} %all-gather.6.cloned.1.call-done.rows_ref), custom_call_target="tpu_custom_call" | custom-call | flops 738197504 | bytes 4194304 | tf_op jit(solution)/shard_map/pallas_call | solution.py:957
  167.7 4.3 all-to-all-start.11
  176.7 19.2 %all-gather.8.cloned.1.call-done.rows_ref = bf16[320,2048]{1,0:T(8,128)(2,1)} async-done(((bf16[80,2048]{1,0:T(8,128)(2,1)}), bf16[320,2048]{1,0:T(8,128)(2,1)}) %all-gather.8.cloned.1.call-update) | async-done | bytes 1310736 | tf_op jit(solution)/shard_map/all_gather | solution.py:296
  198.8 12.0 %shard_map.140 = (bf16[1024,384]{1,0:T(8,128)(2,1)}, bf16[1024,768]{1,0:T(8,128)(2,1)}, bf16[1,512,1024]{2,1,0:T(8,128)(2,1)}, bf16[1,512,1024]{2,1,0:T(8,128)(2...) custom-call(bf16[1,512,1024]{2,1,0:T(8,128)(2,1)} %bitcast.33.h0, ...), custom_call_target="tpu_custom_call" | custom-call | flops 4831838208 | bytes 14680064 | tf_op jit(solution)/shard_map/pallas_call | solution.py:999
  217.5 5.3 %collective-permute-done.58 = bf16[1,2,128,512]{3,2,1,0:T(8,128)(2,1)S(1)} collective-permute-done((bf16[1,2,128,512]{3,2,1,0:T(8,128)(2,1)S(1)}, bf16[1,2,128,512]{3,2,1,0:T(8,128)(2,1)S(1)}, u32[]{:S(2)}, u32[]{:S(2)}) %collective-permute-start.58) | collective-permute-done | bytes 262176 | tf_op jit(solution)/shard_map/ppermute | solution.py:66
  248.7 4.6 %fusion.64 = bf16[1024,768]{1,0:T(8,128)(2,1)} fusion(bf16[1024,768]{1,0:T(8,128)(2,1)S(1)} %copy-done.93, bf16[512,1024]{1,0:T(8,128)(2,1)} %bitcast.67, bf16[512,1024]{1,0:T(8,128)(2,1)} %bitcast.66), kind=kOutput, calls=%fused_computation.175 | convolution fusion | flops 1615593472 | bytes 5242880 | tf_op jit(solution)/shard_map/dot_general | solution.py:47
  253.3 4.7 %all-to-all-start.13 = ((bf16[8,128,768]{2,1,0:T(8,128)(2,1)}), bf16[8,128,768]{2,1,0:T(8,128)(2,1)}, u32[]{:S(2)}, u32[]{:S(2)}) async-start(bf16[8,128,768]{2,1,0:T(8,128)(2,1)} %bitcast.402), calls=%async_computation.13 | async-start | bytes 3145728 | tf_op jit(solution)/shard_map/all_to_all | solution.py:70
  259.4 19.8 %shard_map.141 = (bf16[1024,256]{1,0:T(8,128)(2,1)}, bf16[2,512,1024]{2,1,0:T(8,128)(2,1)}, bf16[2,512,1024]{2,1,0:T(8,128)(2,1)}, f32[8,1024]{1,0:T(8,128)}, bf16[128,1024]{1,0:T(8,128)(2,1)}) custom-call(s32[1]{0:T(128)} %bitcast.5.me_ref, bf16[1,512,1024]{2,1,0:T(8,128)(2,1)} %bitcast.48.m0, bf16[1,512,1024]{2,1,0:T(8,128)(2,1)} %collective-permute-done.66.m1, ...), custom_call_target="tpu_custom_call" | custom-call | flops 6442450944 | bytes 20971520 | tf_op jit(solution)/shard_map/pallas_call | solution.py:1043
  282.4 4.2 all-to-all-start.12
  291.5 5.0 %shard_map.143 = bf16[512,2048]{1,0:T(8,128)(2,1)} custom-call(bf16[512,352]{1,0:T(8,128)(2,1)} %fusion.83.place_ref, bf16[8,128,768]{2,1,0:T(8,128)(2,1)} %all-to-all-done.13.back_ref), custom_call_target="tpu_custom_call" | custom-call | flops 738197504 | bytes 4194304 | tf_op jit(solution)/shard_map/pallas_call | solution.py:1025
  303.2 3.8 collective-permute-start.72
  311.8 8.3 %collective-permute-done.72 = bf16[72,2048]{1,0:T(8,128)(2,1)} collective-permute-done((bf16[72,2048]{1,0:T(8,128)(2,1)}, bf16[72,2048]{1,0:T(8,128)(2,1)}, u32[]{:S(2)}, u32[]{:S(2)}) %collective-permute-start.72) | collective-permute-done | bytes 294944 | tf_op jit(solution)/shard_map/ppermute | solution.py:161
  320.1 11.8 %collective-permute-done.75 = bf16[72,2048]{1,0:T(8,128)(2,1)} collective-permute-done((bf16[72,2048]{1,0:T(8,128)(2,1)}, bf16[72,2048]{1,0:T(8,128)(2,1)}, u32[]{:S(2)}, u32[]{:S(2)}) %collective-permute-start.75) | collective-permute-done | bytes 294944 | tf_op jit(solution)/shard_map/ppermute | solution.py:161
  343.0 5.9 %collective-permute-done.73 = bf16[72,2048]{1,0:T(8,128)(2,1)} collective-permute-done((bf16[72,2048]{1,0:T(8,128)(2,1)}, bf16[72,2048]{1,0:T(8,128)(2,1)}, u32[]{:S(2)}, u32[]{:S(2)}) %collective-permute-start.73) | collective-permute-done | bytes 294944 | tf_op jit(solution)/shard_map/ppermute | solution.py:161
  352.8 4.4 collective-permute-start.74
  363.2 4.6 %collective-permute-done.77 = bf16[72,2048]{1,0:T(8,128)(2,1)} collective-permute-done((bf16[72,2048]{1,0:T(8,128)(2,1)}, bf16[72,2048]{1,0:T(8,128)(2,1)}, u32[]{:S(2)}, u32[]{:S(2)}) %collective-permute-start.77) | collective-permute-done | bytes 294944 | tf_op jit(solution)/shard_map/ppermute | solution.py:161
  377.9 7.5 %collective-permute-done.68 = bf16[2,2,128,512]{3,2,0,1:T(8,128)(2,1)S(1)} collective-permute-done((bf16[2,2,128,512]{3,2,0,1:T(8,128)(2,1)S(1)}, bf16[2,2,128,512]{3,2,0,1:T(8,128)(2,1)S(1)}, u32[]{:S(2)}, u32[]{:S(2)}) %collective-permute-start.68) | collective-permute-done | bytes 524320 | tf_op jit(solution)/shard_map/ppermute | solution.py:66
  386.6 4.1 convolution_convert_fusion.1
  390.8 4.4 all-to-all-start.14
  401.5 27.7 %collective-permute-done.69 = bf16[2,128,512]{2,1,0:T(8,128)(2,1)S(1)} collective-permute-done((bf16[2,128,512]{2,1,0:T(8,128)(2,1)S(1)}, bf16[2,128,512]{2,1,0:T(8,128)(2,1)S(1)}, u32[]{:S(2)}, u32[]{:S(2)}) %collective-permute-start.69) | collective-permute-done | bytes 262176 | tf_op jit(solution)/shard_map/ppermute | solution.py:66
  430.9 9.8 %shard_map.145 = (f32[255,2048]{1,0:T(8,128)}, f32[255,2048]{1,0:T(8,128)}, f32[255,2048]{1,0:T(8,128)}, f32[255,2048]{1,0:T(8,128)}) custom-call(bf16[255,576]{1,0:T(8,128)(2,1)} %copy.186.send, bf16[576,2048]{1,0:T(8,128)(2,1)} %bitcast.72.rows, f32[255,2048]{1,0:T(8,128)} %first.1, f32[255,2048]{1,0:T(8,128)} %second.1, f32[255,2048]{1,0:T(8,128)S(1)} %copy-done.16, ...), custom_call_target="tpu_custom_call" | custom-call | flops 601620480 | bytes 16777216 | tf_op jit(solution)/shard_map/pallas_call | solution.py:610
  (375 shorter events, 170.7 us)
Async XLA Ops:
  10.3 18.7 %collective-permute-start.44 = (bf16[2,128,512]{2,1,0:T(8,128)(2,1)}, bf16[2,128,512]{2,1,0:T(8,128)(2,1)}, u32[]{:S(2)}, u32[]{:S(2)}) collective-permute-start(bf16[2,128,512]{2,1,0:T(8,128)(2,1)} %get-tuple-element.386), channel_id=1, source_target_pairs={{0,4},{1,5},{2,6},{3,7},{4,0},{5,1},{6,2},{7,3},{8,12},{9,13},{10,... | collective-permute-start | bytes 786440 | tf_op jit(solution)/shard_map/ppermute | solution.py:66
  13.3 20.7 %collective-permute-start.42 = (bf16[2,128,512]{2,1,0:T(8,128)(2,1)}, bf16[2,128,512]{2,1,0:T(8,128)(2,1)}, u32[]{:S(2)}, u32[]{:S(2)}) collective-permute-start(bf16[2,128,512]{2,1,0:T(8,128)(2,1)} %get-tuple-element.387), channel_id=1, source_target_pairs={{0,2},{1,3},{2,0},{3,1},{4,6},{5,7},{6,4},{7,5},{8,10},{9,11},{10,... | collective-permute-start | bytes 786440 | tf_op jit(solution)/shard_map/ppermute | solution.py:66
  24.0 17.4 %all-to-all-start.8 = ((bf16[8,24,2048]{2,1,0:T(8,128)(2,1)}), bf16[8,24,2048]{2,1,0:T(8,128)(2,1)}, u32[]{:S(2)}, u32[]{:S(2)}) async-start(bf16[8,24,2048]{2,1,0:T(8,128)(2,1)} %bitcast.396), calls=%async_computation.8 | async-start | bytes 1572864 | tf_op jit(solution)/shard_map/all_to_all | solution.py:70
  28.2 45.1 %all-gather.4.cloned.1.call-start = ((), (), s32[]{:S(2)}) async-start(), calls=%async_computation.17 | async-start | bytes 1474560 | tf_op jit(solution)/shard_map/all_gather | solution.py:296
  30.9 20.2 %collective-permute-start.45 = (bf16[2,2,128,512]{3,2,0,1:T(8,128)(2,1)}, bf16[2,2,128,512]{3,2,0,1:T(8,128)(2,1)}, u32[]{:S(2)}, u32[]{:S(2)}) collective-permute-start(bf16[2,2,128,512]{3,2,0,1:T(8,128)(2,1)} %pad_maximum_fusion.16), channel_id=1, source_target_pairs={{0,2},{1,3},{2,0},{3,1},{4,6},{5,7},{6,4},{7,5},{8,10},{9,11},{10,... | collective-permute-start | bytes 1572872 | tf_op jit(solution)/shard_map/ppermute | solution.py:66
  35.9 16.3 %collective-permute-start.43 = (bf16[2,2,128,512]{3,2,0,1:T(8,128)(2,1)}, bf16[2,2,128,512]{3,2,0,1:T(8,128)(2,1)}, u32[]{:S(2)}, u32[]{:S(2)}) collective-permute-start(bf16[2,2,128,512]{3,2,0,1:T(8,128)(2,1)} %pad_maximum_fusion.15), channel_id=1, source_target_pairs={{0,4},{1,5},{2,6},{3,7},{4,0},{5,1},{6,2},{7,3},{8,12},{9,13},{10,... | collective-permute-start | bytes 1572872 | tf_op jit(solution)/shard_map/ppermute | solution.py:66
  55.8 41.7 %collective-permute-start.46 = (bf16[2,512,1024]{2,1,0:T(8,128)(2,1)}, bf16[2,512,1024]{2,1,0:T(8,128)(2,1)}, u32[]{:S(2)}, u32[]{:S(2)}) collective-permute-start(bf16[2,512,1024]{2,1,0:T(8,128)(2,1)} %bitcast.10.x0.c0), channel_id=1, source_target_pairs={{0,1},{1,0},{2,3},{3,2},{4,5},{5,4},{6,7},{7,6},{8,9},{9,8},{10,11... | collective-permute-start | bytes 6291464 | tf_op jit(solution)/shard_map/ppermute | solution.py:66
  76.7 13.9 %all-to-all-start.9 = ((bf16[8,128,256]{2,1,0:T(8,128)(2,1)}), bf16[8,128,256]{2,1,0:T(8,128)(2,1)}, u32[]{:S(2)}, u32[]{:S(2)}) async-start(bf16[8,128,256]{2,1,0:T(8,128)(2,1)} %get-tuple-element.143), calls=%async_computation.9 | async-start | bytes 1048576 | tf_op jit(solution)/shard_map/all_to_all | solution.py:70
  90.5 25.3 %all-to-all-start.10 = ((bf16[8,48,2048]{2,1,0:T(8,128)(2,1)}), bf16[8,48,2048]{2,1,0:T(8,128)(2,1)}, u32[]{:S(2)}, u32[]{:S(2)}) async-start(bf16[8,48,2048]{2,1,0:T(8,128)(2,1)} %bitcast.395), calls=%async_computation.10 | async-start | bytes 3145728 | tf_op jit(solution)/shard_map/all_to_all | solution.py:70
  94.9 68.1 %all-gather.6.cloned.1.call-start = ((), (), s32[]{:S(2)}) async-start(), calls=%async_computation.18 | async-start | bytes 2621440 | tf_op jit(solution)/shard_map/all_gather | solution.py:296
  108.9 10.8 %collective-permute-start.47 = (bf16[1,512,1024]{2,1,0:T(8,128)(2,1)}, bf16[1,512,1024]{2,1,0:T(8,128)(2,1)}, u32[]{:S(2)}, u32[]{:S(2)}) collective-permute-start(bf16[1,512,1024]{2,1,0:T(8,128)(2,1)} %get-tuple-element.146), channel_id=1, source_target_pairs={{0,1},{1,0},{2,3},{3,2},{4,5},{5,4},{6,7},{7,6},{8,9},{9,8},{10,11... | collective-permute-start | bytes 3145736 | tf_op jit(solution)/shard_map/ppermute | solution.py:66
  119.7 76.2 %all-gather.8.cloned.1.call-start = ((), (), s32[]{:S(2)}) async-start(), calls=%async_computation.19 | async-start | bytes 1638400 | tf_op jit(solution)/shard_map/all_gather | solution.py:296
  144.7 27.6 %collective-permute-start.55 = (bf16[1,2,128,512]{3,2,1,0:T(8,128)(2,1)}, bf16[1,2,128,512]{3,2,1,0:T(8,128)(2,1)}, u32[]{:S(2)}, u32[]{:S(2)}) collective-permute-start(bf16[1,2,128,512]{3,2,1,0:T(8,128)(2,1)} %pad_maximum_fusion.22), channel_id=1, source_target_pairs={{0,2},{1,3},{2,0},{3,1},{4,6},{5,7},{6,4},{7,5},{8,10},{9,11},{10,... | collective-permute-start | bytes 786440 | tf_op jit(solution)/shard_map/ppermute | solution.py:66
  147.9 25.3 %collective-permute-start.53 = (bf16[1,2,128,512]{3,2,1,0:T(8,128)(2,1)}, bf16[1,2,128,512]{3,2,1,0:T(8,128)(2,1)}, u32[]{:S(2)}, u32[]{:S(2)}) collective-permute-start(bf16[1,2,128,512]{3,2,1,0:T(8,128)(2,1)} %pad_maximum_fusion.21), channel_id=1, source_target_pairs={{0,4},{1,5},{2,6},{3,7},{4,0},{5,1},{6,2},{7,3},{8,12},{9,13},{10,... | collective-permute-start | bytes 786440 | tf_op jit(solution)/shard_map/ppermute | solution.py:66
  167.7 31.2 %all-to-all-start.11 = ((bf16[8,128,768]{2,1,0:T(8,128)(2,1)}), bf16[8,128,768]{2,1,0:T(8,128)(2,1)}, u32[]{:S(2)}, u32[]{:S(2)}) async-start(bf16[8,128,768]{2,1,0:T(8,128)(2,1)} %shard_map.138), calls=%async_computation.11 | async-start | bytes 3145728 | tf_op jit(solution)/shard_map/all_to_all | solution.py:70
  172.0 214.6 %reduce-scatter.5.cloned.1.call-start = ((), (), s32[]{:S(2)}) async-start(), calls=%async_computation.21 | async-start | bytes 1638400 | tf_op jit(solution)/shard_map/reduce_scatter | solution.py:323
  175.5 23.3 %collective-permute-start.56 = (bf16[1,512,1024]{2,1,0:T(8,128)(2,1)}, bf16[1,512,1024]{2,1,0:T(8,128)(2,1)}, u32[]{:S(2)}, u32[]{:S(2)}) collective-permute-start(bf16[1,512,1024]{2,1,0:T(8,128)(2,1)} %bitcast.33.h0), channel_id=1, source_target_pairs={{0,1},{1,0},{2,3},{3,2},{4,5},{5,4},{6,7},{7,6},{8,9},{9,8},{10,11... | collective-permute-start | bytes 3145736 | tf_op jit(solution)/shard_map/ppermute | solution.py:66
  248.7 10.7 %collective-permute-start.66 = (bf16[1,512,1024]{2,1,0:T(8,128)(2,1)}, bf16[1,512,1024]{2,1,0:T(8,128)(2,1)}, u32[]{:S(2)}, u32[]{:S(2)}) collective-permute-start(bf16[1,512,1024]{2,1,0:T(8,128)(2,1)} %bitcast.48.m0), channel_id=1, source_target_pairs={{0,1},{1,0},{2,3},{3,2},{4,5},{5,4},{6,7},{7,6},{8,9},{9,8},{10,11... | collective-permute-start | bytes 3145736 | tf_op jit(solution)/shard_map/ppermute | solution.py:66
  253.3 29.1 %all-to-all-start.13 = ((bf16[8,128,768]{2,1,0:T(8,128)(2,1)}), bf16[8,128,768]{2,1,0:T(8,128)(2,1)}, u32[]{:S(2)}, u32[]{:S(2)}) async-start(bf16[8,128,768]{2,1,0:T(8,128)(2,1)} %bitcast.402), calls=%async_computation.13 | async-start | bytes 3145728 | tf_op jit(solution)/shard_map/all_to_all | solution.py:70
  282.4 15.5 %all-to-all-start.12 = ((bf16[8,128,256]{2,1,0:T(8,128)(2,1)}), bf16[8,128,256]{2,1,0:T(8,128)(2,1)}, u32[]{:S(2)}, u32[]{:S(2)}) async-start(bf16[8,128,256]{2,1,0:T(8,128)(2,1)} %bitcast.408), calls=%async_computation.12 | async-start | bytes 1048576 | tf_op jit(solution)/shard_map/all_to_all | solution.py:70
  286.6 100.0 %reduce-scatter.3.cloned.1.call-start = ((), (), s32[]{:S(2)}) async-start(), calls=%async_computation.20 | async-start | bytes 2621440 | tf_op jit(solution)/shard_map/reduce_scatter | solution.py:323
  303.2 16.9 %collective-permute-start.72 = (bf16[72,2048]{1,0:T(8,128)(2,1)}, bf16[72,2048]{1,0:T(8,128)(2,1)}, u32[]{:S(2)}, u32[]{:S(2)}) collective-permute-start(bf16[72,2048]{1,0:T(8,128)(2,1)} %get-tuple-element.378), channel_id=1, source_target_pairs={{0,8},{8,16},{16,24},{1,9},{9,17},{17,25},{2,10},{10,18},{18,26},{... | collective-permute-start | bytes 884744 | tf_op jit(solution)/shard_map/ppermute | solution.py:161
  306.9 25.0 %collective-permute-start.75 = (bf16[72,2048]{1,0:T(8,128)(2,1)}, bf16[72,2048]{1,0:T(8,128)(2,1)}, u32[]{:S(2)}, u32[]{:S(2)}) collective-permute-start(bf16[72,2048]{1,0:T(8,128)(2,1)} %get-tuple-element.379), channel_id=1, source_target_pairs={{8,0},{16,8},{24,16},{9,1},{17,9},{25,17},{10,2},{18,10},{26,18},{... | collective-permute-start | bytes 884744 | tf_op jit(solution)/shard_map/ppermute | solution.py:161
  311.6 58.1 %collective-permute-start.67 = (bf16[2,512,1024]{2,1,0:T(8,128)(2,1)}, bf16[2,512,1024]{2,1,0:T(8,128)(2,1)}, u32[]{:S(2)}, u32[]{:S(2)}) collective-permute-start(bf16[2,512,1024]{2,1,0:T(8,128)(2,1)} %get-tuple-element.156), channel_id=1, source_target_pairs={{0,1},{1,0},{2,3},{3,2},{4,5},{5,4},{6,7},{7,6},{8,9},{9,8},{10,11... | collective-permute-start | bytes 6291464 | tf_op jit(solution)/shard_map/ppermute | solution.py:66
  334.0 14.9 %collective-permute-start.73 = (bf16[72,2048]{1,0:T(8,128)(2,1)}, bf16[72,2048]{1,0:T(8,128)(2,1)}, u32[]{:S(2)}, u32[]{:S(2)}) collective-permute-start(bf16[72,2048]{1,0:T(8,128)(2,1)} %get-tuple-element.376), channel_id=1, source_target_pairs={{0,8},{8,16},{16,24},{1,9},{9,17},{17,25},{2,10},{10,18},{18,26},{... | collective-permute-start | bytes 884744 | tf_op jit(solution)/shard_map/ppermute | solution.py:161
  337.1 13.5 %collective-permute-start.76 = (bf16[72,2048]{1,0:T(8,128)(2,1)}, bf16[72,2048]{1,0:T(8,128)(2,1)}, u32[]{:S(2)}, u32[]{:S(2)}) collective-permute-start(bf16[72,2048]{1,0:T(8,128)(2,1)} %get-tuple-element.377), channel_id=1, source_target_pairs={{8,0},{16,8},{24,16},{9,1},{17,9},{25,17},{10,2},{18,10},{26,18},{... | collective-permute-start | bytes 884744 | tf_op jit(solution)/shard_map/ppermute | solution.py:161
  357.2 10.6 %collective-permute-start.77 = (bf16[72,2048]{1,0:T(8,128)(2,1)}, bf16[72,2048]{1,0:T(8,128)(2,1)}, u32[]{:S(2)}, u32[]{:S(2)}) collective-permute-start(bf16[72,2048]{1,0:T(8,128)(2,1)} %get-tuple-element.375), channel_id=1, source_target_pairs={{8,0},{16,8},{24,16},{9,1},{17,9},{25,17},{10,2},{18,10},{26,18},{... | collective-permute-start | bytes 884744 | tf_op jit(solution)/shard_map/ppermute | solution.py:161
  373.0 12.5 %collective-permute-start.68 = (bf16[2,2,128,512]{3,2,0,1:T(8,128)(2,1)S(1)}, bf16[2,2,128,512]{3,2,0,1:T(8,128)(2,1)S(1)}, u32[]{:S(2)}, u32[]{:S(2)}) collective-permute-start(bf16[2,2,128,512]{3,2,0,1:T(8,128)(2,1)S(1)} %copy.209), channel_id=1, source_target_pairs={{0,4},{1,5},{2,6},{3,7},{4,0},{5,1},{6,2},{7,3},{8,12},{9,13},{10,... | collective-permute-start | bytes 1572872 | tf_op jit(solution)/shard_map/ppermute | solution.py:66
  375.4 22.9 %collective-permute-start.70 = (bf16[2,2,128,512]{3,2,0,1:T(8,128)(2,1)}, bf16[2,2,128,512]{3,2,0,1:T(8,128)(2,1)}, u32[]{:S(2)}, u32[]{:S(2)}) collective-permute-start(bf16[2,2,128,512]{3,2,0,1:T(8,128)(2,1)} %pad_maximum_fusion.19), channel_id=1, source_target_pairs={{0,2},{1,3},{2,0},{3,1},{4,6},{5,7},{6,4},{7,5},{8,10},{9,11},{10,... | collective-permute-start | bytes 1572872 | tf_op jit(solution)/shard_map/ppermute | solution.py:66
  390.8 40.1 %all-to-all-start.14 = ((bf16[8,72,2048]{2,1,0:T(8,128)(2,1)}), bf16[8,72,2048]{2,1,0:T(8,128)(2,1)}, u32[]{:S(2)}, u32[]{:S(2)}) async-start(bf16[8,72,2048]{2,1,0:T(8,128)(2,1)} %bitcast.401), calls=%async_computation.16 | async-start | bytes 4718592 | tf_op jit(solution)/shard_map/all_to_all | solution.py:70
  396.4 32.9 %collective-permute-start.69 = (bf16[2,128,512]{2,1,0:T(8,128)(2,1)S(1)}, bf16[2,128,512]{2,1,0:T(8,128)(2,1)S(1)}, u32[]{:S(2)}, u32[]{:S(2)}) collective-permute-start(bf16[2,128,512]{2,1,0:T(8,128)(2,1)S(1)} %fusion.120), channel_id=1, source_target_pairs={{0,2},{1,3},{2,0},{3,1},{4,6},{5,7},{6,4},{7,5},{8,10},{9,11},{10,... | collective-permute-start | bytes 786440 | tf_op jit(solution)/shard_map/ppermute | solution.py:66
  400.0 29.3 %collective-permute-start.71 = (bf16[2,128,512]{2,1,0:T(8,128)(2,1)S(1)}, bf16[2,128,512]{2,1,0:T(8,128)(2,1)S(1)}, u32[]{:S(2)}, u32[]{:S(2)}) collective-permute-start(bf16[2,128,512]{2,1,0:T(8,128)(2,1)S(1)} %fusion.121), channel_id=1, source_target_pairs={{0,4},{1,5},{2,6},{3,7},{4,0},{5,1},{6,2},{7,3},{8,12},{9,13},{10,... | collective-permute-start | bytes 786440 | tf_op jit(solution)/shard_map/ppermute | solution.py:66
  (71 other events, 980.6 us)
Sparse Core Ops, SparseCore 0:
  43.7 29.6 all-gather.3
  119.8 43.0 all-gather.5
  164.5 31.3 all-gather.7
  244.3 29.7 reduce-scatter.4
  296.7 55.6 reduce-scatter.2
